TPU v7x, 32 devices: a whole 2x2x4 slice. The times are simulated.
32 devices in a mesh: wide: 16 (over z, y, x), narrow: 2 (over core).
Axes of the slice: x: 2, y: 2, z: 4, core: 2. Of those that a mesh axis runs over, the one named last changes fastest.
Arguments:
- tokens: bfloat16 [32, 96, 6400], P(('wide', 'narrow')), may hold values from -6 to 6
- image_sides: int32 [32], P(('wide', 'narrow')), may hold values from 56 to 80, as said below
- grad_out: bfloat16 [32, 96, 6400], P(('wide', 'narrow')), may hold values from -6 to 6
- master: float32 [144960], P('wide')
- first_moment: float32 [144960], P('wide')
- second_moment: float32 [144960], P('wide'), as said below
- weight_average: float32 [144960], P('wide')
Outputs:
- block_out: bfloat16 [32, 96, 6400], P(('wide', 'narrow'))
- grad_in: bfloat16 [32, 96, 6400], P(('wide', 'narrow'))
- new_master: float32 [144960], P('wide')
- new_first: float32 [144960], P('wide')
- new_second: float32 [144960], P('wide')
- new_average: float32 [144960], P('wide')
Inputs may be any that keep to these rules, and one draw needn't show every extreme that they name: `image_sides`: each image's side is one of three values: 4 times (14), 4 times (16), or 80; the first image's side is 80. `second_moment`: every entry is positive.
All inputs are finite; a program needn't handle non-finite values.
Results may differ from a plain program's by a relative error of at most 0.012.
Values may be sent and summed in bfloat16 or wider, within the bound.
No kernel may reach another device: no remote copies, remote signals or barrier semaphores. Data moves between devices by JAX's collectives and lax.ppermute only.
A program may use at most 256 MiB of HBM per device.

v0:
```python
import math

import jax
import jax.numpy as jnp
from jax import lax
from jax.sharding import PartitionSpec as P

D = 96
HID = 384
KSTR = 4
KG = 20
STEP = 5
GRID = 80
TOK = 6400
KK = 400
REL = 159


norm_eps = 1e-06
beta_first = 0.5
beta_second = 0.5
adam_eps = 1e-08
weight_decay = 0.05
rate_factor = 0.4
average_decay = 0.8
high = lax.Precision.HIGHEST
contract_rows = (((1,), (1,)), ((), ()))
contract_cols = (((0,), (0,)), ((), ()))


def segment_list():
    return [
        ("w_qkv", (3 * D, D), D ** (-0.5)),
        ("b_qkv", (3 * D,), 0.2),
        ("pool_q", (D, 9), 1.0 / 3.0),
        ("pool_k", (D, 9), 1.0 / 3.0),
        ("pool_v", (D, 9), 1.0 / 3.0),
        ("rel_h", (REL, D), 0.5 * D ** (-0.5)),
        ("rel_w", (REL, D), 0.5 * D ** (-0.5)),
        ("w_proj", (D, D), D ** (-0.5)),
        ("b_proj", (D,), 0.2),
        ("w_fc1", (HID, D), D ** (-0.5)),
        ("b_fc1", (HID,), 0.2),
        ("w_fc2", (D, HID), HID ** (-0.5)),
        ("b_fc2", (D,), 0.2),
        ("ln1_g", (D,), 0.5),
        ("ln1_b", (D,), 0.2),
        ("ln2_g", (D,), 0.5),
        ("ln2_b", (D,), 0.2),
    ]


def unpack_flat(flat):
    pieces = {}
    offset = 0
    for segment_name, piece_shape, spread in segment_list():
        length = math.prod(piece_shape)
        pieces[segment_name] = flat[offset : offset + length].reshape(piece_shape)
        offset += length
    return pieces


def rate_vector(full_len):
    segment_rates = []
    used_len = 0
    for segment_name, piece_shape, spread in segment_list():
        length = math.prod(piece_shape)
        segment_rates.append(jnp.full((length,), rate_factor * spread, jnp.float32))
        used_len += length
    segment_rates.append(jnp.full((full_len - used_len,), rate_factor * D ** (-0.5), jnp.float32))
    return jnp.concatenate(segment_rates)


def layer_norm(values, scale_gain, shift_bias):
    center = values - jnp.mean(values, axis=0, keepdims=True)
    spread_sq = jnp.mean(center * center, axis=0, keepdims=True)
    return center * lax.rsqrt(spread_sq + norm_eps) * scale_gain[:, None] + shift_bias[:, None]


def depth_pool(field_in, kernel, stride, side_out):
    channels = field_in.shape[0]
    padded = jnp.pad(field_in.reshape(channels, GRID, GRID), ((0, 0), (1, 1), (1, 1)))
    result = jnp.zeros((channels, side_out, side_out), jnp.float32)
    reach = stride * (side_out - 1) + 1
    for row_off in range(3):
        for col_off in range(3):
            window = padded[
                :, row_off : row_off + reach : stride, col_off : col_off + reach : stride
            ]
            result = result + kernel[:, row_off * 3 + col_off][:, None, None] * window
    return result.reshape(channels, side_out * side_out)


def grid_masks(image_side):
    row_valid = (jnp.arange(GRID, dtype=jnp.int32) < image_side).astype(jnp.float32)
    token_mask = (row_valid[:, None] * row_valid[None, :]).reshape(TOK)
    pooled = (jnp.arange(KG, dtype=jnp.int32) * KSTR < image_side).astype(jnp.float32)
    key_mask = (pooled[:, None] * pooled[None, :]).reshape(KK)
    return (token_mask, key_mask)


def masked_softmax(scores, key_mask):
    return jax.nn.softmax(jnp.where(key_mask[:, None] > 0, scores, -1e30), axis=0)


def gelu_exact(values):
    return jax.nn.gelu(values, approximate=False)


def rel_onehot():
    rel_index = (
        jnp.arange(GRID, dtype=jnp.int32)[:, None]
        - KSTR * jnp.arange(KG, dtype=jnp.int32)[None, :]
        + GRID
        - 1
    )
    return (rel_index.reshape(GRID * KG, 1) == jnp.arange(REL, dtype=jnp.int32)[None, :]).astype(
        jnp.bfloat16
    )


def as_float(weights, segment_name):
    return weights[segment_name].astype(jnp.float32)


def forward_parts(weights, onehot, pixels, image_side):
    token_mask, key_mask = grid_masks(image_side)
    pixels_f = pixels.astype(jnp.float32)
    normed, norm_one_back = jax.vjp(
        layer_norm, pixels_f, as_float(weights, "ln1_g"), as_float(weights, "ln1_b")
    )
    normed_low = normed.astype(jnp.bfloat16)
    mixed_qkv = jnp.dot(weights["w_qkv"], normed_low, preferred_element_type=jnp.float32)
    mixed_qkv = (mixed_qkv + as_float(weights, "b_qkv")[:, None]) * token_mask[None, :]

    def pool_all(mixed_in, kernel_q, kernel_k, kernel_v):
        return (
            depth_pool(mixed_in[:D], kernel_q, 1, GRID) * token_mask[None, :],
            depth_pool(mixed_in[D : 2 * D], kernel_k, KSTR, KG) * key_mask[None, :],
            depth_pool(mixed_in[2 * D :], kernel_v, KSTR, KG) * key_mask[None, :],
        )

    pooled_all, pool_back = jax.vjp(
        pool_all,
        mixed_qkv,
        as_float(weights, "pool_q"),
        as_float(weights, "pool_k"),
        as_float(weights, "pool_v"),
    )
    queries_low = pooled_all[0].astype(jnp.bfloat16)
    keyset_low = pooled_all[1].astype(jnp.bfloat16)
    valueset_low = pooled_all[2].astype(jnp.bfloat16)
    table_h = (
        jnp.dot(onehot, weights["rel_h"], preferred_element_type=jnp.float32)
        .astype(jnp.bfloat16)
        .reshape(GRID, KG, D)
    )
    table_w = (
        jnp.dot(onehot, weights["rel_w"], preferred_element_type=jnp.float32)
        .astype(jnp.bfloat16)
        .reshape(GRID, KG, D)
    )
    grid_query = queries_low.reshape(D, GRID, GRID)
    along_rows = jnp.einsum(
        "drc,rad->arc", grid_query, table_h, preferred_element_type=jnp.float32
    ).reshape(KG, 1, TOK)
    along_cols = jnp.einsum(
        "drc,cbd->brc", grid_query, table_w, preferred_element_type=jnp.float32
    ).reshape(1, KG, TOK)
    content = lax.dot_general(
        keyset_low, queries_low, contract_cols, preferred_element_type=jnp.float32
    )
    scores = (D ** (-0.5) * content.reshape(KG, KG, TOK) + along_rows + along_cols).reshape(KK, TOK)

    def soft_fn(score_in):
        return masked_softmax(score_in, key_mask)

    attention, soft_back = jax.vjp(soft_fn, scores)
    attention_low = attention.astype(jnp.bfloat16)
    attended = jnp.dot(
        valueset_low, attention_low, preferred_element_type=jnp.float32
    ) + queries_low.astype(jnp.float32)
    attended_low = attended.astype(jnp.bfloat16)
    middle = (
        pixels_f
        + jnp.dot(weights["w_proj"], attended_low, preferred_element_type=jnp.float32)
        + as_float(weights, "b_proj")[:, None]
    )
    normed_two, norm_two_back = jax.vjp(
        layer_norm, middle, as_float(weights, "ln2_g"), as_float(weights, "ln2_b")
    )
    normed_two_low = normed_two.astype(jnp.bfloat16)
    hidden = (
        jnp.dot(weights["w_fc1"], normed_two_low, preferred_element_type=jnp.float32)
        + as_float(weights, "b_fc1")[:, None]
    )
    active, gelu_back = jax.vjp(gelu_exact, hidden)
    active_low = active.astype(jnp.bfloat16)
    mlp_out = (
        jnp.dot(weights["w_fc2"], active_low, preferred_element_type=jnp.float32)
        + as_float(weights, "b_fc2")[:, None]
    )
    output = (middle + mlp_out) * token_mask[None, :]
    kept = {
        "token_mask": token_mask,
        "normed_low": normed_low,
        "norm_one_back": norm_one_back,
        "pool_back": pool_back,
        "queries_low": queries_low,
        "keyset_low": keyset_low,
        "valueset_low": valueset_low,
        "table_h": table_h,
        "table_w": table_w,
        "soft_back": soft_back,
        "attention_low": attention_low,
        "attended_low": attended_low,
        "norm_two_back": norm_two_back,
        "normed_two_low": normed_two_low,
        "gelu_back": gelu_back,
        "active_low": active_low,
    }
    return (output, kept)


def backward_image(weights, onehot, pixels, image_side, cotangent, full_len):
    output, kept = forward_parts(weights, onehot, pixels, image_side)
    token_mask = kept["token_mask"]
    gradients = {}
    out_grad = cotangent.astype(jnp.float32) * token_mask[None, :]
    out_grad_low = out_grad.astype(jnp.bfloat16)
    gradients["w_fc2"] = lax.dot_general(
        out_grad_low, kept["active_low"], contract_rows, preferred_element_type=jnp.float32
    )
    gradients["b_fc2"] = jnp.sum(out_grad, axis=1)
    d_active = lax.dot_general(
        weights["w_fc2"], out_grad_low, contract_cols, preferred_element_type=jnp.float32
    )
    d_hidden_low = kept["gelu_back"](d_active)[0].astype(jnp.bfloat16)
    gradients["w_fc1"] = lax.dot_general(
        d_hidden_low, kept["normed_two_low"], contract_rows, preferred_element_type=jnp.float32
    )
    gradients["b_fc1"] = jnp.sum(d_hidden_low.astype(jnp.float32), axis=1)
    d_normed_two = lax.dot_general(
        weights["w_fc1"], d_hidden_low, contract_cols, preferred_element_type=jnp.float32
    )
    d_mid_norm, gradients["ln2_g"], gradients["ln2_b"] = kept["norm_two_back"](d_normed_two)
    d_middle = out_grad + d_mid_norm
    d_proj_low = d_middle.astype(jnp.bfloat16)
    gradients["w_proj"] = lax.dot_general(
        d_proj_low, kept["attended_low"], contract_rows, preferred_element_type=jnp.float32
    )
    gradients["b_proj"] = jnp.sum(d_proj_low.astype(jnp.float32), axis=1)
    d_attended_low = lax.dot_general(
        weights["w_proj"], d_proj_low, contract_cols, preferred_element_type=jnp.float32
    ).astype(jnp.bfloat16)
    d_valueset = lax.dot_general(
        d_attended_low, kept["attention_low"], contract_rows, preferred_element_type=jnp.float32
    )
    d_attention = lax.dot_general(
        kept["valueset_low"], d_attended_low, contract_cols, preferred_element_type=jnp.float32
    )
    d_scores_low = kept["soft_back"](d_attention)[0].astype(jnp.bfloat16)
    queries_low = kept["queries_low"]
    d_query = d_attended_low.astype(jnp.float32)
    d_query = d_query + D ** (-0.5) * jnp.dot(
        kept["keyset_low"], d_scores_low, preferred_element_type=jnp.float32
    )
    d_keyset = D ** (-0.5) * lax.dot_general(
        queries_low, d_scores_low, contract_rows, preferred_element_type=jnp.float32
    )
    d_grid = d_scores_low.astype(jnp.float32).reshape(KG, KG, TOK)
    d_rows = jnp.sum(d_grid, axis=1).reshape(KG, GRID, GRID)
    d_cols = jnp.sum(d_grid, axis=0).reshape(KG, GRID, GRID)
    table_h_f = kept["table_h"].astype(jnp.float32)
    table_w_f = kept["table_w"].astype(jnp.float32)
    rel_part = jnp.einsum("arc,rad->drc", d_rows, table_h_f, precision=high) + jnp.einsum(
        "brc,cbd->drc", d_cols, table_w_f, precision=high
    )
    d_query = d_query + rel_part.reshape(D, TOK)
    query_grid_f = queries_low.astype(jnp.float32).reshape(D, GRID, GRID)
    d_table_h = jnp.einsum("arc,drc->rad", d_rows, query_grid_f, precision=high).reshape(
        GRID * KG, D
    )
    d_table_w = jnp.einsum("brc,drc->cbd", d_cols, query_grid_f, precision=high).reshape(
        GRID * KG, D
    )
    onehot_f = onehot.astype(jnp.float32)
    gradients["rel_h"] = lax.dot_general(onehot_f, d_table_h, contract_cols, precision=high)
    gradients["rel_w"] = lax.dot_general(onehot_f, d_table_w, contract_cols, precision=high)
    d_mixed, gradients["pool_q"], gradients["pool_k"], gradients["pool_v"] = kept["pool_back"](
        (d_query, d_keyset, d_valueset)
    )
    d_mixed_low = d_mixed.astype(jnp.bfloat16) * token_mask.astype(jnp.bfloat16)[None, :]
    gradients["w_qkv"] = lax.dot_general(
        d_mixed_low, kept["normed_low"], contract_rows, preferred_element_type=jnp.float32
    )
    gradients["b_qkv"] = jnp.sum(d_mixed_low.astype(jnp.float32), axis=1)
    d_normed = lax.dot_general(
        weights["w_qkv"], d_mixed_low, contract_cols, preferred_element_type=jnp.float32
    )
    d_pix_norm, gradients["ln1_g"], gradients["ln1_b"] = kept["norm_one_back"](d_normed)
    d_pixels = d_middle + d_pix_norm
    pieces_flat = []
    used_len = 0
    for segment_name, piece_shape, spread in segment_list():
        pieces_flat.append(gradients[segment_name].reshape(-1))
        used_len += math.prod(piece_shape)
    pieces_flat.append(jnp.zeros((full_len - used_len,), jnp.float32))
    return (d_pixels, jnp.concatenate(pieces_flat))


def adam_update(gradient, master_part, first_part, second_part, average_part, step_rates):
    moment_one = beta_first * first_part + (1.0 - beta_first) * gradient
    moment_two = beta_second * second_part + (1.0 - beta_second) * gradient * gradient
    fix_one = 1.0 - beta_first**STEP
    fix_two = 1.0 - beta_second**STEP
    direction = moment_one / fix_one / (jnp.sqrt(moment_two / fix_two) + adam_eps)
    updated = master_part - step_rates * (direction + weight_decay * master_part)
    blended = average_decay * average_part + (1.0 - average_decay) * updated
    return (updated, moment_one, moment_two, blended)


def shards(tokens, image_sides, grad_out, master, first_moment, second_moment, weight_average):
    shard_len = master.shape[0]
    full_len = shard_len * lax.axis_size("wide")
    images_all = tokens.shape[0] * lax.axis_size("wide") * lax.axis_size("narrow")
    onehot = rel_onehot()
    gathered = lax.all_gather(master.astype(jnp.bfloat16), "wide", axis=0, tiled=True)
    weights = unpack_flat(gathered)

    def forward_only(inputs):
        pixels, image_side = inputs
        return forward_parts(weights, onehot, pixels, image_side)[0].astype(jnp.bfloat16)

    block_out = lax.map(forward_only, (tokens, image_sides))
    regathered = lax.all_gather(master.astype(jnp.bfloat16), "wide", axis=0, tiled=True)
    back_weights = unpack_flat(regathered)

    def backward_step(running, inputs):
        pixels, image_side, cotangent = inputs
        d_pixels, flat_grad = backward_image(
            back_weights, onehot, pixels, image_side, cotangent, full_len
        )
        return (running + flat_grad, d_pixels.astype(jnp.bfloat16))

    summed, grad_in = lax.scan(
        backward_step, jnp.zeros((full_len,), jnp.float32), (tokens, image_sides, grad_out)
    )
    step_rates = lax.dynamic_slice_in_dim(
        rate_vector(full_len), lax.axis_index("wide") * shard_len, shard_len
    )
    reduced = lax.psum_scatter(summed, "wide", scatter_dimension=0, tiled=True)
    reduced = lax.psum(reduced, "narrow")
    updated, moment_one, moment_two, blended = adam_update(
        reduced / images_all, master, first_moment, second_moment, weight_average, step_rates
    )
    return (block_out, grad_in, updated, moment_one, moment_two, blended)


def solution(mesh):
    return jax.shard_map(
        shards,
        mesh=mesh,
        in_specs=(
            P(("wide", "narrow"), None, None),
            P(("wide", "narrow")),
            P(("wide", "narrow"), None, None),
            P("wide"),
            P("wide"),
            P("wide"),
            P("wide"),
        ),
        out_specs=(
            P(("wide", "narrow"), None, None),
            P(("wide", "narrow"), None, None),
            P("wide"),
            P("wide"),
            P("wide"),
            P("wide"),
        ),
        check_vma=False,
    )
```

profile of v0, /device:TPU:0, one launch (start us, length us, event | category | flops | bytes accessed | tf_op | source)
XLA Modules:
  0.0 938.0 jit_solution(660468561075946080)
XLA Ops:
  18.2 105.6 %all-reduce.65.cloned.1.call-done = bf16[144960]{0:T(1024)(128)(2,1)} async-done(((bf16[144960]{0:T(1024)(128)(2,1)}), bf16[144960]{0:T(1024)(128)(2,1)}) %all-reduce.65.cloned.1.call-update) | async-done | bytes 289936
  137.1 4.1 pad.263
  141.3 11.1 %slice.473 = f32[96,20,20]{0,2,1:T(8,128)} slice(f32[96,82,82]{0,2,1:T(8,128)} %pad.263), slice={[0:96:1], [2:79:4], [2:79:4]} | slice | bytes 307200 | tf_op jit(solution)/shard_map/while/body/eval_jaxpr/jvp()/slice | solution.py:87
  152.3 11.1 %slice.471 = f32[96,20,20]{0,2,1:T(8,128)} slice(f32[96,82,82]{0,2,1:T(8,128)} %pad.263), slice={[0:96:1], [2:79:4], [1:78:4]} | slice | bytes 307200 | tf_op jit(solution)/shard_map/while/body/eval_jaxpr/jvp()/slice | solution.py:87
  163.4 11.1 %slice.469 = f32[96,20,20]{0,2,1:T(8,128)} slice(f32[96,82,82]{0,2,1:T(8,128)} %pad.263), slice={[0:96:1], [2:79:4], [0:77:4]} | slice | bytes 307200 | tf_op jit(solution)/shard_map/while/body/eval_jaxpr/jvp()/slice | solution.py:87
  174.5 11.1 %slice.467 = f32[96,20,20]{0,2,1:T(8,128)} slice(f32[96,82,82]{0,2,1:T(8,128)} %pad.263), slice={[0:96:1], [1:78:4], [2:79:4]} | slice | bytes 307200 | tf_op jit(solution)/shard_map/while/body/eval_jaxpr/jvp()/slice | solution.py:87
  185.6 11.1 %slice.465 = f32[96,20,20]{0,2,1:T(8,128)} slice(f32[96,82,82]{0,2,1:T(8,128)} %pad.263), slice={[0:96:1], [1:78:4], [1:78:4]} | slice | bytes 307200 | tf_op jit(solution)/shard_map/while/body/eval_jaxpr/jvp()/slice | solution.py:87
  196.6 11.1 %slice.463 = f32[96,20,20]{0,2,1:T(8,128)} slice(f32[96,82,82]{0,2,1:T(8,128)} %pad.263), slice={[0:96:1], [1:78:4], [0:77:4]} | slice | bytes 307200 | tf_op jit(solution)/shard_map/while/body/eval_jaxpr/jvp()/slice | solution.py:87
  207.7 11.1 %slice.461 = f32[96,20,20]{0,2,1:T(8,128)} slice(f32[96,82,82]{0,2,1:T(8,128)} %pad.263), slice={[0:96:1], [0:77:4], [2:79:4]} | slice | bytes 307200 | tf_op jit(solution)/shard_map/while/body/eval_jaxpr/jvp()/slice | solution.py:87
  218.8 11.1 %slice.459 = f32[96,20,20]{0,2,1:T(8,128)} slice(f32[96,82,82]{0,2,1:T(8,128)} %pad.263), slice={[0:96:1], [0:77:4], [1:78:4]} | slice | bytes 307200 | tf_op jit(solution)/shard_map/while/body/eval_jaxpr/jvp()/slice | solution.py:87
  229.8 11.1 %slice.457 = f32[96,20,20]{0,2,1:T(8,128)} slice(f32[96,82,82]{0,2,1:T(8,128)} %pad.263), slice={[0:96:1], [0:77:4], [0:77:4]} | slice | bytes 307200 | tf_op jit(solution)/shard_map/while/body/eval_jaxpr/jvp()/slice | solution.py:87
  244.5 4.1 pad.264
  248.6 9.5 %slice.493 = f32[96,20,20]{0,2,1:T(8,128)S(1)} slice(f32[96,82,82]{0,2,1:T(8,128)} %pad.264), slice={[0:96:1], [2:79:4], [2:79:4]} | slice | bytes 307200 | tf_op jit(solution)/shard_map/while/body/eval_jaxpr/jvp()/slice | solution.py:87
  258.1 9.5 %slice.491 = f32[96,20,20]{0,2,1:T(8,128)S(1)} slice(f32[96,82,82]{0,2,1:T(8,128)} %pad.264), slice={[0:96:1], [2:79:4], [1:78:4]} | slice | bytes 307200 | tf_op jit(solution)/shard_map/while/body/eval_jaxpr/jvp()/slice | solution.py:87
  267.6 9.5 %slice.489 = f32[96,20,20]{0,2,1:T(8,128)S(1)} slice(f32[96,82,82]{0,2,1:T(8,128)} %pad.264), slice={[0:96:1], [2:79:4], [0:77:4]} | slice | bytes 307200 | tf_op jit(solution)/shard_map/while/body/eval_jaxpr/jvp()/slice | solution.py:87
  277.2 9.5 %slice.487 = f32[96,20,20]{0,2,1:T(8,128)S(1)} slice(f32[96,82,82]{0,2,1:T(8,128)} %pad.264), slice={[0:96:1], [1:78:4], [2:79:4]} | slice | bytes 307200 | tf_op jit(solution)/shard_map/while/body/eval_jaxpr/jvp()/slice | solution.py:87
  286.7 9.5 %slice.485 = f32[96,20,20]{0,2,1:T(8,128)S(1)} slice(f32[96,82,82]{0,2,1:T(8,128)} %pad.264), slice={[0:96:1], [1:78:4], [1:78:4]} | slice | bytes 307200 | tf_op jit(solution)/shard_map/while/body/eval_jaxpr/jvp()/slice | solution.py:87
  296.3 9.5 %slice.483 = f32[96,20,20]{0,2,1:T(8,128)S(1)} slice(f32[96,82,82]{0,2,1:T(8,128)} %pad.264), slice={[0:96:1], [1:78:4], [0:77:4]} | slice | bytes 307200 | tf_op jit(solution)/shard_map/while/body/eval_jaxpr/jvp()/slice | solution.py:87
  305.8 11.2 %slice.481 = f32[96,20,20]{0,2,1:T(8,128)} slice(f32[96,82,82]{0,2,1:T(8,128)} %pad.264), slice={[0:96:1], [0:77:4], [2:79:4]} | slice | bytes 307200 | tf_op jit(solution)/shard_map/while/body/eval_jaxpr/jvp()/slice | solution.py:87
  317.0 11.1 %slice.479 = f32[96,20,20]{0,2,1:T(8,128)} slice(f32[96,82,82]{0,2,1:T(8,128)} %pad.264), slice={[0:96:1], [0:77:4], [1:78:4]} | slice | bytes 307200 | tf_op jit(solution)/shard_map/while/body/eval_jaxpr/jvp()/slice | solution.py:87
  328.1 11.1 %slice.477 = f32[96,20,20]{0,2,1:T(8,128)} slice(f32[96,82,82]{0,2,1:T(8,128)} %pad.264), slice={[0:96:1], [0:77:4], [0:77:4]} | slice | bytes 307200 | tf_op jit(solution)/shard_map/while/body/eval_jaxpr/jvp()/slice | solution.py:87
  365.2 18.2 %multiply_convert_fusion = (bf16[96,80,80]{0,2,1:T(8,128)(2,1)S(1)}, f32[96,80,80]{0,2,1:T(8,128)}) fusion(f32[80,80]{1,0:T(8,128)S(1)} %broadcast_multiply_fusion.27, f32[96]{0:T(128)} %get-tuple-element.183, f32[96]{0:T(128)} %get-tuple-element.184, f32[96]{0:T(128)} %get-tuple-element.185, f32[96]{0:T(128)} %get-tuple-element.186, ...), kind=kLoop, calls=%fused_computation.107 | loop fusion | flops 11673600 | bytes 6173056 | tf_op jit(solution)/shard_map/while/body/eval_jaxpr/convert_element_type | solution.py:150
  398.5 7.3 select_reduce_fusion
  405.8 11.6 %reshape.708 = f32[400,6400]{1,0:T(8,128)} reshape(f32[20,20,6400]{2,1,0:T(8,128)} %get-tuple-element.262) | data formatting | bytes 20480000 | tf_op jit(solution)/shard_map/while/body/eval_jaxpr/reshape | solution.py:173
  417.4 7.2 fusion
  425.4 4.7 fusion.33
  432.0 24.6 %fusion.4 = (bf16[384,6400]{0,1:T(8,128)(2,1)}, f32[384,6400]{0,1:T(8,128)S(1)}, f32[6400,384]{1,0:T(8,128)}) fusion(f32[384]{0:T(512)S(1)} %slice_convert_fusion.3, bf16[384,96]{1,0:T(8,128)(2,1)S(1)} %reshape.706, f32[96,6400]{1,0:T(8,128)S(1)} %get-tuple-element.264, f32[96]{0:T(128)S(1)} %copy-done.165, f32[96]{0:T(128)S(1)} %copy-done.134, ...), kind=kOutput, calls=%fused_computation.21 | convolution fusion | flops 637132800 | bytes 27160832 | tf_op jit(solution)/shard_map/while/body/eval_jaxpr/dot_general | solution.py:194
  456.6 8.4 convert_reduce_fusion
  481.4 6.1 fusion.99
  491.0 4.7 select_convert_fusion
  495.7 9.4 %reshape.737 = f32[20,20,6400]{2,1,0:T(8,128)} reshape(bf16[400,6400]{1,0:T(8,128)(2,1)} %select_convert_fusion) | data formatting | bytes 15360000 | tf_op jit(solution)/shard_map/while/body/eval_jaxpr/reshape | solution.py:271
  505.1 7.2 fusion.117
  517.8 4.5 fusion.127
  526.9 11.2 %pad.328 = f32[96,80,80]{0,2,1:T(8,128)} pad(f32[96,20,20]{0,2,1:T(8,128)} %get-tuple-element.245, f32[]{:T(128)} %constant.148.clone.1), padding=0_0_0x0_3_3x0_3_3 | pad | bytes 2611204 | tf_op jit(solution)/shard_map/while/body/eval_jaxpr/transpose(jvp(jit(_pad)))/pad | solution.py:82
  538.1 11.2 %pad.327 = f32[96,80,80]{0,2,1:T(8,128)} pad(f32[96,20,20]{0,2,1:T(8,128)} %get-tuple-element.246, f32[]{:T(128)} %constant.148.clone.1), padding=0_0_0x0_3_3x1_2_3 | pad | bytes 2611204 | tf_op jit(solution)/shard_map/while/body/eval_jaxpr/transpose(jvp(jit(_pad)))/pad | solution.py:82
  549.3 7.9 pad.470
  557.2 7.9 pad.471
  565.1 8.0 pad.472
  573.1 8.0 pad.469
  581.1 8.0 pad.268
  589.1 8.1 pad.267
  597.2 8.0 pad.266
  605.3 5.7 convolution_multiply_fusion.1
  617.8 11.1 %pad.335 = f32[96,80,80]{0,2,1:T(8,128)} pad(f32[96,20,20]{0,2,1:T(8,128)} %get-tuple-element.254, f32[]{:T(128)} %constant.148.clone.1), padding=0_0_0x0_3_3x0_3_3 | pad | bytes 2611204 | tf_op jit(solution)/shard_map/while/body/eval_jaxpr/transpose(jvp(jit(_pad)))/pad | solution.py:82
  628.9 8.0 pad.334
  637.0 7.9 pad.466
  644.9 7.9 pad.467
  652.8 8.0 pad.468
  660.8 8.0 pad.465
  668.8 8.1 pad.279
  677.0 8.1 pad.278
  685.1 8.4 pad.277
  697.5 4.4 bitcast_add_fusion
  704.2 7.5 multiply_reduce_fusion.9
  715.5 14.3 %multiply_reduce_fusion.8 = (f32[96]{0:T(128)}, f32[96]{0:T(128)}, f32[96]{0:T(128)}, f32[96]{0:T(128)}, f32[96]{0:T(128)}, /*index=5*/f32[96]{0:T(128)}, f32[96...) fusion(f32[96,80,80]{0,2,1:T(8,128)} %bitcast.291, ...), kind=kLoop, calls=%fused_computation.106 | loop fusion | flops 15359232 | bytes 27040128 | tf_op jit(solution)/shard_map/while/body/eval_jaxpr/transpose(jvp())/reduce_sum | solution.py:90
  743.4 7.3 fusion.47
  751.6 6.0 fusion.42
  757.6 8.2 pad_add_fusion.1
  765.9 6.6 convert_reduce_fusion.1
  799.0 4.1 fusion.59
  803.2 14.0 %concatenate.16 = f32[144960]{0:T(1024)} concatenate(f32[27648]{0:T(1024)S(1)} %reshape.721, f32[288]{0:T(512)S(1)} %get-tuple-element.206, f32[864]{0:T(1024)S(1)} %reshape.722, f32[864]{0:T(1024)S(1)} %reshape.723, f32[864]{0:T(1024)S(1)} %reshape.724, f32[15264]{0:T(1024)S(1)} %reshape.726, f32[15264]{0:T(1024)S(1)} %reshape.728, f32[9216]{0:T(1024)S(1)} %copy-done.82, ...), dimensions={0} | concatenate | bytes 1159680 | tf_op jit(solution)/shard_map/while/body/eval_jaxpr/concatenate | solution.py:309
  818.6 4.7 concatenate.15
  823.4 5.0 fusion.34
  828.4 97.5 %all-reduce.67.cloned.1.call-done = f32[144960]{0:T(1024)} async-done(((f32[144960]{0:T(1024)}), f32[144960]{0:T(1024)}) %all-reduce.67.cloned.1.call-update) | async-done | bytes 579856
  (488 shorter events, 162.3 us)
Async XLA Ops:
  7.2 119.7 %copy-start = (bf16[1,96,6400]{2,1,0:T(8,128)(2,1)S(1)}, bf16[1,96,6400]{2,1,0:T(8,128)(2,1)}, u32[]{:S(2)}) copy-start(bf16[1,96,6400]{2,1,0:T(8,128)(2,1)} %param.7) | copy-start | bytes 3686404
  7.2 116.6 %all-reduce.65.cloned.1.call-start = ((), (), s32[]{:S(2)}) async-start(), calls=%async_computation | async-start | bytes 581632
  11.3 914.5 %all-reduce.67.cloned.1.call-start = ((), (), s32[]{:S(2)}) async-start(), calls=%async_computation.1 | async-start | bytes 1163264
  15.6 112.6 %copy-start.53 = (f32[6400]{0:T(1024)}, f32[6400]{0:T(1024)S(1)}, u32[]{:S(2)}) copy-start(f32[6400]{0:T(1024)S(1)} %broadcast_multiply_fusion.29) | copy-start | bytes 76804
  17.3 106.5 %copy-start.76 = (f32[6400]{0:T(1024)}, f32[6400]{0:T(1024)S(1)}, u32[]{:S(2)}) copy-start(f32[6400]{0:T(1024)S(1)} %fusion.63) | copy-start | bytes 76804
  18.1 326.4 %copy-start.83 = (s32[1600]{0:T(1024)}, s32[1600]{0:T(1024)S(1)}, u32[]{:S(2)}) copy-start(s32[1600]{0:T(1024)S(1)} %sub.139) | copy-start | bytes 19204
  18.2 110.0 %copy-start.70 = (f32[6400]{0:T(1024)}, f32[6400]{0:T(1024)S(1)}, u32[]{:S(2)}) copy-start(f32[6400]{0:T(1024)S(1)} %fusion.112) | copy-start | bytes 76804
  248.6 90.6 %copy-start.72 = (bf16[144960]{0:T(1024)(128)(2,1)S(1)}, bf16[144960]{0:T(1024)(128)(2,1)}, u32[]{:S(2)}) copy-start(bf16[144960]{0:T(1024)(128)(2,1)} %all-reduce.65.cloned.1.call-done) | copy-start | bytes 869764
  258.1 103.0 %copy-start.38 = (f32[96,20,20]{0,2,1:T(8,128)}, f32[96,20,20]{0,2,1:T(8,128)S(1)}, u32[]{:S(2)}) copy-start(f32[96,20,20]{0,2,1:T(8,128)S(1)} %slice.493) | copy-start | bytes 460804
  267.6 93.4 %copy-start.40 = (f32[96,20,20]{0,2,1:T(8,128)}, f32[96,20,20]{0,2,1:T(8,128)S(1)}, u32[]{:S(2)}) copy-start(f32[96,20,20]{0,2,1:T(8,128)S(1)} %slice.491) | copy-start | bytes 460804
  277.2 83.9 %copy-start.42 = (f32[96,20,20]{0,2,1:T(8,128)}, f32[96,20,20]{0,2,1:T(8,128)S(1)}, u32[]{:S(2)}) copy-start(f32[96,20,20]{0,2,1:T(8,128)S(1)} %slice.489) | copy-start | bytes 460804
  286.7 74.4 %copy-start.44 = (f32[96,20,20]{0,2,1:T(8,128)}, f32[96,20,20]{0,2,1:T(8,128)S(1)}, u32[]{:S(2)}) copy-start(f32[96,20,20]{0,2,1:T(8,128)S(1)} %slice.487) | copy-start | bytes 460804
  296.3 64.8 %copy-start.46 = (f32[96,20,20]{0,2,1:T(8,128)}, f32[96,20,20]{0,2,1:T(8,128)S(1)}, u32[]{:S(2)}) copy-start(f32[96,20,20]{0,2,1:T(8,128)S(1)} %slice.485) | copy-start | bytes 460804
  305.8 55.3 %copy-start.48 = (f32[96,20,20]{0,2,1:T(8,128)}, f32[96,20,20]{0,2,1:T(8,128)S(1)}, u32[]{:S(2)}) copy-start(f32[96,20,20]{0,2,1:T(8,128)S(1)} %slice.483) | copy-start | bytes 460804
  342.6 10.5 %copy-start.116 = (f32[96]{0:T(128)S(1)}, f32[96]{0:T(128)}, u32[]{:S(2)}) copy-start(f32[96]{0:T(128)} %get-tuple-element.150) | copy-start | bytes 1156
  342.6 10.5 %copy-start.118 = (f32[96]{0:T(128)S(1)}, f32[96]{0:T(128)}, u32[]{:S(2)}) copy-start(f32[96]{0:T(128)} %get-tuple-element.151) | copy-start | bytes 1156
  342.6 10.5 %copy-start.120 = (f32[96]{0:T(128)S(1)}, f32[96]{0:T(128)}, u32[]{:S(2)}) copy-start(f32[96]{0:T(128)} %get-tuple-element.152) | copy-start | bytes 1156
  342.6 10.5 %copy-start.122 = (f32[96]{0:T(128)S(1)}, f32[96]{0:T(128)}, u32[]{:S(2)}) copy-start(f32[96]{0:T(128)} %get-tuple-element.153) | copy-start | bytes 1156
  344.3 8.9 copy-start.124
  344.3 8.9 copy-start.126
  347.2 40.3 %copy-start.34 = (bf16[80,20,96]{2,1,0:T(8,128)(2,1)}, bf16[80,20,96]{2,1,0:T(8,128)(2,1)S(1)}, u32[]{:S(2)}) copy-start(bf16[80,20,96]{2,1,0:T(8,128)(2,1)S(1)} %reshape.703) | copy-start | bytes 921604
  383.4 15.1 %copy-start.8 = (bf16[96,80,80]{0,2,1:T(8,128)(2,1)}, bf16[96,80,80]{0,2,1:T(8,128)(2,1)S(1)}, u32[]{:S(2)}) copy-start(bf16[96,80,80]{0,2,1:T(8,128)(2,1)S(1)} %get-tuple-element.212) | copy-start | bytes 3686404
  405.8 18.8 %copy-start.61 = (f32[96,20,20]{0,2,1:T(8,128)S(1)}, f32[96,20,20]{0,2,1:T(8,128)}, u32[]{:S(2)}) copy-start(f32[96,20,20]{0,2,1:T(8,128)} %multiply_add_fusion.2) | copy-start | bytes 460804
  430.7 36.5 %copy-start.2 = (f32[96,6400]{1,0:T(8,128)}, f32[96,6400]{1,0:T(8,128)S(1)}, u32[]{:S(2)}) copy-start(f32[96,6400]{1,0:T(8,128)S(1)} %get-tuple-element.264) | copy-start | bytes 7372804
  432.0 24.6 %copy-start.28 = (bf16[1,96,6400]{2,1,0:T(8,128)(2,1)S(1)}, bf16[1,96,6400]{2,1,0:T(8,128)(2,1)}, u32[]{:S(2)}) copy-start(bf16[1,96,6400]{2,1,0:T(8,128)(2,1)} %param.9) | copy-start | bytes 3686404
  432.0 24.6 %copy-start.73 = (bf16[96,384]{1,0:T(8,128)(2,1)S(1)}, bf16[96,384]{1,0:T(8,128)(2,1)}, u32[]{:S(2)}) copy-start(bf16[96,384]{1,0:T(8,128)(2,1)} %reshape.707) | copy-start | bytes 221188
  478.5 9.1 slice-start
  526.9 22.3 %copy-start.64 = (f32[96,20,20]{0,2,1:T(8,128)S(1)}, f32[96,20,20]{0,2,1:T(8,128)}, u32[]{:S(2)}) copy-start(f32[96,20,20]{0,2,1:T(8,128)} %get-tuple-element.242) | copy-start | bytes 460804
  538.1 19.1 %copy-start.62 = (f32[96,20,20]{0,2,1:T(8,128)S(1)}, f32[96,20,20]{0,2,1:T(8,128)}, u32[]{:S(2)}) copy-start(f32[96,20,20]{0,2,1:T(8,128)} %get-tuple-element.243) | copy-start | bytes 460804
  589.1 16.1 %copy-start.96 = (f32[400]{0:T(512)S(1)}, f32[400]{0:T(512)}, u32[]{:S(2)}) copy-start(f32[400]{0:T(512)} %broadcast_multiply_fusion.31) | copy-start | bytes 4804
  605.2 9.2 copy-start.39
  605.2 9.2 copy-start.41
  605.2 9.2 copy-start.43
  605.2 9.2 copy-start.45
  605.2 9.2 copy-start.47
  605.2 9.2 copy-start.49
  605.2 9.2 copy-start.50
  605.2 9.2 copy-start.99
  605.3 9.2 copy-start.101
  605.3 9.2 copy-start.103
  605.3 9.2 copy-start.105
  605.3 9.2 copy-start.107
  605.3 9.2 copy-start.109
  605.3 9.2 copy-start.111
  605.3 9.2 copy-start.113
  605.3 9.2 copy-start.115
  617.8 11.2 %copy-start.66 = (f32[96,20,20]{0,2,1:T(8,128)S(1)}, f32[96,20,20]{0,2,1:T(8,128)}, u32[]{:S(2)}) copy-start(f32[96,20,20]{0,2,1:T(8,128)} %get-tuple-element.255) | copy-start | bytes 460804
  617.8 19.2 %copy-start.65 = (f32[96,20,20]{0,2,1:T(8,128)S(1)}, f32[96,20,20]{0,2,1:T(8,128)}, u32[]{:S(2)}) copy-start(f32[96,20,20]{0,2,1:T(8,128)} %get-tuple-element.251) | copy-start | bytes 460804
  628.9 15.9 %copy-start.63 = (f32[96,20,20]{0,2,1:T(8,128)S(1)}, f32[96,20,20]{0,2,1:T(8,128)}, u32[]{:S(2)}) copy-start(f32[96,20,20]{0,2,1:T(8,128)} %get-tuple-element.252) | copy-start | bytes 460804
  637.0 15.8 %copy-start.60 = (f32[96,20,20]{0,2,1:T(8,128)S(1)}, f32[96,20,20]{0,2,1:T(8,128)}, u32[]{:S(2)}) copy-start(f32[96,20,20]{0,2,1:T(8,128)} %get-tuple-element.253) | copy-start | bytes 460804
  644.9 15.9 %copy-start.59 = (f32[96,20,20]{0,2,1:T(8,128)S(1)}, f32[96,20,20]{0,2,1:T(8,128)}, u32[]{:S(2)}) copy-start(f32[96,20,20]{0,2,1:T(8,128)} %get-tuple-element.250) | copy-start | bytes 460804
  652.8 16.0 %copy-start.58 = (f32[96,20,20]{0,2,1:T(8,128)S(1)}, f32[96,20,20]{0,2,1:T(8,128)}, u32[]{:S(2)}) copy-start(f32[96,20,20]{0,2,1:T(8,128)} %get-tuple-element.256) | copy-start | bytes 460804
  660.8 16.2 %copy-start.57 = (f32[96,20,20]{0,2,1:T(8,128)S(1)}, f32[96,20,20]{0,2,1:T(8,128)}, u32[]{:S(2)}) copy-start(f32[96,20,20]{0,2,1:T(8,128)} %get-tuple-element.257) | copy-start | bytes 460804
  668.8 16.3 %copy-start.56 = (f32[96,20,20]{0,2,1:T(8,128)S(1)}, f32[96,20,20]{0,2,1:T(8,128)}, u32[]{:S(2)}) copy-start(f32[96,20,20]{0,2,1:T(8,128)} %get-tuple-element.258) | copy-start | bytes 460804
  677.0 16.6 %copy-start.37 = (f32[20,6400]{1,0:T(8,128)S(1)}, f32[20,6400]{1,0:T(8,128)}, u32[]{:S(2)}) copy-start(f32[20,6400]{1,0:T(8,128)} %get-tuple-element.95) | copy-start | bytes 1536004
  715.5 14.3 %copy-start.12 = (f32[96,82,82]{0,2,1:T(8,128)S(1)}, f32[96,82,82]{0,2,1:T(8,128)}, u32[]{:S(2)}) copy-start(f32[96,82,82]{0,2,1:T(8,128)} %pad.268) | copy-start | bytes 7746052
  715.5 14.3 %copy-start.13 = (f32[96,82,82]{0,2,1:T(8,128)S(1)}, f32[96,82,82]{0,2,1:T(8,128)}, u32[]{:S(2)}) copy-start(f32[96,82,82]{0,2,1:T(8,128)} %pad.267) | copy-start | bytes 7746052
  715.5 14.3 %copy-start.14 = (f32[96,82,82]{0,2,1:T(8,128)S(1)}, f32[96,82,82]{0,2,1:T(8,128)}, u32[]{:S(2)}) copy-start(f32[96,82,82]{0,2,1:T(8,128)} %pad.266) | copy-start | bytes 7746052
  803.1 20.3 %copy-start.4 = (f32[96,6400]{1,0:T(8,128)S(1)}, f32[96,6400]{1,0:T(8,128)}, u32[]{:S(2)}) copy-start(f32[96,6400]{1,0:T(8,128)} %copy-done.2) | copy-start | bytes 7372804
  803.1 20.3 %copy-start.97 = (f32[96]{0:T(128)S(1)}, f32[96]{0:T(128)}, u32[]{:S(2)}) copy-start(f32[96]{0:T(128)} %get-tuple-element.228) | copy-start | bytes 1156
  823.4 106.8 %copy-start.81 = (f32[9060]{0:T(1024)S(1)}, f32[9060]{0:T(1024)}, u32[]{:S(2)}) copy-start(f32[9060]{0:T(1024)} %param.10) | copy-start | bytes 108724
  823.4 106.8 %copy-start.88 = (f32[9060]{0:T(1024)S(1)}, f32[9060]{0:T(1024)}, u32[]{:S(2)}) copy-start(f32[9060]{0:T(1024)} %param.13) | copy-start | bytes 108724
  823.4 106.8 %copy-start.89 = (f32[9060]{0:T(1024)S(1)}, f32[9060]{0:T(1024)}, u32[]{:S(2)}) copy-start(f32[9060]{0:T(1024)} %param.11) | copy-start | bytes 108724
  823.4 106.8 %copy-start.90 = (f32[9060]{0:T(1024)S(1)}, f32[9060]{0:T(1024)}, u32[]{:S(2)}) copy-start(f32[9060]{0:T(1024)} %param.12) | copy-start | bytes 108724
  (109 other events, 475.0 us)
Sparse Core Ops, SparseCore 0:
  13.8 109.9 all-reduce.64
  817.3 108.5 all-reduce.66
where the time goes:
time: 950 us; the launch traced here: 938 us
  local copies, waits for them, and re-layouts  475 us (50%)
  waiting for transfers between devices  203 us (21%)
  other arithmetic  125 us (13%)
  matrix products  113 us (12%)
  between operations  18.5 us (2%)
    unnamed x4, waiting for transfers between devices  203 us
    slice x18, local copies, waits for them, and re-layouts, depth_pool(): padded[:, row_off:row_off + reach:stride, col_off:col_off + reach:stride]  190 us
    unnamed x354, local copies, waits for them, and re-layouts  80.6 us
    pad x6, local copies, waits for them, and re-layouts, depth_pool(): jnp.pad(field_in.reshape(channels, GRID, GRID), ((0, 0), (1, 1), (1, 1)))  49.8 us
    pad x6, local copies, waits for them, and re-layouts, depth_pool(): padded[:, row_off:row_off + reach:stride, col_off:col_off + reach:stride]  48.8 us
    add_any x6, other arithmetic, depth_pool(): padded[:, row_off:row_off + reach:stride, col_off:col_off + reach:stride]  28.2 us
    dot_general x1, matrix products, forward_parts(): jnp.dot(weights['w_fc1'], normed_two_low, preferred_element_type=jnp.floa...  24.6 us
    reduce_sum x3, other arithmetic, depth_pool(): result = result + kernel[:, row_off * 3 + col_off][:, None, None] * window  20.9 us
  transfers between devices with their start and end apart: 2, of which 2 were waited for; matrix products, arithmetic and copies ran while one was open for 2% of the time, Pallas kernels for 0%

commit v1 on v0

v1 whole, which is shorter than its diff:
```python
import functools
import math

import jax
import jax.numpy as jnp
import numpy as np
from jax import lax
from jax.experimental import pallas as pl
from jax.experimental.pallas import tpu as pltpu
from jax.sharding import PartitionSpec as P

D = 96
HID = 384
KSTR = 4
KG = 20
STEP = 5
GRID = 80
TOK = 6400
KK = 400
REL = 159

norm_eps = 1e-06
beta_first = 0.5
beta_second = 0.5
adam_eps = 1e-08
weight_decay = 0.05
rate_factor = 0.4
average_decay = 0.8

f32 = jnp.float32
bf16 = jnp.bfloat16

HALO = 128
LEAD = 88
FIELD = LEAD + TOK + 8
TILE_ONE = 640
TILE_TWO = 640
TILE_THREE = 640
SCORE_SCALE = D ** (-0.5)
LOG2E = 1.4426950408889634


def segment_list():
    return [
        ("w_qkv", (3 * D, D), D ** (-0.5)),
        ("b_qkv", (3 * D,), 0.2),
        ("pool_q", (D, 9), 1.0 / 3.0),
        ("pool_k", (D, 9), 1.0 / 3.0),
        ("pool_v", (D, 9), 1.0 / 3.0),
        ("rel_h", (REL, D), 0.5 * D ** (-0.5)),
        ("rel_w", (REL, D), 0.5 * D ** (-0.5)),
        ("w_proj", (D, D), D ** (-0.5)),
        ("b_proj", (D,), 0.2),
        ("w_fc1", (HID, D), D ** (-0.5)),
        ("b_fc1", (HID,), 0.2),
        ("w_fc2", (D, HID), HID ** (-0.5)),
        ("b_fc2", (D,), 0.2),
        ("ln1_g", (D,), 0.5),
        ("ln1_b", (D,), 0.2),
        ("ln2_g", (D,), 0.5),
        ("ln2_b", (D,), 0.2),
    ]


def row_bases():
    bases = {}
    offset = 0
    for name, shape, _ in segment_list():
        assert offset % D == 0
        bases[name] = offset // D
        offset += math.prod(shape)
    return bases


ROW = row_bases()


def rate_values(full_len):
    rates = np.full((full_len,), rate_factor * D ** (-0.5), np.float32)
    offset = 0
    for _, shape, spread in segment_list():
        length = math.prod(shape)
        rates[offset : offset + length] = rate_factor * spread
        offset += length
    return rates


def block_rows(shard_len):
    return 16 * (-(-(-(-(shard_len + D - 1) // D)) // 16))


def pool_selectors():
    flat = np.arange(9 * D).reshape(9, D)
    channel = (flat[:, None, :] // 9 == np.arange(D)[None, :, None]).astype(np.float32)
    tap = (flat[:, :, None] % 9 == np.arange(128)[None, None, :]).astype(np.float32)
    return jnp.asarray(channel, bf16), jnp.asarray(tap, bf16)


def lane_index():
    place = np.arange(-HALO, TOK + HALO)
    table = np.zeros((8, TOK + 2 * HALO), np.int32)
    table[0] = place // GRID
    table[1] = place % GRID
    return jnp.asarray(table)


def dot(a, b):
    return lax.dot_general(a, b, (((1,), (0,)), ((), ())), preferred_element_type=f32)


def dot_nt(a, b):
    return lax.dot_general(a, b, (((1,), (1,)), ((), ())), preferred_element_type=f32)


def dot_tn(a, b):
    return lax.dot_general(a, b, (((0,), (0,)), ((), ())), preferred_element_type=f32)


def normalize(values):
    mean = jnp.sum(values, axis=0, keepdims=True) * (1.0 / D)
    center = values - mean
    spread = jnp.sum(center * center, axis=0, keepdims=True) * (1.0 / D)
    inv = lax.rsqrt(spread + norm_eps)
    return center * inv, inv


def normalize_back(grad, unit, inv):
    mean = jnp.sum(grad, axis=0, keepdims=True) * (1.0 / D)
    along = jnp.sum(grad * unit, axis=0, keepdims=True) * (1.0 / D)
    return inv * (grad - mean - unit * along)


def gelu_both(v):
    e = jnp.exp2((v * v) * (-0.5 * LOG2E))
    t = 1.0 / (1.0 + (0.3275911 * math.sqrt(0.5)) * jnp.abs(v))
    series = 0.5 * 1.061405429
    for coef in (-1.453152027, 1.421413741, -0.284496736, 0.254829592):
        series = series * t + 0.5 * coef
    tail = series * t * e
    below = jnp.where(v < 0, tail, 1.0 - tail)
    return v * below, below + (v * (1.0 / math.sqrt(2.0 * math.pi))) * e


def skew_in(rows, place, width):
    where = jnp.broadcast_to(place, (40, width))
    residue = where & 3
    picked = jnp.where(
        residue < 2,
        jnp.where(residue == 0, rows[0:40], rows[40:80]),
        jnp.where(residue == 2, rows[80:120], rows[120:160]),
    )
    shift = where >> 2
    for step in (16, 8, 4, 2, 1):
        picked = jnp.where((shift & step) != 0, pltpu.roll(picked, 40 - step, 0), picked)
    return picked[0:32]


def skew_out(rows, place, width, put):
    where = jnp.broadcast_to(place, (40, width))
    spread = jnp.concatenate([rows, jnp.zeros((8, width), f32)], axis=0)
    shift = where >> 2
    for step in (1, 2, 4, 8, 16):
        spread = jnp.where((shift & step) != 0, pltpu.roll(spread, step, 0), spread)
    residue = where & 3
    for k in range(4):
        put(k, jnp.where(residue == k, spread, 0.0))


def fold_lanes(values):
    width = values.shape[1]
    total = values[:, 0:128]
    for k in range(1, width // 128):
        total = total + values[:, k * 128 : (k + 1) * 128]
    return total


def column_row(column):
    return jnp.transpose(jnp.broadcast_to(column, (D, 128)))[0:1, :]


def image_kernel(
    starts,
    rows_of,
    side_ref,
    chunk_ref,
    x_ref,
    gy_ref,
    idx_ref,
    zsel_ref,
    tsel_ref,
    out_ref,
    gin_ref,
    gchunk_ref,
    wf, wq, wqt, wkt, wvt, wp, wpt, w1, w1t, w2, w2t, rel, relt, cols, kq, kk, kv,
    fq, fk, fv, gfk, gfv, qb, gq, gm,
    a1, a2, vb, vbt, kp, vpool,
    rhs, gse, aaug, n2aug, oaug, n1aug,
    dw2, dw1, dpr, gv, gkr, ln2acc, dwq, dwk, dwv, ln1acc, kqacc, gkt, gvt, gr,
):
    side = side_ref[0]

    wf[...] = jnp.zeros(wf.shape, f32)
    for w, start in enumerate(starts):
        wf[start : start + rows_of, 0:D] += chunk_ref[w].astype(f32)

    def piece(name, count, first=0):
        base = ROW[name] + first
        return wf[base : base + count, :]

    wq[...] = piece("w_qkv", D)[:, :D].astype(bf16)
    wqt[...] = jnp.transpose(piece("w_qkv", D))[:D, :].astype(bf16)
    wkt[...] = jnp.zeros(wkt.shape, bf16)
    wvt[...] = jnp.zeros(wvt.shape, bf16)
    wkt[:, 0:D] = jnp.transpose(piece("w_qkv", D, D))[:D, :].astype(bf16)
    wvt[:, 0:D] = jnp.transpose(piece("w_qkv", D, 2 * D))[:D, :].astype(bf16)
    wp[...] = piece("w_proj", D)[:, :D].astype(bf16)
    wpt[...] = jnp.transpose(piece("w_proj", D))[:D, :].astype(bf16)
    w1[...] = piece("w_fc1", HID)[:, :D].astype(bf16)
    w1t[...] = jnp.transpose(piece("w_fc1", HID))[:D, :].astype(bf16)
    for k in range(4):
        block = wf[pl.ds(ROW["w_fc2"] + k, D, stride=4), :]
        w2t[k * D : (k + 1) * D, :] = jnp.transpose(block)[:D, :].astype(bf16)
    w2[...] = jnp.transpose(w2t[...].astype(f32)).astype(bf16)
    for k in range(4):
        rel[k * 40 : k * 40 + 40, :] = wf[pl.ds(ROW["rel_h"] + 3 + k, 40, stride=4), :][:, :D].astype(bf16)
        rel[160 + k * 40 : 200 + k * 40, :] = wf[pl.ds(ROW["rel_w"] + 3 + k, 40, stride=4), :][:, :D].astype(bf16)
    relt[...] = jnp.transpose(rel[...].astype(f32)).astype(bf16)

    vec_rows = [ROW["b_qkv"], ROW["b_proj"], ROW["b_fc2"], ROW["ln1_g"], ROW["ln1_b"], ROW["ln2_g"], ROW["ln2_b"]]
    vec_rows += [ROW["b_fc1"] + k for k in range(4)]
    stacked = jnp.concatenate([wf[r : r + 1, :] for r in vec_rows] + [jnp.zeros((128 - len(vec_rows), 128), f32)], axis=0)
    cols[...] = jnp.transpose(stacked)[:D, :]

    def pool_columns(name):
        total = jnp.zeros((D, 128), f32)
        for i in range(9):
            row = wf[ROW[name] + i : ROW[name] + i + 1, :][:, :D]
            total = total + dot((zsel_ref[i].astype(f32) * row).astype(bf16), tsel_ref[i])
        return total

    def pool_rows(name):
        full = jnp.concatenate([pool_columns(name), jnp.zeros((32, 128), f32)], axis=0)
        return jnp.transpose(full)[0:16, :]

    kq[...] = pool_columns("pool_q")
    kk[...] = pool_rows("pool_k")
    kv[...] = pool_rows("pool_v")

    b_q, b_proj, b_fc2 = cols[:, 0:1], cols[:, 1:2], cols[:, 2:3]
    ln1_g, ln1_b, ln2_g, ln2_b = cols[:, 3:4], cols[:, 4:5], cols[:, 5:6], cols[:, 6:7]
    b_fc1 = jnp.concatenate([cols[:, 7 + k : 8 + k] for k in range(4)], axis=0)
    b_k = wf[ROW["b_qkv"] + 1 : ROW["b_qkv"] + 2, :]
    b_v = wf[ROW["b_qkv"] + 2 : ROW["b_qkv"] + 3, :]

    for ref in (fq, gq):
        ref[:, 0:HALO] = jnp.zeros((D, HALO), f32)
        ref[:, HALO + TOK :] = jnp.zeros((D, HALO), f32)
    for ref in (fk, fv):
        ref[0:LEAD, :] = jnp.zeros((LEAD, 128), f32)
    for ref in (gfk, gfv, gr, dw2, dw1, dpr, gv, gkr, ln2acc, dwq, dwk, dwv, ln1acc, kqacc):
        ref[...] = jnp.zeros(ref.shape, ref.dtype)

    def first_row_one(width):
        return jnp.where(lax.broadcasted_iota(jnp.int32, (16, width), 0) == 0, 1.0, 0.0).astype(bf16)

    n1aug[D:, :] = first_row_one(TILE_ONE)
    n2aug[D:, :] = first_row_one(TILE_TWO)
    oaug[D:, :] = first_row_one(TILE_TWO)
    aaug[HID:, :] = first_row_one(TILE_TWO)
    rhs[160:176, :] = first_row_one(TILE_TWO)

    def window(i, tile):
        return pl.ds(pl.multiple_of(i * tile, 128), tile + 2 * HALO)

    def inner(i, tile):
        return pl.ds(pl.multiple_of(i * tile + HALO, 128), tile)

    def plain(i, tile):
        return pl.ds(pl.multiple_of(i * tile, 128), tile)

    def token_mask(i, tile):
        place = idx_ref[0:2, inner(i, tile)]
        return jnp.where((place[0:1] < side) & (place[1:2] < side), 1.0, 0.0)

    def project(i, carry):
        unit, _ = normalize(x_ref[:, plain(i, TILE_ONE)].astype(f32))
        low = (unit * ln1_g + ln1_b).astype(bf16)
        fq[:, inner(i, TILE_ONE)] = (dot(wq[...], low) + b_q) * token_mask(i, TILE_ONE)
        field = pl.ds(pl.multiple_of(i * TILE_ONE + LEAD, 8), TILE_ONE)
        fk[field, :] = dot_tn(low, wkt[...]) + b_k
        fv[field, :] = dot_tn(low, wvt[...]) + b_v
        return carry

    lax.fori_loop(0, TOK // TILE_ONE, project, 0)

    def pool_queries(i, carry):
        tile = TILE_ONE
        wide = tile + 2 * HALO
        field = fq[:, window(i, tile)]
        col = jnp.broadcast_to(idx_ref[1:2, window(i, tile)], (D, wide))
        left = jnp.where(col != 0, pltpu.roll(field, 1, 1), 0.0)
        right = jnp.where(col != GRID - 1, pltpu.roll(field, wide - 1, 1), 0.0)

        def row_sum(u):
            return kq[:, 3 * u : 3 * u + 1] * left + kq[:, 3 * u + 1 : 3 * u + 2] * field + kq[:, 3 * u + 2 : 3 * u + 3] * right

        total = pltpu.roll(row_sum(0), GRID, 1) + row_sum(1) + pltpu.roll(row_sum(2), wide - GRID, 1)
        qb[:, plain(i, tile)] = (total[:, HALO : HALO + tile] * token_mask(i, tile)).astype(bf16)
        return carry

    lax.fori_loop(0, TOK // TILE_ONE, pool_queries, 0)

    b_index = lax.broadcasted_iota(jnp.int32, (KG, 128), 0)

    def tap_start(a, u, v):
        return LEAD + GRID * (KSTR * a + u - 1) + v - 1

    for field, kernel_rows, pooled in ((fk, kk, kp), (fv, kv, vpool)):
        for a in range(KG):
            total = jnp.zeros((KG, 128), f32)
            for u in range(3):
                for v in range(3):
                    block = field[pl.ds(tap_start(a, u, v), KG, stride=KSTR), :]
                    if v == 0:
                        block = jnp.where(b_index == 0, 0.0, block)
                    total = total + kernel_rows[3 * u + v : 3 * u + v + 1, :] * block
            keep = (KSTR * b_index < side) & (KSTR * a < side)
            pooled[KG * a : KG * a + KG, :] = jnp.where(keep, total, 0.0)

    key = lax.broadcasted_iota(jnp.int32, (KK, 80), 0)
    key_a = idx_key = lax.div(key, KG)
    key_b = key - KG * idx_key
    place = lax.broadcasted_iota(jnp.int32, (KK, 80), 1)
    one_a = (place < 32) & (KG - 1 - key_a == place)
    one_b = (place >= 32) & (place < 64) & (KG - 1 - key_b == place - 32)
    hot = jnp.where(one_a | one_b, 1.0, 0.0)
    shut = (place == 64) & ((KSTR * key_a >= side) | (KSTR * key_b >= side))
    a1[:, 0:D] = kp[...][:, :D].astype(bf16)
    a1[:, D : D + 80] = jnp.where(shut, -1e30, hot).astype(bf16)
    vbt[...] = vpool[...][:, :D].astype(bf16)
    a2[0:D, :] = jnp.transpose(kp[...])[:D, :].astype(bf16)
    vb[...] = jnp.transpose(vpool[...])[:D, :].astype(bf16)
    key_l = lax.broadcasted_iota(jnp.int32, (64, KK), 1)
    a_l = lax.div(key_l, KG)
    b_l = key_l - KG * a_l
    row_l = lax.broadcasted_iota(jnp.int32, (64, KK), 0)
    hot_l = ((row_l < 32) & (KG - 1 - a_l == row_l)) | ((row_l >= 32) & (KG - 1 - b_l == row_l - 32))
    a2[D : D + 64, :] = jnp.where(hot_l, 1.0, 0.0).astype(bf16)

    def attend(i, carry):
        tile = TILE_TWO
        here = plain(i, tile)
        mask = token_mask(i, tile)
        row, col = idx_ref[0:1, inner(i, tile)], idx_ref[1:2, inner(i, tile)]
        q = qb[:, here]
        seen = dot(rel[...], q)
        rhs[0:D, :] = q
        rhs[D : D + 32, :] = (skew_in(seen[0:160], row, tile) * math.sqrt(D)).astype(bf16)
        rhs[D + 32 : D + 64, :] = (skew_in(seen[160:320], col, tile) * math.sqrt(D)).astype(bf16)
        scores = dot(a1[...], rhs[...])
        top = jnp.max(scores, axis=0, keepdims=True)
        weight = jnp.exp2((scores - top) * (SCORE_SCALE * LOG2E))
        inv_sum = 1.0 / jnp.sum(weight, axis=0, keepdims=True)
        weight_low = weight.astype(bf16)
        mixed = dot(vb[...], weight_low) * inv_sum
        attended = (mixed + q.astype(f32)).astype(bf16)
        oaug[0:D, :] = attended
        middle = x_ref[:, here].astype(f32) + dot(wp[...], attended) + b_proj
        unit, inv = normalize(middle)
        low = (unit * ln2_g + ln2_b).astype(bf16)
        n2aug[0:D, :] = low
        hidden = dot(w1[...], low) + b_fc1
        active, slope = gelu_both(hidden)
        aaug[0:HID, :] = active.astype(bf16)
        out_ref[:, here] = ((middle + dot(w2[...], aaug[0:HID, :]) + b_fc2) * mask).astype(bf16)

        gy = gy_ref[:, here].astype(f32) * mask
        gy_low = gy.astype(bf16)
        dw2[:, 0:KK] += dot_nt(gy_low, aaug[...])
        gh_low = (slope * dot(w2t[...], gy_low)).astype(bf16)
        dw1[...] += dot_nt(n2aug[...], gh_low)
        gn = dot(w1t[...], gh_low)
        ln2acc[0] += fold_lanes(gn * unit)
        ln2acc[1] += fold_lanes(gn)
        gmid = gy + normalize_back(gn * ln2_g, unit, inv)
        gm[:, here] = gmid
        gm_low = gmid.astype(bf16)
        dpr[:, 0:112] += dot_nt(gm_low, oaug[...])
        go = dot(wpt[...], gm_low)
        go_low = (go * inv_sum).astype(bf16)
        delta = jnp.sum(go_low.astype(f32) * mixed, axis=0, keepdims=True)
        gv[:, 0:KK] += dot_nt(go_low, weight_low)
        gs = weight * (dot(vbt[...], go_low) - delta)
        gse[0:KK, :] = gs.astype(bf16)
        back = dot(a2[...], gse[0:KK, :])

        def put(base):
            def write(k, block):
                gse[base + 40 * k : base + 40 * k + 40, :] = block.astype(bf16)

            return write

        skew_out(back[D : D + 32], row, tile, put(KK))
        skew_out(back[D + 32 : D + 64], col, tile, put(KK + 160))
        gkr[:, 0:720] += dot_nt(q, gse[...])
        gq[:, inner(i, tile)] = go + SCORE_SCALE * back[0:D] + dot(relt[...], gse[KK:720, :])
        return carry

    lax.fori_loop(0, TOK // TILE_TWO, attend, 0)

    gkt[...] = jnp.transpose(gkr[:, 0:512])[0:KK, :] * SCORE_SCALE
    gvt[...] = jnp.transpose(gv[...])[0:KK, :]

    def pool_gradient(name, columns):
        low = columns.astype(bf16)
        for i in range(9):
            spread = dot_nt(low, tsel_ref[i]) * zsel_ref[i].astype(f32)
            gr[ROW[name] + i : ROW[name] + i + 1, 0:D] = jnp.sum(spread, axis=0, keepdims=True)

    for field, kernel_rows, pooled, gfield, name in ((fk, kk, gkt, gfk, "pool_k"), (fv, kv, gvt, gfv, "pool_v")):
        sums = []
        for u in range(3):
            for v in range(3):
                total = jnp.zeros((KG, D), f32)
                for a in range(KG):
                    where = pl.ds(tap_start(a, u, v), KG, stride=KSTR)
                    grad = pooled[KG * a : KG * a + KG, :]
                    if v == 0:
                        grad = jnp.where(b_index[:, :D] == 0, 0.0, grad)
                    total = total + grad * field[where, :][:, :D]
                    spread = kernel_rows[3 * u + v : 3 * u + v + 1, :][:, :D] * grad
                    gfield[where, :] = jnp.concatenate([spread, jnp.zeros((KG, 128 - D), f32)], axis=1)
                sums.append(jnp.sum(total, axis=0, keepdims=True))
        rows = jnp.concatenate(sums + [jnp.zeros((128 - 9, D), f32)], axis=0)
        pool_gradient(name, jnp.transpose(rows))

    def finish(i, carry):
        tile = TILE_THREE
        wide = tile + 2 * HALO
        here = plain(i, tile)
        mid = slice(HALO, HALO + tile)
        mask = token_mask(i, tile)
        grad = gq[:, window(i, tile)]
        col = jnp.broadcast_to(idx_ref[1:2, window(i, tile)], (D, wide))
        after = jnp.where(col != GRID - 1, pltpu.roll(grad, wide - 1, 1), 0.0)
        before = jnp.where(col != 0, pltpu.roll(grad, 1, 1), 0.0)

        def row_sum(u):
            return kq[:, 3 * u : 3 * u + 1] * after + kq[:, 3 * u + 1 : 3 * u + 2] * grad + kq[:, 3 * u + 2 : 3 * u + 3] * before

        total = pltpu.roll(row_sum(0), wide - GRID, 1) + row_sum(1) + pltpu.roll(row_sum(2), GRID, 1)
        gq_low = (total[:, mid] * mask).astype(bf16)
        field = fq[:, window(i, tile)]
        for u, rows in enumerate((pltpu.roll(field, GRID, 1), field, pltpu.roll(field, wide - GRID, 1))):
            for v, moved in enumerate((after, grad, before)):
                kqacc[3 * u + v] += fold_lanes(moved[:, mid] * rows[:, mid])

        unit, inv = normalize(x_ref[:, here].astype(f32))
        n1aug[0:D, :] = (unit * ln1_g + ln1_b).astype(bf16)
        flat = pl.ds(pl.multiple_of(i * tile + LEAD, 8), tile)
        gk_low = gfk[flat, :].astype(bf16)
        gv_low = gfv[flat, :].astype(bf16)
        dwq[:, 0:112] += dot_nt(gq_low, n1aug[...])
        dwk[...] += dot(n1aug[...], gk_low)
        dwv[...] += dot(n1aug[...], gv_low)
        gn = dot(wqt[...], gq_low) + dot_nt(wkt[...], gk_low) + dot_nt(wvt[...], gv_low)
        ln1acc[0] += fold_lanes(gn * unit)
        ln1acc[1] += fold_lanes(gn)
        gin_ref[:, here] = (gm[:, here] + normalize_back(gn * ln1_g, unit, inv)).astype(bf16)
        return carry

    lax.fori_loop(0, TOK // TILE_THREE, finish, 0)

    def write(name, rows, first=0):
        base = ROW[name] + first
        gr[base : base + rows.shape[0], 0:D] = rows

    write("w_qkv", dwq[:, 0:D])
    write("b_qkv", jnp.transpose(dwq[...])[D : D + 1, :])
    for k, ref in ((1, dwk), (2, dwv)):
        write("w_qkv", jnp.transpose(ref[0:D, :])[0:D, :], k * D)
        write("b_qkv", ref[D : D + 1, 0:D], k)
    lane = lax.broadcasted_iota(jnp.int32, (D, 128), 1)
    columns = jnp.zeros((D, 128), f32)
    for k in range(9):
        columns = jnp.where(lane == k, jnp.sum(kqacc[k], axis=1, keepdims=True), columns)
    pool_gradient("pool_q", columns)
    rel_rows = jnp.transpose(gkr[:, 384:768])[16:336, :]
    gse_rows = rel_rows
    for k in range(4):
        gr[pl.ds(ROW["rel_h"] + 3 + k, 39, stride=4), :] = jnp.concatenate(
            [gse_rows[40 * k : 40 * k + 39], jnp.zeros((39, 128 - D), f32)], axis=1
        )
        gr[pl.ds(ROW["rel_w"] + 3 + k, 39, stride=4), :] = jnp.concatenate(
            [gse_rows[160 + 40 * k : 160 + 40 * k + 39], jnp.zeros((39, 128 - D), f32)], axis=1
        )
    write("w_proj", dpr[:, 0:D])
    write("b_proj", jnp.transpose(dpr[...])[D : D + 1, :])
    write("w_fc1", jnp.transpose(dw1[0:D, :]))
    for k in range(4):
        write("b_fc1", dw1[D : D + 1, k * D : (k + 1) * D], k)
        gr[pl.ds(ROW["w_fc2"] + k, D, stride=4), :] = jnp.concatenate(
            [dw2[:, k * D : (k + 1) * D], jnp.zeros((D, 128 - D), f32)], axis=1
        )
    write("b_fc2", jnp.transpose(dw2[:, HID:512])[0:1, :])
    write("ln1_g", column_row(jnp.sum(ln1acc[0], axis=1, keepdims=True)))
    write("ln1_b", column_row(jnp.sum(ln1acc[1], axis=1, keepdims=True)))
    write("ln2_g", column_row(jnp.sum(ln2acc[0], axis=1, keepdims=True)))
    write("ln2_b", column_row(jnp.sum(ln2acc[1], axis=1, keepdims=True)))
    for w, start in enumerate(starts):
        gchunk_ref[w] = gr[start : start + rows_of, 0:D].astype(bf16)


def image_step(starts, rows_of, chunks, pixels, image_side, cotangent):
    depth = 8 * (-(-(starts[-1] + rows_of) // 8))
    zsel, tsel = pool_selectors()
    vm = pltpu.VMEM
    scratch = [
        vm((depth, 128), f32),
        vm((D, D), bf16), vm((D, D), bf16), vm((D, 128), bf16), vm((D, 128), bf16),
        vm((D, D), bf16), vm((D, D), bf16),
        vm((HID, D), bf16), vm((D, HID), bf16), vm((D, HID), bf16), vm((HID, D), bf16),
        vm((320, D), bf16), vm((D, 320), bf16), vm((D, 128), f32), vm((D, 128), f32),
        vm((16, 128), f32), vm((16, 128), f32),
        vm((D, TOK + 2 * HALO), f32), vm((FIELD, 128), f32), vm((FIELD, 128), f32),
        vm((FIELD, 128), f32), vm((FIELD, 128), f32),
        vm((D, TOK), bf16), vm((D, TOK + 2 * HALO), f32), vm((D, TOK), f32),
        vm((KK, 176), bf16), vm((160, KK), bf16), vm((D, KK), bf16), vm((KK, D), bf16),
        vm((KK, 128), f32), vm((KK, 128), f32),
        vm((176, TILE_TWO), bf16), vm((720, TILE_TWO), bf16), vm((KK, TILE_TWO), bf16),
        vm((112, TILE_TWO), bf16), vm((112, TILE_TWO), bf16), vm((112, TILE_THREE), bf16),
        vm((D, 512), f32), vm((112, HID), f32), vm((D, 128), f32), vm((D, 512), f32), vm((D, 768), f32),
        vm((2, D, 128), f32), vm((D, 128), f32), vm((112, 128), f32), vm((112, 128), f32),
        vm((2, D, 128), f32), vm((9, D, 128), f32), vm((KK, D), f32), vm((KK, D), f32),
        vm((depth, 128), f32),
    ]
    whole = pl.BlockSpec(memory_space=pltpu.VMEM)
    return pl.pallas_call(
        functools.partial(image_kernel, starts, rows_of),
        out_shape=(
            jax.ShapeDtypeStruct((D, TOK), bf16),
            jax.ShapeDtypeStruct((D, TOK), bf16),
            jax.ShapeDtypeStruct((len(starts), rows_of, D), bf16),
        ),
        in_specs=[pl.BlockSpec(memory_space=pltpu.SMEM)] + [whole] * 6,
        out_specs=(whole, whole, whole),
        scratch_shapes=scratch,
        compiler_params=pltpu.CompilerParams(vmem_limit_bytes=60 * 1024 * 1024),
        name="image_step",
    )(image_side, chunks, pixels, cotangent, lane_index(), zsel, tsel)


def adam_update(gradient, master_part, first_part, second_part, average_part, step_rates):
    moment_one = beta_first * first_part + (1.0 - beta_first) * gradient
    moment_two = beta_second * second_part + (1.0 - beta_second) * gradient * gradient
    fix_one = 1.0 - beta_first**STEP
    fix_two = 1.0 - beta_second**STEP
    direction = moment_one / fix_one / (jnp.sqrt(moment_two / fix_two) + adam_eps)
    updated = master_part - step_rates * (direction + weight_decay * master_part)
    blended = average_decay * average_part + (1.0 - average_decay) * updated
    return (updated, moment_one, moment_two, blended)


def shards(tokens, image_sides, grad_out, master, first_moment, second_moment, weight_average):
    shard_len = master.shape[0]
    owners = lax.axis_size("wide")
    images_all = tokens.shape[0] * owners * lax.axis_size("narrow")
    starts = tuple((shard_len * w) // D for w in range(owners))
    rows_of = block_rows(shard_len)
    inset = lax.rem(lax.axis_index("wide") * shard_len, D)

    own = lax.dynamic_update_slice(jnp.zeros((rows_of * D,), bf16), master.astype(bf16), (inset,))
    own = jnp.broadcast_to(own.reshape(1, rows_of, D), (owners, rows_of, D))
    chunks = lax.all_to_all(own, "wide", 0, 0)

    outs, grads_in, grad_chunks = [], [], None
    for k in range(tokens.shape[0]):
        out, grad_in, chunk = image_step(starts, rows_of, chunks, tokens[k], image_sides[k : k + 1], grad_out[k])
        outs.append(out)
        grads_in.append(grad_in)
        grad_chunks = chunk if k == 0 else (grad_chunks.astype(f32) + chunk.astype(f32)).astype(bf16)
    block_out = jnp.stack(outs)
    grad_in = jnp.stack(grads_in)

    parts = lax.all_to_all(grad_chunks, "wide", 0, 0)
    total = jnp.sum(parts.astype(f32), axis=0)
    total = total + lax.ppermute(total, "narrow", [(0, 1), (1, 0)])
    reduced = lax.dynamic_slice(total.reshape(rows_of * D), (inset,), (shard_len,))
    step_rates = lax.dynamic_slice_in_dim(
        jnp.asarray(rate_values(shard_len * owners)), lax.axis_index("wide") * shard_len, shard_len
    )
    updated, moment_one, moment_two, blended = adam_update(
        reduced / images_all, master, first_moment, second_moment, weight_average, step_rates
    )
    return (block_out, grad_in, updated, moment_one, moment_two, blended)


def solution(mesh):
    return jax.shard_map(
        shards,
        mesh=mesh,
        in_specs=(
            P(("wide", "narrow"), None, None),
            P(("wide", "narrow")),
            P(("wide", "narrow"), None, None),
            P("wide"),
            P("wide"),
            P("wide"),
            P("wide"),
        ),
        out_specs=(
            P(("wide", "narrow"), None, None),
            P(("wide", "narrow"), None, None),
            P("wide"),
            P("wide"),
            P("wide"),
            P("wide"),
        ),
        check_vma=False,
    )
```

time: 950 us -> 112 us (0.12); the launches traced: 938 us -> 112 us
  local copies, waits for them, and re-layouts: 475 us -> 2.07 us
  waiting for transfers between devices: 203 us -> 13.2 us
  other arithmetic: 125 us -> 2.4 us
  matrix products: 113 us -> 0 us
  Pallas kernels: 0 us -> 68.8 us
  between operations: 18.5 us -> 1.37 us
  blocking collectives: 3.45 us -> 15.7 us
    slice x29 -> x0, local copies, waits for them, and re-layouts: 208 us -> none  [the longest x18 190 us: depth_pool(): padded[:, row_off:row_off + reach:stride, col_off:col_off + reach:stride]]
    unnamed x4 -> x0, waiting for transfers between devices: 203 us -> none
    dot_general x28 -> x0, matrix products: 113 us -> none  [the longest x1 24.6 us: forward_parts(): jnp.dot(weights['w_fc1'], normed_two_low, preferred_element_type=jnp.floa...]
    pad x12 -> x0, local copies, waits for them, and re-layouts: 98.6 us -> none  [the longest x6 49.8 us: depth_pool(): jnp.pad(field_in.reshape(channels, GRID, GRID), ((0, 0), (1, 1), (1, 1)))]
    unnamed x354 -> x10, local copies, waits for them, and re-layouts: 80.6 us -> 0.76 us
    pallas_call x0 -> x1, Pallas kernels: none -> 68.8 us  [image_step(): pl.pallas_call(functools.partial(image_kernel, starts, rows_of), out_shap...]
    reduce_sum x15 -> x1, other arithmetic: 60.3 us -> 0.08 us  [shards(): total = jnp.sum(parts.astype(f32), axis=0)]
    reshape x32 -> x1, local copies, waits for them, and re-layouts: 49.1 us -> 0.09 us  [shards(): total.reshape(rows_of * D)]
  transfers between devices with their start and end apart: 2 -> 2, of which waited for: 2 -> 2; matrix products, arithmetic and copies ran while one was open for 2% -> 0% of each run, Pallas kernels for 0% -> 0%
where the time goes in v1:
time: 112 us
  Pallas kernels  68.8 us (61%)
  blocking collectives  15.7 us (14%)
  waiting for transfers between devices  13.2 us (12%)
  starting transfers between devices  8.38 us (7%)
  other arithmetic  2.4 us (2%)
  local copies, waits for them, and re-layouts  2.07 us (2%)
  between operations  1.37 us (1%)
    pallas_call x1, Pallas kernels, image_step(): pl.pallas_call(functools.partial(image_kernel, starts, rows_of), out_shap...  68.8 us
    all_to_all x1, blocking collectives, shards(): parts = lax.all_to_all(grad_chunks, 'wide', 0, 0)  15.7 us
    all_to_all x1, waiting for transfers between devices, shards(): chunks = lax.all_to_all(own, 'wide', 0, 0)  12 us
    all_to_all x1, starting transfers between devices, shards(): chunks = lax.all_to_all(own, 'wide', 0, 0)  8.31 us
  transfers between devices with their start and end apart: 2, of which 2 were waited for; matrix products, arithmetic and copies ran while one was open for 0% of the time, Pallas kernels for 0%

profile of v1, /device:TPU:0, one launch (start us, length us, event | category | flops | bytes accessed | tf_op | source)
XLA Modules:
  0.0 112.0 jit_solution(1877883198706291177)
XLA Ops:
  0.6 0.8 convert_element_type.6
  1.4 0.3 dynamic_update_slice.3
  1.7 0.1 broadcast_in_dim.11
  1.8 0.8 broadcast_in_dim.12
  2.6 8.3 %all-to-all-start = ((bf16[16,96,96]{2,1,0:T(8,128)(2,1)}), bf16[16,96,96]{2,1,0:T(8,128)(2,1)S(1)}, u32[]{:S(2)}, u32[]{:S(2)}) async-start(bf16[16,96,96]{2,1,0:T(8,128)(2,1)} %broadcast_in_dim.12), calls=%async_computation | async-start | bytes 786432 | tf_op jit(solution)/shard_map/all_to_all | solution.py:574
  11.6 12.0 %all-to-all-done.chunk_ref = bf16[16,96,96]{2,1,0:T(8,128)(2,1)S(1)} async-done(((bf16[16,96,96]{2,1,0:T(8,128)(2,1)}), bf16[16,96,96]{2,1,0:T(8,128)(2,1)S(1)}, u32[]{:S(2)}, u32[]{:S(2)}) %all-to-all-start) | async-done | bytes 294944 | tf_op jit(solution)/shard_map/all_to_all | solution.py:574
  23.6 0.0 copy-start
  23.6 0.7 copy-done
  24.3 68.8 %image_step.1 = (bf16[96,6400]{1,0:T(8,128)(2,1)}, bf16[96,6400]{1,0:T(8,128)(2,1)}, bf16[16,96,96]{2,1,0:T(8,128)(2,1)}) custom-call(s32[1]{0:T(128)S(6)} %copy.18.side_ref, bf16[16,96,96]{2,1,0:T(8,128)(2,1)} %copy-done, bf16[96,6400]{1,0:T(8,128)(2,1)} %bitcast.4, bf16[96,6400]{1,0:T(8,128)(2,1)} %bitcast.5, s32[8,6656]{1,0:T(8,128)} %constant.49.clone.idx_ref, ...), custom_call_target="tpu_custom_call" | custom-call | tf_op jit(solution)/shard_map/image_step/pallas_call | solution.py:538
  93.2 0.0 copy-start.1
  93.2 0.0 copy-start.2
  93.2 0.0 copy-start.3
  93.2 0.0 copy-start.4
  93.2 15.7 %all_to_all.10 = bf16[16,96,96]{2,1,0:T(8,128)(2,1)S(1)} all-to-all(bf16[16,96,96]{2,1,0:T(8,128)(2,1)} %get-tuple-element.11), channel_id=1, replica_groups=mesh['wide'=16,'narrow'=2] {'wide'}, dimensions={0} | all-to-all | bytes 589824 | tf_op jit(solution)/shard_map/all_to_all | solution.py:585
  108.9 0.1 convert_reduce_fusion
  109.0 0.1 collective-permute-start
  109.1 1.2 %collective-permute-done = f32[96,96]{1,0:T(8,128)S(1)} collective-permute-done((f32[96,96]{1,0:T(8,128)S(1)}, f32[96,96]{1,0:T(8,128)S(1)}, u32[]{:S(2)}, u32[]{:S(2)}) %collective-permute-start) | collective-permute-done | bytes 36896 | tf_op jit(solution)/shard_map/ppermute | solution.py:587
  110.3 0.1 reshape.17
  110.4 0.0 copy-done.1
  110.4 0.0 copy-done.2
  110.4 0.0 copy-done.3
  110.4 0.0 copy-done.4
  110.4 1.5 %multiply_add_fusion = (f32[9060]{0:T(1024)}, f32[9060]{0:T(1024)}, f32[9060]{0:T(1024)}, f32[9060]{0:T(1024)}) fusion(f32[9060]{0:T(1024)S(1)} %copy-done.2, f32[9060]{0:T(1024)S(1)} %copy-done.1, f32[144960]{0:T(1024)} %constant.50.clone, s32[]{:T(128)S(6)} %select_n.8, f32[9216]{0:T(1024)S(1)} %reshape.17, s32[]{:T(128)S(6)} %select_n.7, ...), kind=kLoop, calls=%fused_computation.1 | loop fusion | flops 163080 | bytes 362408 | tf_op jit(solution)/shard_map/add | solution.py:560
  (2 shorter events, 0.0 us)
Async XLA Ops:
  2.6 21.0 %all-to-all-start = ((bf16[16,96,96]{2,1,0:T(8,128)(2,1)}), bf16[16,96,96]{2,1,0:T(8,128)(2,1)S(1)}, u32[]{:S(2)}, u32[]{:S(2)}) async-start(bf16[16,96,96]{2,1,0:T(8,128)(2,1)} %broadcast_in_dim.12), calls=%async_computation | async-start | bytes 786432 | tf_op jit(solution)/shard_map/all_to_all | solution.py:574
  23.6 0.7 copy-start
  93.2 17.2 %copy-start.1 = (f32[9060]{0:T(1024)S(1)}, f32[9060]{0:T(1024)}, u32[]{:S(2)}) copy-start(f32[9060]{0:T(1024)} %param.14) | copy-start | bytes 108724
  93.2 17.2 %copy-start.2 = (f32[9060]{0:T(1024)S(1)}, f32[9060]{0:T(1024)}, u32[]{:S(2)}) copy-start(f32[9060]{0:T(1024)} %param.17) | copy-start | bytes 108724
  93.2 17.3 %copy-start.3 = (f32[9060]{0:T(1024)S(1)}, f32[9060]{0:T(1024)}, u32[]{:S(2)}) copy-start(f32[9060]{0:T(1024)} %param.15) | copy-start | bytes 108724
  93.2 17.3 %copy-start.4 = (f32[9060]{0:T(1024)S(1)}, f32[9060]{0:T(1024)}, u32[]{:S(2)}) copy-start(f32[9060]{0:T(1024)} %param.16) | copy-start | bytes 108724
  109.0 1.3 %collective-permute-start = (f32[96,96]{1,0:T(8,128)S(1)}, f32[96,96]{1,0:T(8,128)S(1)}, u32[]{:S(2)}, u32[]{:S(2)}) collective-permute-start(f32[96,96]{1,0:T(8,128)S(1)} %convert_reduce_fusion), channel_id=1, source_target_pairs={{0,1},{1,0},{2,3},{3,2},{4,5},{5,4},{6,7},{7,6},{8,9},{9,8},{10,11... | collective-permute-start | bytes 110600 | tf_op jit(solution)/shard_map/ppermute | solution.py:587

commit v2 on v1

v2 whole, which is shorter than its diff:
```python
import functools
import math

import jax
import jax.numpy as jnp
import numpy as np
from jax import lax
from jax.experimental import pallas as pl
from jax.experimental.pallas import tpu as pltpu
from jax.sharding import PartitionSpec as P

D = 96
HID = 384
KSTR = 4
KG = 20
STEP = 5
GRID = 80
TOK = 6400
KK = 400
REL = 159

norm_eps = 1e-06
beta_first = 0.5
beta_second = 0.5
adam_eps = 1e-08
weight_decay = 0.05
rate_factor = 0.4
average_decay = 0.8

f32 = jnp.float32
bf16 = jnp.bfloat16

HALO = 128
LEAD = 88
FIELD = LEAD + TOK + 8
TILE_ONE = 6400
TILE_TWO = 1280
TILE_THREE = 1280
SCORE_SCALE = D ** (-0.5)
LOG2E = 1.4426950408889634


def segment_list():
    return [
        ("w_qkv", (3 * D, D), D ** (-0.5)),
        ("b_qkv", (3 * D,), 0.2),
        ("pool_q", (D, 9), 1.0 / 3.0),
        ("pool_k", (D, 9), 1.0 / 3.0),
        ("pool_v", (D, 9), 1.0 / 3.0),
        ("rel_h", (REL, D), 0.5 * D ** (-0.5)),
        ("rel_w", (REL, D), 0.5 * D ** (-0.5)),
        ("w_proj", (D, D), D ** (-0.5)),
        ("b_proj", (D,), 0.2),
        ("w_fc1", (HID, D), D ** (-0.5)),
        ("b_fc1", (HID,), 0.2),
        ("w_fc2", (D, HID), HID ** (-0.5)),
        ("b_fc2", (D,), 0.2),
        ("ln1_g", (D,), 0.5),
        ("ln1_b", (D,), 0.2),
        ("ln2_g", (D,), 0.5),
        ("ln2_b", (D,), 0.2),
    ]


def row_bases():
    bases = {}
    offset = 0
    for name, shape, _ in segment_list():
        assert offset % D == 0
        bases[name] = offset // D
        offset += math.prod(shape)
    return bases


ROW = row_bases()


def rate_values(full_len):
    rates = np.full((full_len,), rate_factor * D ** (-0.5), np.float32)
    offset = 0
    for _, shape, spread in segment_list():
        length = math.prod(shape)
        rates[offset : offset + length] = rate_factor * spread
        offset += length
    return rates


def block_rows(shard_len):
    return 16 * (-(-(-(-(shard_len + D - 1) // D)) // 16))


def pool_selectors():
    flat = np.arange(9 * D).reshape(9, D)
    channel = (flat[:, None, :] // 9 == np.arange(D)[None, :, None]).astype(np.float32)
    tap = (flat[:, :, None] % 9 == np.arange(128)[None, None, :]).astype(np.float32)
    return jnp.asarray(channel, bf16), jnp.asarray(tap, bf16)


def lane_index():
    place = np.arange(-HALO, TOK + HALO)
    table = np.zeros((8, TOK + 2 * HALO), np.int32)
    table[0] = place // GRID
    table[1] = place % GRID
    return jnp.asarray(table)


def dot(a, b):
    return lax.dot_general(a, b, (((1,), (0,)), ((), ())), preferred_element_type=f32)


def dot_nt(a, b):
    return lax.dot_general(a, b, (((1,), (1,)), ((), ())), preferred_element_type=f32)


def dot_tn(a, b):
    return lax.dot_general(a, b, (((0,), (0,)), ((), ())), preferred_element_type=f32)


def normalize(values):
    mean = jnp.sum(values, axis=0, keepdims=True) * (1.0 / D)
    center = values - mean
    spread = jnp.sum(center * center, axis=0, keepdims=True) * (1.0 / D)
    inv = lax.rsqrt(spread + norm_eps)
    return center * inv, inv


def skew_rows(rows, place):
    width = rows.shape[1]
    where = jnp.broadcast_to(place, (24, width))
    residue = where & 3
    picked = jnp.where(
        residue < 2,
        jnp.where(residue == 0, rows[0:24], rows[24:48]),
        jnp.where(residue == 2, rows[48:72], rows[72:96]),
    )
    picked = jnp.where((where & 8) != 0, pltpu.roll(picked, 22, 0), picked)
    return jnp.where((where & 4) != 0, pltpu.roll(picked, 23, 0), picked)


def skew_columns(rows, place):
    width = rows.shape[1]
    where = jnp.broadcast_to(place, (40, width))
    residue = where & 3
    x = jnp.where(
        residue < 2,
        jnp.where(residue == 0, rows[0:40], rows[40:80]),
        jnp.where(residue == 2, rows[80:120], rows[120:160]),
    )
    x = jnp.concatenate([jnp.where((where[0:24] & 64) != 0, x[16:40], x[0:24]), x[24:40]], axis=0)
    x = jnp.where((where[0:32] & 32) != 0, x[8:40], x[0:32])
    where = where[0:24]
    x = jnp.where((where & 16) != 0, pltpu.roll(x, 28, 0)[0:24], x[0:24])
    x = jnp.where((where & 8) != 0, pltpu.roll(x, 22, 0), x)
    return jnp.where((where & 4) != 0, pltpu.roll(x, 23, 0), x)


def unskew_rows(x, place):
    where = jnp.broadcast_to(place, x.shape)
    x = jnp.where((where & 4) != 0, pltpu.roll(x, 1, 0), x)
    x = jnp.where((where & 8) != 0, pltpu.roll(x, 2, 0), x)
    residue = where & 3
    return jnp.concatenate([jnp.where(residue == k, x, 0.0) for k in range(4)], axis=0)


def unskew_columns(x, place):
    width = x.shape[1]
    zero = jnp.zeros((8, width), f32)
    where = jnp.broadcast_to(place, (40, width))
    x = jnp.where((where[0:24] & 4) != 0, pltpu.roll(x, 1, 0), x)
    x = jnp.where((where[0:24] & 8) != 0, pltpu.roll(x, 2, 0), x)
    x = jnp.concatenate([x, zero], axis=0)
    x = jnp.where((where[0:32] & 16) != 0, pltpu.roll(x, 4, 0), x)
    x = jnp.where((where & 32) != 0, jnp.concatenate([zero, x], axis=0), jnp.concatenate([x, zero], axis=0))
    far = (where & 64) != 0
    x = jnp.concatenate([jnp.where(far[0:16], 0.0, x[0:16]), jnp.where(far[16:40], x[0:24], x[16:40])], axis=0)
    residue = where & 3
    return jnp.concatenate([jnp.where(residue == k, x, 0.0) for k in range(4)], axis=0)


def column_row(column):
    return jnp.transpose(jnp.broadcast_to(column, (D, 128)))[0:1, :]


def two_columns(column):
    high = column.astype(bf16).astype(f32)
    place = lax.broadcasted_iota(jnp.int32, (column.shape[0], 16), 1)
    return jnp.where(place == 0, high, jnp.where(place == 1, column - high, 0.0)).astype(bf16)


def two_rows(row):
    high = row.astype(bf16).astype(f32)
    place = lax.broadcasted_iota(jnp.int32, (16, row.shape[1]), 0)
    return jnp.where(place == 0, high, jnp.where(place == 1, row - high, 0.0)).astype(bf16)


def two_ones(width):
    return jnp.where(lax.broadcasted_iota(jnp.int32, (16, width), 0) < 2, 1.0, 0.0).astype(bf16)


def image_kernel(
    starts,
    rows_of,
    side_ref,
    chunk_ref,
    x_ref,
    gy_ref,
    idx_ref,
    zsel_ref,
    tsel_ref,
    out_ref,
    gin_ref,
    gchunk_ref,
    wf, wq, wqt, wkt, wvt, wkvg, wp, wpt, w1, w1t, w2, w2t, relh, rel, relt, cols, kq, kk, kv,
    fq, fk, fv, gfk, gfv, qb, gq, gm, un, inv1, fcol,
    a1, a2, vb, vbt, kp, vpool,
    rhs, gse, aaug, n1aug, n2aug, oaug, goaug, gsh, gkv,
    dw2, dw1, dpr, gv, gkr, hacc, dwq, dwkv, kqacc, gkt, gvt, gr,
):
    side = side_ref[0]

    wf[...] = jnp.zeros(wf.shape, f32)
    for w, start in enumerate(starts):
        wf[start : start + rows_of, 0:D] += chunk_ref[w].astype(f32)

    def piece(name, count, first=0):
        base = ROW[name] + first
        return wf[base : base + count, :]

    vec_rows = [ROW["b_qkv"], ROW["b_proj"], ROW["b_fc2"], ROW["ln1_g"], ROW["ln1_b"], ROW["ln2_g"], ROW["ln2_b"]]
    vec_rows += [ROW["b_fc1"] + k for k in range(4)]
    stacked = jnp.concatenate([wf[r : r + 1, :] for r in vec_rows] + [jnp.zeros((128 - len(vec_rows), 128), f32)], axis=0)
    cols[...] = jnp.transpose(stacked)[:D, :]
    cols_low = cols[...].astype(bf16)
    g1_row, b1_row = piece("ln1_g", 1), piece("ln1_b", 1)
    g2_row, b2_row = piece("ln2_g", 1), piece("ln2_b", 1)

    def through(name, count, first, column):
        return dot(piece(name, count, first)[:, :D].astype(bf16), cols_low)[:, column : column + 1]

    wq_gain = piece("w_qkv", D) * g1_row
    wq[:, 0:D] = piece("w_qkv", D)[:, :D].astype(bf16)
    wq[:, D:] = two_columns(cols[:, 0:1])
    wqt[...] = jnp.transpose(wq_gain)[:D, :].astype(bf16)
    for k, ref in ((1, wkt), (2, wvt)):
        ref[...] = jnp.zeros(ref.shape, bf16)
        ref[0:D, 0:D] = jnp.transpose(piece("w_qkv", D, k * D))[:D, :].astype(bf16)
        ref[D:, 0:D] = two_rows(piece("b_qkv", 1, k)[:, :D])
        wkvg[:, 128 * k - 128 : 128 * k] = jnp.zeros((D, 128), bf16)
        wkvg[:, 128 * k - 128 : 128 * k - 128 + D] = jnp.transpose(piece("w_qkv", D, k * D) * g1_row)[:D, :].astype(bf16)
    wp[:, 0:D] = piece("w_proj", D)[:, :D].astype(bf16)
    wp[:, D:] = two_columns(cols[:, 1:2])
    wpt[...] = jnp.transpose(piece("w_proj", D))[:D, :].astype(bf16)
    w1_gain = piece("w_fc1", HID) * g2_row
    b_fc1 = jnp.concatenate([cols[:, 7 + k : 8 + k] for k in range(4)], axis=0)
    w1[:, 0:D] = w1_gain[:, :D].astype(bf16)
    w1[:, D:] = two_columns((b_fc1 + through("w_fc1", HID, 0, 6)) * math.sqrt(0.5))
    w1t[...] = jnp.transpose(w1_gain)[:D, :].astype(bf16)
    for k in range(4):
        block = wf[pl.ds(ROW["w_fc2"] + k, D, stride=4), :]
        w2t[k * D : (k + 1) * D, :] = jnp.transpose(block)[:D, :].astype(bf16)
    w2[:, 0:HID] = jnp.transpose(w2t[...].astype(f32)).astype(bf16)
    w2[:, HID:] = two_columns(cols[:, 2:3] * math.sqrt(0.5 * math.pi))
    for k in range(4):
        relh[k * 40 : k * 40 + 40, :] = wf[pl.ds(ROW["rel_h"] + 3 + k, 40, stride=4), :]
    rel_w = jnp.concatenate([wf[pl.ds(ROW["rel_w"] + 3 + k, 40, stride=4), :] for k in range(4)], axis=0)
    rel[D:256, :] = rel_w[:, :D].astype(bf16)
    relt[:, D:256] = jnp.transpose(rel_w)[:D, :].astype(bf16)

    def pool_columns(name):
        total = jnp.zeros((D, 128), f32)
        for i in range(9):
            row = wf[ROW[name] + i : ROW[name] + i + 1, :][:, :D]
            total = total + dot((zsel_ref[i].astype(f32) * row).astype(bf16), tsel_ref[i])
        return total

    def pool_rows(name):
        full = jnp.concatenate([pool_columns(name), jnp.zeros((32, 128), f32)], axis=0)
        return jnp.transpose(full)[0:16, :]

    pooled_kernel = pool_columns("pool_q")
    for k in range(9):
        kq[k] = jnp.broadcast_to(pooled_kernel[:, k : k + 1], (D, 128))

    def tap(k, ch, width):
        return jnp.concatenate([kq[k, ch, :]] * (width // 128), axis=1)

    kk[...] = pool_rows("pool_k")
    kv[...] = pool_rows("pool_v")

    for ref in (fq, gq):
        ref[:, 0:HALO] = jnp.zeros((D, HALO), f32)
        ref[:, HALO + TOK :] = jnp.zeros((D, HALO), f32)
    for ref in (fk, fv):
        ref[0:LEAD, :] = jnp.zeros((LEAD, 128), f32)
    for ref in (dw2, dw1, dpr, gv, gkr, dwq, dwkv, kqacc):
        ref[...] = jnp.zeros(ref.shape, ref.dtype)
    gr[ROW["rel_h"] : ROW["w_proj"], :] = jnp.zeros((2 * REL, 128), f32)
    tail = ROW["ln2_b"]
    gr[tail:, :] = jnp.zeros((gr.shape[0] - tail, 128), f32)

    un[D:, :] = two_ones(TOK)
    n1aug[D:, :] = two_ones(TILE_ONE)
    n2aug[D:, :] = two_ones(TILE_TWO)
    oaug[D:, :] = two_ones(TILE_TWO)
    aaug[HID:, :] = two_ones(TILE_TWO)
    rhs[192:208, :] = two_ones(TILE_TWO)

    def window(i, tile):
        return pl.ds(pl.multiple_of(i * tile, 128), tile + 2 * HALO)

    def inner(i, tile):
        return pl.ds(pl.multiple_of(i * tile + HALO, 128), tile)

    def plain(i, tile):
        return pl.ds(pl.multiple_of(i * tile, 128), tile)

    def token_mask(i, tile):
        place = idx_ref[0:2, inner(i, tile)]
        return jnp.where((place[0:1] < side) & (place[1:2] < side), 1.0, 0.0)

    def project(i, carry):
        here = plain(i, TILE_ONE)
        unit, inv = normalize(x_ref[:, here].astype(f32))
        un[0:D, here] = unit.astype(bf16)
        inv1[0:1, here] = inv
        n1aug[0:D, :] = (unit * cols[:, 3:4] + cols[:, 4:5]).astype(bf16)
        fq[:, inner(i, TILE_ONE)] = dot(wq[...], n1aug[...]) * token_mask(i, TILE_ONE)
        field = pl.ds(pl.multiple_of(i * TILE_ONE + LEAD, 8), TILE_ONE)
        fk[field, :] = dot_tn(n1aug[...], wkt[...])
        fv[field, :] = dot_tn(n1aug[...], wvt[...])
        return carry

    lax.fori_loop(0, TOK // TILE_ONE, project, 0)

    def pool_queries(i, carry):
        tile = TILE_ONE
        wide = tile + 2 * HALO
        mid = slice(HALO, HALO + tile)
        col = jnp.broadcast_to(idx_ref[1:2, window(i, tile)], (8, wide))
        first, last = col == 0, col == GRID - 1
        mask = token_mask(i, tile)
        for pair in range(D // 16):
            pooled, moved = [], []
            for half in range(2):
                ch = slice(16 * pair + 8 * half, 16 * pair + 8 * half + 8)
                field = fq[ch, window(i, tile)]
                left = jnp.where(first, 0.0, pltpu.roll(field, 1, 1))
                right = jnp.where(last, 0.0, pltpu.roll(field, wide - 1, 1))

                def row_sum(u):
                    return tap(3 * u, ch, wide) * left + tap(3 * u + 1, ch, wide) * field + tap(3 * u + 2, ch, wide) * right

                total = pltpu.roll(row_sum(0), GRID, 1) + row_sum(1) + pltpu.roll(row_sum(2), wide - GRID, 1)
                pooled.append(total[:, mid] * mask)
                moved.append((left[:, mid], field[:, mid], right[:, mid]))
            qb[16 * pair : 16 * pair + 16, plain(i, tile)] = jnp.concatenate(pooled, axis=0).astype(bf16)
            for v in range(3):
                both = jnp.concatenate([moved[0][v], moved[1][v]], axis=0)
                fcol[v * D + 16 * pair : v * D + 16 * pair + 16, plain(i, tile)] = both.astype(bf16)
        return carry

    lax.fori_loop(0, TOK // TILE_ONE, pool_queries, 0)

    b_index = lax.broadcasted_iota(jnp.int32, (KG, 128), 0)

    def tap_start(a, u, v):
        return LEAD + GRID * (KSTR * a + u - 1) + v - 1

    def tap_rows(kernel_rows):
        taps = [jnp.broadcast_to(kernel_rows[k : k + 1, :], (KG, 128)) for k in range(9)]
        return [jnp.where(b_index == 0, 0.0, tap) if k % 3 == 0 else tap for k, tap in enumerate(taps)]

    for field, kernel_rows, pooled in ((fk, kk, kp), (fv, kv, vpool)):
        taps = tap_rows(kernel_rows)
        for a in range(KG):
            total = jnp.zeros((KG, 128), f32)
            for k in range(9):
                total = total + taps[k] * field[pl.ds(tap_start(a, k // 3, k % 3), KG, stride=KSTR), :]
            keep = (KSTR * b_index < side) & (KSTR * a < side)
            pooled[KG * a : KG * a + KG, :] = jnp.where(keep, total, 0.0)

    key = lax.broadcasted_iota(jnp.int32, (KK, 112), 0)
    key_a = lax.div(key, KG)
    key_b = key - KG * key_a
    place = lax.broadcasted_iota(jnp.int32, (KK, 112), 1)
    hot = jnp.zeros((KK, 112), f32)
    for base in (0, 48):
        one_a = (place >= base) & (place < base + 24) & (KG - 1 - key_a == place - base)
        one_b = (place >= base + 24) & (place < base + 48) & (KG - 1 - key_b == place - base - 24)
        hot = jnp.where(one_a | one_b, 1.0, hot)
    shut = (place == 96) & ((KSTR * key_a >= side) | (KSTR * key_b >= side))
    a1[:, 0:D] = kp[...][:, :D].astype(bf16)
    a1[:, D:] = jnp.where(shut, -1e30, hot).astype(bf16)
    vbt[:, 0:D] = vpool[...][:, :D].astype(bf16)
    vbt[:, D:] = jnp.where(lax.broadcasted_iota(jnp.int32, (KK, 16), 1) < 2, -1.0, 0.0).astype(bf16)
    a2[0:D, :] = jnp.transpose(kp[...])[:D, :].astype(bf16)
    vb[0:D, :] = jnp.transpose(vpool[...])[:D, :].astype(bf16)
    vb[D:, :] = jnp.ones((16, KK), bf16)
    key_l = lax.broadcasted_iota(jnp.int32, (48, KK), 1)
    a_l = lax.div(key_l, KG)
    b_l = key_l - KG * a_l
    row_l = lax.broadcasted_iota(jnp.int32, (48, KK), 0)
    hot_l = ((row_l < 24) & (KG - 1 - a_l == row_l)) | ((row_l >= 24) & (KG - 1 - b_l == row_l - 24))
    a2[D:, :] = jnp.where(hot_l, 1.0, 0.0).astype(bf16)

    def attend(i, carry):
        tile = TILE_TWO
        here = plain(i, tile)
        mask = token_mask(i, tile)
        row, col = idx_ref[0:1, inner(i, tile)], idx_ref[1:2, inner(i, tile)]
        near = jnp.concatenate([relh[pl.ds(40 * k + 4 * i, 24), :] for k in range(4)], axis=0)
        rel[0:D, :] = near[:, :D].astype(bf16)
        relt[:, 0:D] = jnp.transpose(near)[:D, :].astype(bf16)
        q = qb[:, here]
        seen = dot(rel[...], q)
        rhs[0:D, :] = q
        sides = jnp.concatenate([skew_rows(seen[0:D], row), skew_columns(seen[D:256], col)], axis=0)
        sides = sides * math.sqrt(D)
        sides_low = sides.astype(bf16)
        rhs[D : D + 48, :] = sides_low
        rhs[D + 48 : D + 96, :] = (sides - sides_low.astype(f32)).astype(bf16)
        scores = dot(a1[...], rhs[...])
        weight = jnp.exp2((scores - jnp.max(scores, axis=0, keepdims=True)) * (SCORE_SCALE * LOG2E))
        weight_low = weight.astype(bf16)
        mixed = dot(vb[...], weight_low)
        inv_sum = 1.0 / mixed[D : D + 1]
        mixed = mixed[0:D] * inv_sum
        oaug[0:D, :] = (mixed + q.astype(f32)).astype(bf16)
        middle = x_ref[:, here].astype(f32) + dot(wp[...], oaug[...])

        center = middle - jnp.sum(middle, axis=0, keepdims=True) * (1.0 / D)
        inv = lax.rsqrt(jnp.sum(center * center, axis=0, keepdims=True) * (1.0 / D) + norm_eps)
        half = center * (inv * math.sqrt(0.5))
        n2aug[0:D, :] = half.astype(bf16)
        z = dot(w1[...], n2aug[...])
        below = lax.erf(z) * (0.5 * math.sqrt(math.pi)) + 0.5 * math.sqrt(math.pi)
        aaug[0:HID, :] = (z * below).astype(bf16)
        slope = below + z * jnp.exp2((z * z) * -LOG2E)
        mlp = dot(w2[...], aaug[...])
        out_ref[:, here] = ((middle + mlp * math.sqrt(2.0 / math.pi)) * mask).astype(bf16)

        gy = gy_ref[:, here].astype(f32) * mask
        gy_low = gy.astype(bf16)
        dw2[:, 0:KK] += dot_nt(gy_low, aaug[...])
        gh_low = (slope * dot(w2t[...], gy_low)).astype(bf16)
        dw1[0:112, :] += dot_nt(n2aug[...], gh_low)
        gn = dot(w1t[...], gh_low)
        mean = jnp.sum(gn, axis=0, keepdims=True) * (1.0 / D)
        along = jnp.sum(gn * half, axis=0, keepdims=True) * (2.0 / D)
        gmid = gy + (gn - mean - half * along) * (inv * math.sqrt(1.0 / math.pi))
        gm[:, here] = gmid
        gm_low = gmid.astype(bf16)
        dpr[:, 0:112] += dot_nt(gm_low, oaug[...])
        go = dot(wpt[...], gm_low)
        go_low = (go * inv_sum).astype(bf16)
        goaug[0:D, :] = go_low
        goaug[D:, :] = two_rows(jnp.sum(go_low.astype(f32) * mixed, axis=0, keepdims=True))
        gv[0:D, 0:KK] += dot_nt(go_low, weight_low)
        gse[0:KK, :] = (weight * dot(vbt[...], goaug[...])).astype(bf16)
        back = dot(a2[...], gse[0:KK, :])
        gse[KK : KK + D, :] = unskew_rows(back[D : D + 24], row).astype(bf16)
        gse[KK + D : KK + 256, :] = unskew_columns(back[D + 24 : D + 48], col).astype(bf16)
        flat = pl.ds(pl.multiple_of(i * tile + LEAD, 8), tile)
        gfk[flat, :] = jnp.zeros((tile, 128), f32)
        gfv[flat, :] = jnp.zeros((tile, 128), f32)
        outer = dot_nt(q, gse[...])
        gkr[0:D, 0 : KK + 256] += outer
        hacc[i] = outer[:, 384:512]
        gq[:, inner(i, tile)] = go + SCORE_SCALE * back[0:D] + dot(relt[...], gse[KK : KK + 256, :])
        return carry

    lax.fori_loop(0, TOK // TILE_TWO, attend, 0)

    gkt[...] = jnp.transpose(gkr[:, 0:512])[0:KK, :] * SCORE_SCALE
    gvt[...] = jnp.transpose(gv[...])[0:KK, :]

    def pool_gradient(name, columns):
        low = columns.astype(bf16)
        for i in range(9):
            spread = dot_nt(low, tsel_ref[i]) * zsel_ref[i].astype(f32)
            gr[ROW[name] + i : ROW[name] + i + 1, 0:D] = jnp.sum(spread, axis=0, keepdims=True)

    for field, kernel_rows, pooled, gfield, name in ((fk, kk, gkt, gfk, "pool_k"), (fv, kv, gvt, gfv, "pool_v")):
        taps = tap_rows(kernel_rows)
        sums = [jnp.zeros((KG, 128), f32) for _ in range(9)]
        for a in range(KG):
            grad = pooled[KG * a : KG * a + KG, :]
            inside = jnp.where(b_index == 0, 0.0, grad)
            for k in range(9):
                where = pl.ds(tap_start(a, k // 3, k % 3), KG, stride=KSTR)
                sums[k] = sums[k] + (inside if k % 3 == 0 else grad) * field[where, :]
                gfield[where, :] = taps[k] * grad
        rows = [jnp.sum(total, axis=0, keepdims=True) for total in sums]
        rows = jnp.concatenate(rows + [jnp.zeros((128 - 9, 128), f32)], axis=0)
        pool_gradient(name, jnp.transpose(rows)[:D, :])

    def finish(i, carry):
        tile = TILE_THREE
        wide = tile + 2 * HALO
        here = plain(i, tile)
        mid = slice(HALO, HALO + tile)
        mask = token_mask(i, tile)
        col = jnp.broadcast_to(idx_ref[1:2, inner(i, tile)], (8, tile))
        first, last = col == 0, col == GRID - 1
        for pair in range(D // 16):
            fields, moved = [], []
            for half in range(2):
                ch = slice(16 * pair + 8 * half, 16 * pair + 8 * half + 8)
                grad = gq[ch, window(i, tile)]
                below, above = pltpu.roll(grad, wide - GRID, 1), pltpu.roll(grad, GRID, 1)

                def col_sum(v):
                    return tap(v, ch, wide) * below + tap(v + 3, ch, wide) * grad + tap(v + 6, ch, wide) * above

                after = jnp.where(last, 0.0, pltpu.roll(col_sum(0), wide - 1, 1)[:, mid])
                before = jnp.where(first, 0.0, pltpu.roll(col_sum(2), 1, 1)[:, mid])
                fields.append((after + col_sum(1)[:, mid] + before) * mask)
                moved.append((below[:, mid], grad[:, mid], above[:, mid]))
            gsh[3 * D + 16 * pair : 3 * D + 16 * pair + 16, :] = jnp.concatenate(fields, axis=0).astype(bf16)
            for u in range(3):
                both = jnp.concatenate([moved[0][u], moved[1][u]], axis=0)
                gsh[u * D + 16 * pair : u * D + 16 * pair + 16, :] = both.astype(bf16)
        kqacc[:, 0 : 3 * D] += dot_nt(gsh[0 : 3 * D, :], fcol[:, here])
        gq_low = gsh[3 * D : 4 * D, :]
        flat = pl.ds(pl.multiple_of(i * tile + LEAD, 8), tile)
        gkv[:, 0:128] = gfk[flat, :].astype(bf16)
        gkv[:, 128:256] = gfv[flat, :].astype(bf16)
        dwq[:, 0:112] += dot_nt(gq_low, un[:, here])
        dwkv[0:112, :] += dot(un[:, here], gkv[...])
        gn = dot(wqt[...], gq_low) + dot_nt(wkvg[...], gkv[...])
        unit = un[0:D, here].astype(f32)
        mean = jnp.sum(gn, axis=0, keepdims=True) * (1.0 / D)
        along = jnp.sum(gn * unit, axis=0, keepdims=True) * (1.0 / D)
        gin_ref[:, here] = (gm[:, here] + (gn - mean - unit * along) * inv1[0:1, here]).astype(bf16)
        return carry

    lax.fori_loop(0, TOK // TILE_THREE, finish, 0)

    def write(name, rows, first=0):
        base = ROW[name] + first
        gr[base : base + rows.shape[0], 0:D] = rows

    def wide_rows(rows):
        return jnp.concatenate([rows, jnp.zeros((rows.shape[0], 128 - D), f32)], axis=1)

    def through_norm(name, first, outer, bias, gain_row, shift_row):
        raw = piece(name, outer.shape[0], first)[:, :D]
        write(name, outer * gain_row[:, :D] + bias * shift_row[:, :D], first)
        return jnp.sum(raw * outer, axis=0, keepdims=True), jnp.sum(raw * bias, axis=0, keepdims=True)

    gain, shift = through_norm("w_qkv", 0, dwq[:, 0:D], dwq[:, D : D + 1], g1_row, b1_row)
    write("b_qkv", jnp.transpose(dwq[...])[D : D + 1, :])
    for k in (1, 2):
        turned = jnp.transpose(dwkv[:, 128 * k - 128 : 128 * k])[0:D, :]
        more_gain, more_shift = through_norm("w_qkv", k * D, turned[:, 0:D], turned[:, D : D + 1], g1_row, b1_row)
        gain, shift = gain + more_gain, shift + more_shift
        write("b_qkv", dwkv[D : D + 1, 128 * k - 128 : 128 * k - 128 + D], k)
    write("ln1_g", gain)
    write("ln1_b", shift)

    lane = lax.broadcasted_iota(jnp.int32, (D, 128), 1)
    wide_lane = lax.broadcasted_iota(jnp.int32, (D, 3 * 128), 1) - lax.broadcasted_iota(jnp.int32, (D, 3 * 128), 0)
    columns = jnp.zeros((D, 128), f32)
    for k in range(9):
        u, v = k // 3, k % 3
        one = jnp.where(wide_lane == v * D, kqacc[u * D : u * D + D, :], 0.0)
        columns = jnp.where(lane == k, jnp.sum(one, axis=1, keepdims=True), columns)
    pool_gradient("pool_q", columns)

    for i in range(TOK // TILE_TWO):
        turned = jnp.transpose(hacc[i])
        for k in range(4):
            where = pl.ds(ROW["rel_h"] + 3 + k + 16 * i, 23, stride=4)
            gr[where, :] = gr[where, :] + wide_rows(turned[16 + 24 * k : 39 + 24 * k])
    turned = jnp.transpose(gkr[0:D, 384:768])
    for k in range(4):
        gr[pl.ds(ROW["rel_w"] + 3 + k, 39, stride=4), :] = wide_rows(turned[112 + 40 * k : 151 + 40 * k])

    write("w_proj", dpr[:, 0:D])
    write("b_proj", jnp.transpose(dpr[...])[D : D + 1, :])
    turned = jnp.transpose(dw1[...])
    gain, shift = through_norm(
        "w_fc1", 0, turned[:, 0:D] * math.sqrt(2.0 / math.pi), turned[:, D : D + 1] * math.sqrt(1.0 / math.pi), g2_row, b2_row
    )
    write("ln2_g", gain)
    write("ln2_b", shift)
    for k in range(4):
        write("b_fc1", dw1[D : D + 1, k * D : (k + 1) * D] * math.sqrt(1.0 / math.pi), k)
        gr[pl.ds(ROW["w_fc2"] + k, D, stride=4), :] = wide_rows(dw2[:, k * D : (k + 1) * D] * math.sqrt(2.0 / math.pi))
    write("b_fc2", jnp.transpose(dw2[:, HID:512])[0:1, :])
    for w, start in enumerate(starts):
        gchunk_ref[w] = gr[start : start + rows_of, 0:D].astype(bf16)


def image_step(starts, rows_of, chunks, pixels, image_side, cotangent):
    depth = 8 * (-(-(starts[-1] + rows_of) // 8))
    zsel, tsel = pool_selectors()
    vm = pltpu.VMEM
    scratch = [
        vm((depth, 128), f32),
        vm((D, 112), bf16), vm((D, D), bf16), vm((112, 128), bf16), vm((112, 128), bf16), vm((D, 256), bf16),
        vm((D, 112), bf16), vm((D, D), bf16),
        vm((HID, 112), bf16), vm((D, HID), bf16), vm((D, KK), bf16), vm((HID, D), bf16),
        vm((160, 128), f32), vm((256, D), bf16), vm((D, 256), bf16),
        vm((D, 128), f32), vm((9, D, 128), f32), vm((16, 128), f32), vm((16, 128), f32),
        vm((D, TOK + 2 * HALO), f32), vm((FIELD, 128), f32), vm((FIELD, 128), f32),
        vm((FIELD, 128), f32), vm((FIELD, 128), f32),
        vm((D, TOK), bf16), vm((D, TOK + 2 * HALO), f32), vm((D, TOK), f32),
        vm((112, TOK), bf16), vm((8, TOK), f32), vm((3 * D, TOK), bf16),
        vm((KK, 208), bf16), vm((144, KK), bf16), vm((112, KK), bf16), vm((KK, 112), bf16),
        vm((KK, 128), f32), vm((KK, 128), f32),
        vm((208, TILE_TWO), bf16), vm((KK + 256, TILE_TWO), bf16), vm((KK, TILE_TWO), bf16),
        vm((112, TILE_ONE), bf16), vm((112, TILE_TWO), bf16), vm((112, TILE_TWO), bf16), vm((112, TILE_TWO), bf16),
        vm((4 * D, TILE_THREE), bf16), vm((TILE_THREE, 256), bf16),
        vm((D, 512), f32), vm((128, HID), f32), vm((D, 128), f32), vm((128, 512), f32), vm((128, 768), f32),
        vm((TOK // TILE_TWO, D, 128), f32),
        vm((D, 128), f32), vm((128, 256), f32), vm((3 * D, 3 * 128), f32), vm((KK, 128), f32), vm((KK, 128), f32),
        vm((depth, 128), f32),
    ]
    whole = pl.BlockSpec(memory_space=pltpu.VMEM)
    return pl.pallas_call(
        functools.partial(image_kernel, starts, rows_of),
        out_shape=(
            jax.ShapeDtypeStruct((D, TOK), bf16),
            jax.ShapeDtypeStruct((D, TOK), bf16),
            jax.ShapeDtypeStruct((len(starts), rows_of, D), bf16),
        ),
        in_specs=[pl.BlockSpec(memory_space=pltpu.SMEM)] + [whole] * 6,
        out_specs=(whole, whole, whole),
        scratch_shapes=scratch,
        compiler_params=pltpu.CompilerParams(vmem_limit_bytes=63 * 1024 * 1024),
        name="image_step",
    )(image_side, chunks, pixels, cotangent, lane_index(), zsel, tsel)


def adam_update(gradient, master_part, first_part, second_part, average_part, step_rates):
    moment_one = beta_first * first_part + (1.0 - beta_first) * gradient
    moment_two = beta_second * second_part + (1.0 - beta_second) * gradient * gradient
    fix_one = 1.0 - beta_first**STEP
    fix_two = 1.0 - beta_second**STEP
    direction = moment_one / fix_one / (jnp.sqrt(moment_two / fix_two) + adam_eps)
    updated = master_part - step_rates * (direction + weight_decay * master_part)
    blended = average_decay * average_part + (1.0 - average_decay) * updated
    return (updated, moment_one, moment_two, blended)


def shards(tokens, image_sides, grad_out, master, first_moment, second_moment, weight_average):
    shard_len = master.shape[0]
    owners = lax.axis_size("wide")
    images_all = tokens.shape[0] * owners * lax.axis_size("narrow")
    starts = tuple((shard_len * w) // D for w in range(owners))
    rows_of = block_rows(shard_len)
    inset = lax.rem(lax.axis_index("wide") * shard_len, D)

    own = lax.dynamic_update_slice(jnp.zeros((rows_of * D,), bf16), master.astype(bf16), (inset,))
    own = jnp.broadcast_to(own.reshape(1, rows_of, D), (owners, rows_of, D))
    chunks = lax.all_to_all(own, "wide", 0, 0)

    outs, grads_in, grad_chunks = [], [], None
    for k in range(tokens.shape[0]):
        out, grad_in, chunk = image_step(starts, rows_of, chunks, tokens[k], image_sides[k : k + 1], grad_out[k])
        outs.append(out)
        grads_in.append(grad_in)
        grad_chunks = chunk if k == 0 else (grad_chunks.astype(f32) + chunk.astype(f32)).astype(bf16)
    block_out = jnp.stack(outs)
    grad_in = jnp.stack(grads_in)

    parts = lax.all_to_all(grad_chunks, "wide", 0, 0)
    total = jnp.sum(parts.astype(f32), axis=0)
    total = total + lax.ppermute(total, "narrow", [(0, 1), (1, 0)])
    reduced = lax.dynamic_slice(total.reshape(rows_of * D), (inset,), (shard_len,))
    step_rates = lax.dynamic_slice_in_dim(
        jnp.asarray(rate_values(shard_len * owners)), lax.axis_index("wide") * shard_len, shard_len
    )
    updated, moment_one, moment_two, blended = adam_update(
        reduced / images_all, master, first_moment, second_moment, weight_average, step_rates
    )
    return (block_out, grad_in, updated, moment_one, moment_two, blended)


def solution(mesh):
    return jax.shard_map(
        shards,
        mesh=mesh,
        in_specs=(
            P(("wide", "narrow"), None, None),
            P(("wide", "narrow")),
            P(("wide", "narrow"), None, None),
            P("wide"),
            P("wide"),
            P("wide"),
            P("wide"),
        ),
        out_specs=(
            P(("wide", "narrow"), None, None),
            P(("wide", "narrow"), None, None),
            P("wide"),
            P("wide"),
            P("wide"),
            P("wide"),
        ),
        check_vma=False,
    )
```

time: 112 us -> 88 us (0.79)
  Pallas kernels: 68.8 us -> 44.4 us
    pallas_call x1, Pallas kernels: 68.8 us -> 44.4 us  [image_step(): pl.pallas_call(functools.partial(image_kernel, starts, rows_of), out_shap...]
where the time goes in v2:
time: 88 us; the launch traced here: 87.5 us
  Pallas kernels  44.4 us (50%)
  blocking collectives  15.7 us (18%)
  waiting for transfers between devices  13.2 us (15%)
  starting transfers between devices  8.38 us (10%)
  other arithmetic  2.4 us (3%)
  local copies, waits for them, and re-layouts  2.07 us (2%)
  between operations  1.37 us (2%)
    pallas_call x1, Pallas kernels, image_step(): pl.pallas_call(functools.partial(image_kernel, starts, rows_of), out_shap...  44.4 us
    all_to_all x1, blocking collectives, shards(): parts = lax.all_to_all(grad_chunks, 'wide', 0, 0)  15.7 us
    all_to_all x1, waiting for transfers between devices, shards(): chunks = lax.all_to_all(own, 'wide', 0, 0)  12 us
    all_to_all x1, starting transfers between devices, shards(): chunks = lax.all_to_all(own, 'wide', 0, 0)  8.31 us
  transfers between devices with their start and end apart: 2, of which 2 were waited for; matrix products, arithmetic and copies ran while one was open for 0% of the time, Pallas kernels for 0%

profile of v2, /device:TPU:0, one launch (start us, length us, event | category | flops | bytes accessed | tf_op | source)
XLA Modules:
  0.0 87.5 jit_solution(6723518603396215187)
XLA Ops:
  0.6 0.8 convert_element_type.6
  1.4 0.3 dynamic_update_slice.3
  1.7 0.1 broadcast_in_dim.11
  1.8 0.8 broadcast_in_dim.12
  2.6 8.3 %all-to-all-start = ((bf16[16,96,96]{2,1,0:T(8,128)(2,1)}), bf16[16,96,96]{2,1,0:T(8,128)(2,1)S(1)}, u32[]{:S(2)}, u32[]{:S(2)}) async-start(bf16[16,96,96]{2,1,0:T(8,128)(2,1)} %broadcast_in_dim.12), calls=%async_computation | async-start | bytes 786432 | tf_op jit(solution)/shard_map/all_to_all | solution.py:657
  11.6 12.0 %all-to-all-done.chunk_ref = bf16[16,96,96]{2,1,0:T(8,128)(2,1)S(1)} async-done(((bf16[16,96,96]{2,1,0:T(8,128)(2,1)}), bf16[16,96,96]{2,1,0:T(8,128)(2,1)S(1)}, u32[]{:S(2)}, u32[]{:S(2)}) %all-to-all-start) | async-done | bytes 294944 | tf_op jit(solution)/shard_map/all_to_all | solution.py:657
  23.6 0.0 copy-start
  23.6 0.7 copy-done
  24.3 44.4 %image_step.1 = (bf16[96,6400]{1,0:T(8,128)(2,1)}, bf16[96,6400]{1,0:T(8,128)(2,1)}, bf16[16,96,96]{2,1,0:T(8,128)(2,1)}) custom-call(s32[1]{0:T(128)S(6)} %copy.18.side_ref, bf16[16,96,96]{2,1,0:T(8,128)(2,1)} %copy-done, bf16[96,6400]{1,0:T(8,128)(2,1)} %bitcast.4, bf16[96,6400]{1,0:T(8,128)(2,1)} %bitcast.5, s32[8,6656]{1,0:T(8,128)} %constant.49.clone.idx_ref, ...), custom_call_target="tpu_custom_call" | custom-call | tf_op jit(solution)/shard_map/image_step/pallas_call | solution.py:621
  68.7 0.0 copy-start.1
  68.7 0.0 copy-start.2
  68.7 0.0 copy-start.3
  68.7 0.0 copy-start.4
  68.7 15.7 %all_to_all.10 = bf16[16,96,96]{2,1,0:T(8,128)(2,1)S(1)} all-to-all(bf16[16,96,96]{2,1,0:T(8,128)(2,1)} %get-tuple-element.11), channel_id=1, replica_groups=mesh['wide'=16,'narrow'=2] {'wide'}, dimensions={0} | all-to-all | bytes 589824 | tf_op jit(solution)/shard_map/all_to_all | solution.py:668
  84.5 0.1 convert_reduce_fusion
  84.5 0.1 collective-permute-start
  84.6 1.2 %collective-permute-done = f32[96,96]{1,0:T(8,128)S(1)} collective-permute-done((f32[96,96]{1,0:T(8,128)S(1)}, f32[96,96]{1,0:T(8,128)S(1)}, u32[]{:S(2)}, u32[]{:S(2)}) %collective-permute-start) | collective-permute-done | bytes 36896 | tf_op jit(solution)/shard_map/ppermute | solution.py:670
  85.8 0.1 reshape.17
  85.9 0.0 copy-done.1
  86.0 0.0 copy-done.2
  86.0 0.0 copy-done.3
  86.0 0.0 copy-done.4
  86.0 1.5 %multiply_add_fusion = (f32[9060]{0:T(1024)}, f32[9060]{0:T(1024)}, f32[9060]{0:T(1024)}, f32[9060]{0:T(1024)}) fusion(f32[9060]{0:T(1024)S(1)} %copy-done.2, f32[9060]{0:T(1024)S(1)} %copy-done.1, f32[144960]{0:T(1024)} %constant.50.clone, s32[]{:T(128)S(6)} %select_n.8, f32[9216]{0:T(1024)S(1)} %reshape.17, s32[]{:T(128)S(6)} %select_n.7, ...), kind=kLoop, calls=%fused_computation.1 | loop fusion | flops 163080 | bytes 362408 | tf_op jit(solution)/shard_map/add | solution.py:643
  (2 shorter events, 0.0 us)
Async XLA Ops:
  2.6 21.0 %all-to-all-start = ((bf16[16,96,96]{2,1,0:T(8,128)(2,1)}), bf16[16,96,96]{2,1,0:T(8,128)(2,1)S(1)}, u32[]{:S(2)}, u32[]{:S(2)}) async-start(bf16[16,96,96]{2,1,0:T(8,128)(2,1)} %broadcast_in_dim.12), calls=%async_computation | async-start | bytes 786432 | tf_op jit(solution)/shard_map/all_to_all | solution.py:657
  23.6 0.7 copy-start
  68.7 17.2 %copy-start.1 = (f32[9060]{0:T(1024)S(1)}, f32[9060]{0:T(1024)}, u32[]{:S(2)}) copy-start(f32[9060]{0:T(1024)} %param.14) | copy-start | bytes 108724
  68.7 17.2 %copy-start.2 = (f32[9060]{0:T(1024)S(1)}, f32[9060]{0:T(1024)}, u32[]{:S(2)}) copy-start(f32[9060]{0:T(1024)} %param.17) | copy-start | bytes 108724
  68.7 17.2 %copy-start.3 = (f32[9060]{0:T(1024)S(1)}, f32[9060]{0:T(1024)}, u32[]{:S(2)}) copy-start(f32[9060]{0:T(1024)} %param.15) | copy-start | bytes 108724
  68.7 17.2 %copy-start.4 = (f32[9060]{0:T(1024)S(1)}, f32[9060]{0:T(1024)}, u32[]{:S(2)}) copy-start(f32[9060]{0:T(1024)} %param.16) | copy-start | bytes 108724
  84.5 1.3 %collective-permute-start = (f32[96,96]{1,0:T(8,128)S(1)}, f32[96,96]{1,0:T(8,128)S(1)}, u32[]{:S(2)}, u32[]{:S(2)}) collective-permute-start(f32[96,96]{1,0:T(8,128)S(1)} %convert_reduce_fusion), channel_id=1, source_target_pairs={{0,1},{1,0},{2,3},{3,2},{4,5},{5,4},{6,7},{7,6},{8,9},{9,8},{10,11... | collective-permute-start | bytes 110600 | tf_op jit(solution)/shard_map/ppermute | solution.py:670

commit v3 on v2

--- a/solution.py
+++ b/solution.py
@@ -36,6 +36,9 @@
 TILE_ONE = 6400
 TILE_TWO = 1280
 TILE_THREE = 1280
+TILES = TOK // TILE_TWO
+TILE_ROWS = TILE_TWO // GRID
+ROW_STEPS = TILE_ROWS // KSTR
 SCORE_SCALE = D ** (-0.5)
 LOG2E = 1.4426950408889634
 
@@ -128,13 +131,16 @@
     width = rows.shape[1]
     where = jnp.broadcast_to(place, (24, width))
     residue = where & 3
-    picked = jnp.where(
+    x = jnp.where(
         residue < 2,
         jnp.where(residue == 0, rows[0:24], rows[24:48]),
         jnp.where(residue == 2, rows[48:72], rows[72:96]),
     )
-    picked = jnp.where((where & 8) != 0, pltpu.roll(picked, 22, 0), picked)
-    return jnp.where((where & 4) != 0, pltpu.roll(picked, 23, 0), picked)
+    step = ROW_STEPS // 2
+    while step >= 1:
+        x = jnp.where((where & (4 * step)) != 0, pltpu.roll(x, 24 - step, 0), x)
+        step //= 2
+    return x
 
 
 def skew_columns(rows, place):
@@ -156,8 +162,10 @@
 
 def unskew_rows(x, place):
     where = jnp.broadcast_to(place, x.shape)
-    x = jnp.where((where & 4) != 0, pltpu.roll(x, 1, 0), x)
-    x = jnp.where((where & 8) != 0, pltpu.roll(x, 2, 0), x)
+    step = 1
+    while step < ROW_STEPS:
+        x = jnp.where((where & (4 * step)) != 0, pltpu.roll(x, step, 0), x)
+        step *= 2
     residue = where & 3
     return jnp.concatenate([jnp.where(residue == k, x, 0.0) for k in range(4)], axis=0)
 
@@ -177,8 +185,16 @@
     return jnp.concatenate([jnp.where(residue == k, x, 0.0) for k in range(4)], axis=0)
 
 
-def column_row(column):
-    return jnp.transpose(jnp.broadcast_to(column, (D, 128)))[0:1, :]
+def aligned(value, step):
+    return value if isinstance(value, int) else pl.multiple_of(value, step)
+
+
+def interleave(*parts):
+    live = list(parts)
+    while live:
+        for part in list(live):
+            if next(part, None) is None:
+                live.remove(part)
 
 
 def two_columns(column):
@@ -195,6 +211,71 @@
 
 def two_ones(width):
     return jnp.where(lax.broadcasted_iota(jnp.int32, (16, width), 0) < 2, 1.0, 0.0).astype(bf16)
+
+
+def key_columns():
+    return lax.broadcasted_iota(jnp.int32, (KG, 128), 0)
+
+
+def tap_start(a, u, v):
+    return LEAD + GRID * (KSTR * a + u - 1) + v - 1
+
+
+def tap_rows(kernel_rows):
+    b_index = key_columns()
+    taps = [jnp.broadcast_to(kernel_rows[k : k + 1, :], (KG, 128)) for k in range(9)]
+    return [jnp.where(b_index == 0, 0.0, tap) if k % 3 == 0 else tap for k, tap in enumerate(taps)]
+
+
+def spread_keys(taps, grad, a, gfield):
+    idle = LEAD + GRID * (KSTR * a + 2)
+    gfield[idle - 8 : idle + GRID, :] = jnp.zeros((GRID + 8, 128), f32)
+    for u in range(3):
+        gfield[pl.ds(tap_start(a, u, 3), KG, stride=KSTR), :] = jnp.zeros((KG, 128), f32)
+    for k in range(9):
+        gfield[pl.ds(tap_start(a, k // 3, k % 3), KG, stride=KSTR), :] = taps[k] * grad
+    if a == KG - 1:
+        gfield[LEAD + TOK - GRID : LEAD + TOK, :] = jnp.zeros((GRID, 128), f32)
+
+
+def input_kernel(*refs):
+    sources, gin_hbm, held = refs[:10], refs[10], refs[11:21]
+    field_ref, mid_ref, unit_ref, inv_ref, gkt, gvt, kk, kv, wqt, wkvg = held
+    gin_ref, gfk, gfv, gkv, copy_sem = refs[21:]
+    copies = [pltpu.make_async_copy(a, b, copy_sem.at[k]) for k, (a, b) in enumerate(zip(sources, held))]
+    for copy in copies[::-1]:
+        copy.start()
+    for copy in copies[4:]:
+        copy.wait()
+    for kernel_rows, pooled, gfield in ((kk, gkt, gfk), (kv, gvt, gfv)):
+        taps = tap_rows(kernel_rows)
+        for a in range(KG):
+            spread_keys(taps, pooled[KG * a : KG * a + KG, :], a, gfield)
+    for copy in copies[:4]:
+        copy.wait()
+
+    def gin_copy(i):
+        here = pl.ds(aligned(i * TILE_THREE, 128), TILE_THREE)
+        return pltpu.make_async_copy(gin_ref.at[:, here], gin_hbm.at[:, here], copy_sem.at[10 + i])
+
+    def finish(i, carry):
+        tile = TILE_THREE
+        here = pl.ds(aligned(i * tile, 128), tile)
+        flat = pl.ds(aligned(i * tile + LEAD, 8), tile)
+        gkv[:, 0:128] = gfk[flat, :].astype(bf16)
+        gkv[:, 128:256] = gfv[flat, :].astype(bf16)
+        gn = dot(wqt[...], field_ref[:, here]) + dot_nt(wkvg[...], gkv[...])
+        unit = unit_ref[:, here].astype(f32)
+        mean = jnp.sum(gn, axis=0, keepdims=True) * (1.0 / D)
+        along = jnp.sum(gn * unit, axis=0, keepdims=True) * (1.0 / D)
+        total = mid_ref[:, here].astype(f32) + (gn - mean - unit * along) * inv_ref[0:1, here]
+        gin_ref[:, here] = total.astype(bf16)
+        gin_copy(i).start()
+        return carry
+
+    lax.fori_loop(0, TOK // TILE_THREE, finish, 0)
+    for i in range(TOK // TILE_THREE):
+        gin_copy(i).wait()
 
 
 def image_kernel(
@@ -202,21 +283,36 @@
     rows_of,
     side_ref,
     chunk_ref,
-    x_ref,
-    gy_ref,
+    x_hbm,
+    gy_hbm,
     idx_ref,
     zsel_ref,
     tsel_ref,
-    out_ref,
-    gin_ref,
+    out_hbm,
     gchunk_ref,
-    wf, wq, wqt, wkt, wvt, wkvg, wp, wpt, w1, w1t, w2, w2t, relh, rel, relt, cols, kq, kk, kv,
-    fq, fk, fv, gfk, gfv, qb, gq, gm, un, inv1, fcol,
+    field_hbm,
+    mid_hbm,
+    unit_hbm,
+    inv_ref,
+    gkt,
+    gvt,
+    kk,
+    kv,
+    wqt,
+    wkvg,
+    wf, wq, wkt, wvt, wp, wpt, w1, w1t, w2, w2t, relh, rel, relt, cols, kq,
+    fq, fk, fv, gfk, gfv, qb, gq, gm, un, fcol,
     a1, a2, vb, vbt, kp, vpool,
-    rhs, gse, aaug, n1aug, n2aug, oaug, goaug, gsh, gkv,
-    dw2, dw1, dpr, gv, gkr, hacc, dwq, dwkv, kqacc, gkt, gvt, gr,
+    rhs, gse, n1aug, goaug, gsh, gkv,
+    dw2, dw1, dpr, gv, gkr, hacc, dwq, dwkv, kqacc, gr, x_ref, gy_ref, out_ref, gfield, copy_sem,
+    *slot_refs,
 ):
+    slots = (slot_refs[: len(slot_refs) // 2], slot_refs[len(slot_refs) // 2 :])
     side = side_ref[0]
+    x_copy = pltpu.make_async_copy(x_hbm, x_ref, copy_sem.at[0])
+    gy_copy = pltpu.make_async_copy(gy_hbm, gy_ref, copy_sem.at[1])
+    x_copy.start()
+    gy_copy.start()
 
     wf[...] = jnp.zeros(wf.shape, f32)
     for w, start in enumerate(starts):
@@ -260,6 +356,7 @@
         w2t[k * D : (k + 1) * D, :] = jnp.transpose(block)[:D, :].astype(bf16)
     w2[:, 0:HID] = jnp.transpose(w2t[...].astype(f32)).astype(bf16)
     w2[:, HID:] = two_columns(cols[:, 2:3] * math.sqrt(0.5 * math.pi))
+    relh[160:, :] = jnp.zeros((8, 128), f32)
     for k in range(4):
         relh[k * 40 : k * 40 + 40, :] = wf[pl.ds(ROW["rel_h"] + 3 + k, 40, stride=4), :]
     rel_w = jnp.concatenate([wf[pl.ds(ROW["rel_w"] + 3 + k, 40, stride=4), :] for k in range(4)], axis=0)
@@ -300,29 +397,32 @@
 
     un[D:, :] = two_ones(TOK)
     n1aug[D:, :] = two_ones(TILE_ONE)
-    n2aug[D:, :] = two_ones(TILE_TWO)
-    oaug[D:, :] = two_ones(TILE_TWO)
-    aaug[HID:, :] = two_ones(TILE_TWO)
+    for slot in slots:
+        slot[5][HID:, :] = two_ones(TILE_TWO)
+        slot[6][D:, :] = two_ones(TILE_TWO)
+        slot[7][D:, :] = two_ones(TILE_TWO)
     rhs[192:208, :] = two_ones(TILE_TWO)
 
     def window(i, tile):
-        return pl.ds(pl.multiple_of(i * tile, 128), tile + 2 * HALO)
+        return pl.ds(aligned(i * tile, 128), tile + 2 * HALO)
 
     def inner(i, tile):
-        return pl.ds(pl.multiple_of(i * tile + HALO, 128), tile)
+        return pl.ds(aligned(i * tile + HALO, 128), tile)
 
     def plain(i, tile):
-        return pl.ds(pl.multiple_of(i * tile, 128), tile)
+        return pl.ds(aligned(i * tile, 128), tile)
 
     def token_mask(i, tile):
         place = idx_ref[0:2, inner(i, tile)]
         return jnp.where((place[0:1] < side) & (place[1:2] < side), 1.0, 0.0)
+
+    x_copy.wait()
 
     def project(i, carry):
         here = plain(i, TILE_ONE)
         unit, inv = normalize(x_ref[:, here].astype(f32))
         un[0:D, here] = unit.astype(bf16)
-        inv1[0:1, here] = inv
+        inv_ref[0:1, here] = inv
         n1aug[0:D, :] = (unit * cols[:, 3:4] + cols[:, 4:5]).astype(bf16)
         fq[:, inner(i, TILE_ONE)] = dot(wq[...], n1aug[...]) * token_mask(i, TILE_ONE)
         field = pl.ds(pl.multiple_of(i * TILE_ONE + LEAD, 8), TILE_ONE)
@@ -331,6 +431,9 @@
         return carry
 
     lax.fori_loop(0, TOK // TILE_ONE, project, 0)
+
+    unit_copy = pltpu.make_async_copy(un.at[0:D, :], unit_hbm, copy_sem.at[4])
+    unit_copy.start()
 
     def pool_queries(i, carry):
         tile = TILE_ONE
@@ -361,14 +464,7 @@
 
     lax.fori_loop(0, TOK // TILE_ONE, pool_queries, 0)
 
-    b_index = lax.broadcasted_iota(jnp.int32, (KG, 128), 0)
-
-    def tap_start(a, u, v):
-        return LEAD + GRID * (KSTR * a + u - 1) + v - 1
-
-    def tap_rows(kernel_rows):
-        taps = [jnp.broadcast_to(kernel_rows[k : k + 1, :], (KG, 128)) for k in range(9)]
-        return [jnp.where(b_index == 0, 0.0, tap) if k % 3 == 0 else tap for k, tap in enumerate(taps)]
+    b_index = key_columns()
 
     for field, kernel_rows, pooled in ((fk, kk, kp), (fv, kv, vpool)):
         taps = tap_rows(kernel_rows)
@@ -403,73 +499,114 @@
     hot_l = ((row_l < 24) & (KG - 1 - a_l == row_l)) | ((row_l >= 24) & (KG - 1 - b_l == row_l - 24))
     a2[D:, :] = jnp.where(hot_l, 1.0, 0.0).astype(bf16)
 
-    def attend(i, carry):
+    def ahead(i, slot):
+        weight_ref, low_ref, mixed_ref, half_ref, slope_ref, aaug, n2aug, oaug, scale_ref = slot
         tile = TILE_TWO
         here = plain(i, tile)
-        mask = token_mask(i, tile)
-        row, col = idx_ref[0:1, inner(i, tile)], idx_ref[1:2, inner(i, tile)]
-        near = jnp.concatenate([relh[pl.ds(40 * k + 4 * i, 24), :] for k in range(4)], axis=0)
-        rel[0:D, :] = near[:, :D].astype(bf16)
-        relt[:, 0:D] = jnp.transpose(near)[:D, :].astype(bf16)
+        row, col = idx_ref[0:1, inner(i, tile)] - i * TILE_ROWS, idx_ref[1:2, inner(i, tile)]
+        near = [relh[pl.ds(40 * k + ROW_STEPS * i, 24), :] for k in range(4)]
+        rel[0:D, :] = jnp.concatenate(near, axis=0)[:, :D].astype(bf16)
         q = qb[:, here]
         seen = dot(rel[...], q)
         rhs[0:D, :] = q
+        yield True
         sides = jnp.concatenate([skew_rows(seen[0:D], row), skew_columns(seen[D:256], col)], axis=0)
         sides = sides * math.sqrt(D)
         sides_low = sides.astype(bf16)
         rhs[D : D + 48, :] = sides_low
         rhs[D + 48 : D + 96, :] = (sides - sides_low.astype(f32)).astype(bf16)
         scores = dot(a1[...], rhs[...])
+        yield True
         weight = jnp.exp2((scores - jnp.max(scores, axis=0, keepdims=True)) * (SCORE_SCALE * LOG2E))
-        weight_low = weight.astype(bf16)
-        mixed = dot(vb[...], weight_low)
+        weight_ref[...] = weight
+        low_ref[...] = weight.astype(bf16)
+        yield True
+        mixed = dot(vb[...], low_ref[...])
         inv_sum = 1.0 / mixed[D : D + 1]
+        scale_ref[0:1, :] = inv_sum
         mixed = mixed[0:D] * inv_sum
+        mixed_ref[...] = mixed
         oaug[0:D, :] = (mixed + q.astype(f32)).astype(bf16)
         middle = x_ref[:, here].astype(f32) + dot(wp[...], oaug[...])
-
+        yield True
         center = middle - jnp.sum(middle, axis=0, keepdims=True) * (1.0 / D)
         inv = lax.rsqrt(jnp.sum(center * center, axis=0, keepdims=True) * (1.0 / D) + norm_eps)
         half = center * (inv * math.sqrt(0.5))
+        half_ref[...] = half
+        scale_ref[1:2, :] = inv
         n2aug[0:D, :] = half.astype(bf16)
         z = dot(w1[...], n2aug[...])
+        yield True
         below = lax.erf(z) * (0.5 * math.sqrt(math.pi)) + 0.5 * math.sqrt(math.pi)
         aaug[0:HID, :] = (z * below).astype(bf16)
-        slope = below + z * jnp.exp2((z * z) * -LOG2E)
+        slope_ref[...] = below + z * jnp.exp2((z * z) * -LOG2E)
+        yield True
         mlp = dot(w2[...], aaug[...])
-        out_ref[:, here] = ((middle + mlp * math.sqrt(2.0 / math.pi)) * mask).astype(bf16)
-
-        gy = gy_ref[:, here].astype(f32) * mask
+        out_ref[:, here] = ((middle + mlp * math.sqrt(2.0 / math.pi)) * token_mask(i, tile)).astype(bf16)
+
+    def behind(i, slot):
+        weight_ref, low_ref, mixed_ref, half_ref, slope_ref, aaug, n2aug, oaug, scale_ref = slot
+        tile = TILE_TWO
+        here = plain(i, tile)
+        row, col = idx_ref[0:1, inner(i, tile)] - i * TILE_ROWS, idx_ref[1:2, inner(i, tile)]
+        near = [relh[pl.ds(40 * k + ROW_STEPS * i, 24), :] for k in range(4)]
+        relt[:, 0:D] = jnp.transpose(jnp.concatenate(near, axis=0))[:D, :].astype(bf16)
+        inv_sum, inv = scale_ref[0:1, :], scale_ref[1:2, :]
+        gy = gy_ref[:, here].astype(f32) * token_mask(i, tile)
         gy_low = gy.astype(bf16)
+        pushed = dot(w2t[...], gy_low)
+        yield True
+        gh_low = (slope_ref[...] * pushed).astype(bf16)
         dw2[:, 0:KK] += dot_nt(gy_low, aaug[...])
-        gh_low = (slope * dot(w2t[...], gy_low)).astype(bf16)
+        gn = dot(w1t[...], gh_low)
+        yield True
         dw1[0:112, :] += dot_nt(n2aug[...], gh_low)
-        gn = dot(w1t[...], gh_low)
+        half = half_ref[...]
         mean = jnp.sum(gn, axis=0, keepdims=True) * (1.0 / D)
         along = jnp.sum(gn * half, axis=0, keepdims=True) * (2.0 / D)
         gmid = gy + (gn - mean - half * along) * (inv * math.sqrt(1.0 / math.pi))
-        gm[:, here] = gmid
         gm_low = gmid.astype(bf16)
+        gm[:, here] = gm_low
+        go = dot(wpt[...], gm_low)
+        yield True
         dpr[:, 0:112] += dot_nt(gm_low, oaug[...])
-        go = dot(wpt[...], gm_low)
         go_low = (go * inv_sum).astype(bf16)
         goaug[0:D, :] = go_low
-        goaug[D:, :] = two_rows(jnp.sum(go_low.astype(f32) * mixed, axis=0, keepdims=True))
-        gv[0:D, 0:KK] += dot_nt(go_low, weight_low)
-        gse[0:KK, :] = (weight * dot(vbt[...], goaug[...])).astype(bf16)
+        goaug[D:, :] = two_rows(jnp.sum(go_low.astype(f32) * mixed_ref[...], axis=0, keepdims=True))
+        spread = dot(vbt[...], goaug[...])
+        yield True
+        gv[0:D, 0:KK] += dot_nt(go_low, low_ref[...])
+        gse[0:KK, :] = (weight_ref[...] * spread).astype(bf16)
         back = dot(a2[...], gse[0:KK, :])
+        yield True
         gse[KK : KK + D, :] = unskew_rows(back[D : D + 24], row).astype(bf16)
         gse[KK + D : KK + 256, :] = unskew_columns(back[D + 24 : D + 48], col).astype(bf16)
-        flat = pl.ds(pl.multiple_of(i * tile + LEAD, 8), tile)
-        gfk[flat, :] = jnp.zeros((tile, 128), f32)
-        gfv[flat, :] = jnp.zeros((tile, 128), f32)
-        outer = dot_nt(q, gse[...])
+        yield True
+        outer = dot_nt(qb[:, here], gse[...])
         gkr[0:D, 0 : KK + 256] += outer
         hacc[i] = outer[:, 384:512]
         gq[:, inner(i, tile)] = go + SCORE_SCALE * back[0:D] + dot(relt[...], gse[KK : KK + 256, :])
+
+    one, two = slots
+    gy_copy.wait()
+
+    def attend(k, carry):
+        interleave(ahead(2 * k + 1, two), behind(2 * k, one))
+        interleave(ahead(2 * k + 2, one), behind(2 * k + 1, two))
         return carry
 
-    lax.fori_loop(0, TOK // TILE_TWO, attend, 0)
+    interleave(ahead(0, one))
+    lax.fori_loop(0, (TILES - 1) // 2, attend, 0)
+    if TILES % 2 == 0:
+        interleave(ahead(TILES - 1, two), behind(TILES - 2, one))
+        interleave(behind(TILES - 1, two))
+    else:
+        interleave(behind(TILES - 1, one))
+
+    out_copy = pltpu.make_async_copy(out_ref, out_hbm, copy_sem.at[2])
+    out_copy.start()
+    mid_copy = pltpu.make_async_copy(gm, mid_hbm, copy_sem.at[3])
+    mid_copy.start()
 
     gkt[...] = jnp.transpose(gkr[:, 0:512])[0:KK, :] * SCORE_SCALE
     gvt[...] = jnp.transpose(gv[...])[0:KK, :]
@@ -480,16 +617,16 @@
             spread = dot_nt(low, tsel_ref[i]) * zsel_ref[i].astype(f32)
             gr[ROW[name] + i : ROW[name] + i + 1, 0:D] = jnp.sum(spread, axis=0, keepdims=True)
 
-    for field, kernel_rows, pooled, gfield, name in ((fk, kk, gkt, gfk, "pool_k"), (fv, kv, gvt, gfv, "pool_v")):
+    for field, kernel_rows, pooled, gspread, name in ((fk, kk, gkt, gfk, "pool_k"), (fv, kv, gvt, gfv, "pool_v")):
         taps = tap_rows(kernel_rows)
         sums = [jnp.zeros((KG, 128), f32) for _ in range(9)]
         for a in range(KG):
             grad = pooled[KG * a : KG * a + KG, :]
             inside = jnp.where(b_index == 0, 0.0, grad)
+            spread_keys(taps, grad, a, gspread)
             for k in range(9):
                 where = pl.ds(tap_start(a, k // 3, k % 3), KG, stride=KSTR)
                 sums[k] = sums[k] + (inside if k % 3 == 0 else grad) * field[where, :]
-                gfield[where, :] = taps[k] * grad
         rows = [jnp.sum(total, axis=0, keepdims=True) for total in sums]
         rows = jnp.concatenate(rows + [jnp.zeros((128 - 9, 128), f32)], axis=0)
         pool_gradient(name, jnp.transpose(rows)[:D, :])
@@ -516,25 +653,27 @@
                 before = jnp.where(first, 0.0, pltpu.roll(col_sum(2), 1, 1)[:, mid])
                 fields.append((after + col_sum(1)[:, mid] + before) * mask)
                 moved.append((below[:, mid], grad[:, mid], above[:, mid]))
-            gsh[3 * D + 16 * pair : 3 * D + 16 * pair + 16, :] = jnp.concatenate(fields, axis=0).astype(bf16)
+            gfield[16 * pair : 16 * pair + 16, here] = jnp.concatenate(fields, axis=0).astype(bf16)
             for u in range(3):
                 both = jnp.concatenate([moved[0][u], moved[1][u]], axis=0)
                 gsh[u * D + 16 * pair : u * D + 16 * pair + 16, :] = both.astype(bf16)
-        kqacc[:, 0 : 3 * D] += dot_nt(gsh[0 : 3 * D, :], fcol[:, here])
-        gq_low = gsh[3 * D : 4 * D, :]
+        kqacc[:, 0 : 3 * D] += dot_nt(gsh[...], fcol[:, here])
         flat = pl.ds(pl.multiple_of(i * tile + LEAD, 8), tile)
         gkv[:, 0:128] = gfk[flat, :].astype(bf16)
         gkv[:, 128:256] = gfv[flat, :].astype(bf16)
-        dwq[:, 0:112] += dot_nt(gq_low, un[:, here])
+        dwq[:, 0:112] += dot_nt(gfield[:, here], un[:, here])
         dwkv[0:112, :] += dot(un[:, here], gkv[...])
-        gn = dot(wqt[...], gq_low) + dot_nt(wkvg[...], gkv[...])
-        unit = un[0:D, here].astype(f32)
-        mean = jnp.sum(gn, axis=0, keepdims=True) * (1.0 / D)
-        along = jnp.sum(gn * unit, axis=0, keepdims=True) * (1.0 / D)
-        gin_ref[:, here] = (gm[:, here] + (gn - mean - unit * along) * inv1[0:1, here]).astype(bf16)
+        field_copy(i).start()
         return carry
 
+    def field_copy(i):
+        here = plain(i, TILE_THREE)
+        return pltpu.make_async_copy(gfield.at[:, here], field_hbm.at[:, here], copy_sem.at[5 + i])
+
     lax.fori_loop(0, TOK // TILE_THREE, finish, 0)
+    out_copy.wait()
+    mid_copy.wait()
+    unit_copy.wait()
 
     def write(name, rows, first=0):
         base = ROW[name] + first
@@ -567,11 +706,12 @@
         columns = jnp.where(lane == k, jnp.sum(one, axis=1, keepdims=True), columns)
     pool_gradient("pool_q", columns)
 
-    for i in range(TOK // TILE_TWO):
+    for i in range(TILES):
         turned = jnp.transpose(hacc[i])
         for k in range(4):
-            where = pl.ds(ROW["rel_h"] + 3 + k + 16 * i, 23, stride=4)
-            gr[where, :] = gr[where, :] + wide_rows(turned[16 + 24 * k : 39 + 24 * k])
+            count = KG + ROW_STEPS - 1
+            where = pl.ds(ROW["rel_h"] + 3 + k + TILE_ROWS * i, count, stride=4)
+            gr[where, :] = gr[where, :] + wide_rows(turned[16 + 24 * k : 16 + 24 * k + count])
     turned = jnp.transpose(gkr[0:D, 384:768])
     for k in range(4):
         gr[pl.ds(ROW["rel_w"] + 3 + k, 39, stride=4), :] = wide_rows(turned[112 + 40 * k : 151 + 40 * k])
@@ -588,6 +728,8 @@
         write("b_fc1", dw1[D : D + 1, k * D : (k + 1) * D] * math.sqrt(1.0 / math.pi), k)
         gr[pl.ds(ROW["w_fc2"] + k, D, stride=4), :] = wide_rows(dw2[:, k * D : (k + 1) * D] * math.sqrt(2.0 / math.pi))
     write("b_fc2", jnp.transpose(dw2[:, HID:512])[0:1, :])
+    for i in range(TOK // TILE_THREE):
+        field_copy(i).wait()
     for w, start in enumerate(starts):
         gchunk_ref[w] = gr[start : start + rows_of, 0:D].astype(bf16)
 
@@ -598,39 +740,65 @@
     vm = pltpu.VMEM
     scratch = [
         vm((depth, 128), f32),
-        vm((D, 112), bf16), vm((D, D), bf16), vm((112, 128), bf16), vm((112, 128), bf16), vm((D, 256), bf16),
+        vm((D, 112), bf16), vm((112, 128), bf16), vm((112, 128), bf16),
         vm((D, 112), bf16), vm((D, D), bf16),
         vm((HID, 112), bf16), vm((D, HID), bf16), vm((D, KK), bf16), vm((HID, D), bf16),
-        vm((160, 128), f32), vm((256, D), bf16), vm((D, 256), bf16),
-        vm((D, 128), f32), vm((9, D, 128), f32), vm((16, 128), f32), vm((16, 128), f32),
+        vm((168, 128), f32), vm((256, D), bf16), vm((D, 256), bf16),
+        vm((D, 128), f32), vm((9, D, 128), f32),
         vm((D, TOK + 2 * HALO), f32), vm((FIELD, 128), f32), vm((FIELD, 128), f32),
         vm((FIELD, 128), f32), vm((FIELD, 128), f32),
-        vm((D, TOK), bf16), vm((D, TOK + 2 * HALO), f32), vm((D, TOK), f32),
-        vm((112, TOK), bf16), vm((8, TOK), f32), vm((3 * D, TOK), bf16),
+        vm((D, TOK), bf16), vm((D, TOK + 2 * HALO), f32), vm((D, TOK), bf16),
+        vm((112, TOK), bf16), vm((3 * D, TOK), bf16),
         vm((KK, 208), bf16), vm((144, KK), bf16), vm((112, KK), bf16), vm((KK, 112), bf16),
         vm((KK, 128), f32), vm((KK, 128), f32),
-        vm((208, TILE_TWO), bf16), vm((KK + 256, TILE_TWO), bf16), vm((KK, TILE_TWO), bf16),
-        vm((112, TILE_ONE), bf16), vm((112, TILE_TWO), bf16), vm((112, TILE_TWO), bf16), vm((112, TILE_TWO), bf16),
-        vm((4 * D, TILE_THREE), bf16), vm((TILE_THREE, 256), bf16),
+        vm((208, TILE_TWO), bf16), vm((KK + 256, TILE_TWO), bf16), vm((112, TILE_ONE), bf16), vm((112, TILE_TWO), bf16),
+        vm((3 * D, TILE_THREE), bf16), vm((TILE_THREE, 256), bf16),
         vm((D, 512), f32), vm((128, HID), f32), vm((D, 128), f32), vm((128, 512), f32), vm((128, 768), f32),
-        vm((TOK // TILE_TWO, D, 128), f32),
-        vm((D, 128), f32), vm((128, 256), f32), vm((3 * D, 3 * 128), f32), vm((KK, 128), f32), vm((KK, 128), f32),
+        vm((TILES, D, 128), f32),
+        vm((D, 128), f32), vm((128, 256), f32), vm((3 * D, 3 * 128), f32),
         vm((depth, 128), f32),
+        vm((D, TOK), bf16), vm((D, TOK), bf16), vm((D, TOK), bf16), vm((D, TOK), bf16),
+        pltpu.SemaphoreType.DMA((5 + TOK // TILE_THREE,)),
+    ]
+    slot = [
+        vm((KK, TILE_TWO), f32), vm((KK, TILE_TWO), bf16), vm((D, TILE_TWO), f32), vm((D, TILE_TWO), f32), vm((HID, TILE_TWO), f32),
+        vm((KK, TILE_TWO), bf16), vm((112, TILE_TWO), bf16), vm((112, TILE_TWO), bf16), vm((8, TILE_TWO), f32),
     ]
     whole = pl.BlockSpec(memory_space=pltpu.VMEM)
-    return pl.pallas_call(
+    far = pl.BlockSpec(memory_space=pl.ANY)
+    shape = jax.ShapeDtypeStruct
+    out, grad_chunks, *rest = pl.pallas_call(
         functools.partial(image_kernel, starts, rows_of),
         out_shape=(
-            jax.ShapeDtypeStruct((D, TOK), bf16),
-            jax.ShapeDtypeStruct((D, TOK), bf16),
-            jax.ShapeDtypeStruct((len(starts), rows_of, D), bf16),
+            shape((D, TOK), bf16), shape((len(starts), rows_of, D), bf16),
+            shape((D, TOK), bf16), shape((D, TOK), bf16), shape((D, TOK), bf16), shape((8, TOK), f32),
+            shape((KK, 128), f32), shape((KK, 128), f32), shape((16, 128), f32), shape((16, 128), f32),
+            shape((D, D), bf16), shape((D, 256), bf16),
         ),
-        in_specs=[pl.BlockSpec(memory_space=pltpu.SMEM)] + [whole] * 6,
-        out_specs=(whole, whole, whole),
-        scratch_shapes=scratch,
+        in_specs=[pl.BlockSpec(memory_space=pltpu.SMEM), whole, far, far, whole, whole, whole],
+        out_specs=(far, whole, far, far, far) + (whole,) * 7,
+        scratch_shapes=scratch + slot + slot,
         compiler_params=pltpu.CompilerParams(vmem_limit_bytes=63 * 1024 * 1024),
         name="image_step",
     )(image_side, chunks, pixels, cotangent, lane_index(), zsel, tsel)
+    return out, grad_chunks, rest
+
+
+def input_step(rest):
+    far = pl.BlockSpec(memory_space=pl.ANY)
+    vm = pltpu.VMEM
+    scratch = [vm(part.shape, part.dtype) for part in rest]
+    scratch += [vm((D, TOK), bf16), vm((FIELD, 128), f32), vm((FIELD, 128), f32), vm((TILE_THREE, 256), bf16)]
+    return pl.pallas_call(
+        input_kernel,
+        out_shape=jax.ShapeDtypeStruct((D, TOK), bf16),
+        in_specs=[far] * len(rest),
+        out_specs=far,
+        scratch_shapes=scratch + [pltpu.SemaphoreType.DMA((10 + TOK // TILE_THREE,))],
+        compiler_params=pltpu.CompilerParams(vmem_limit_bytes=60 * 1024 * 1024),
+        cost_estimate=pl.CostEstimate(flops=2 * D * 3 * D * TOK, bytes_accessed=16 * 1024 * 1024, transcendentals=0),
+        name="input_step",
+    )(*rest)
 
 
 def adam_update(gradient, master_part, first_part, second_part, average_part, step_rates):
@@ -658,14 +826,15 @@
 
     outs, grads_in, grad_chunks = [], [], None
     for k in range(tokens.shape[0]):
-        out, grad_in, chunk = image_step(starts, rows_of, chunks, tokens[k], image_sides[k : k + 1], grad_out[k])
+        out, chunk, rest = image_step(starts, rows_of, chunks, tokens[k], image_sides[k : k + 1], grad_out[k])
         outs.append(out)
-        grads_in.append(grad_in)
+        grads_in.append(input_step(rest))
         grad_chunks = chunk if k == 0 else (grad_chunks.astype(f32) + chunk.astype(f32)).astype(bf16)
     block_out = jnp.stack(outs)
     grad_in = jnp.stack(grads_in)
 
     parts = lax.all_to_all(grad_chunks, "wide", 0, 0)
+    parts, grad_in = lax.optimization_barrier((parts, grad_in))
     total = jnp.sum(parts.astype(f32), axis=0)
     total = total + lax.ppermute(total, "narrow", [(0, 1), (1, 0)])
     reduced = lax.dynamic_slice(total.reshape(rows_of * D), (inset,), (shard_len,))

time: 88 us -> 83.2 us (0.945)
  blocking collectives: 15.7 us -> 0 us
  waiting for transfers between devices: 13.2 us -> 19.3 us
  starting transfers between devices: 8.38 us -> 12 us
  Pallas kernels: 44.4 us -> 45.5 us
    all_to_all x1 -> x0, blocking collectives: 15.7 us -> none  [shards(): parts = lax.all_to_all(grad_chunks, 'wide', 0, 0)]
    all_to_all x0 -> x1, waiting for transfers between devices: none -> 6.05 us  [shards(): parts = lax.all_to_all(grad_chunks, 'wide', 0, 0)]
    pallas_call x0 -> x1, Pallas kernels: none -> 5.89 us  [input_step(): pl.pallas_call(input_kernel, out_shape=jax.ShapeDtypeStruct((D, TOK), bf1...]
    pallas_call x1, Pallas kernels: 44.4 us -> 39.7 us  [image_step(): pl.pallas_call(functools.partial(image_kernel, starts, rows_of), out_shap...]
    all_to_all x0 -> x1, starting transfers between devices: none -> 3.59 us  [shards(): parts = lax.all_to_all(grad_chunks, 'wide', 0, 0)]
  transfers between devices with their start and end apart: 2 -> 3, of which waited for: 2 -> 3; matrix products, arithmetic and copies ran while one was open for 0% -> 0% of each run, Pallas kernels for 0% -> 7%
where the time goes in v3:
time: 83.2 us; the launch traced here: 82.7 us
  Pallas kernels  45.5 us (55%)
  waiting for transfers between devices  19.3 us (23%)
  starting transfers between devices  12 us (14%)
  other arithmetic  2.4 us (3%)
  local copies, waits for them, and re-layouts  2.08 us (2%)
  between operations  1.42 us (2%)
    pallas_call x1, Pallas kernels, image_step(): pl.pallas_call(functools.partial(image_kernel, starts, rows_of), out_shap...  39.7 us
    all_to_all x1, waiting for transfers between devices, shards(): chunks = lax.all_to_all(own, 'wide', 0, 0)  12 us
    all_to_all x1, starting transfers between devices, shards(): chunks = lax.all_to_all(own, 'wide', 0, 0)  8.31 us
    all_to_all x1, waiting for transfers between devices, shards(): parts = lax.all_to_all(grad_chunks, 'wide', 0, 0)  6.05 us
    pallas_call x1, Pallas kernels, input_step(): pl.pallas_call(input_kernel, out_shape=jax.ShapeDtypeStruct((D, TOK), bf1...  5.89 us
    all_to_all x1, starting transfers between devices, shards(): parts = lax.all_to_all(grad_chunks, 'wide', 0, 0)  3.59 us
  transfers between devices with their start and end apart: 3, of which 3 were waited for; matrix products, arithmetic and copies ran while one was open for 0% of the time, Pallas kernels for 7%

profile of v3, /device:TPU:0, one launch (start us, length us, event | category | flops | bytes accessed | tf_op | source)
XLA Modules:
  0.0 82.7 jit_solution(11191476708975719713)
XLA Ops:
  0.6 0.8 convert_element_type.6
  1.4 0.3 dynamic_update_slice.3
  1.7 0.1 broadcast_in_dim.11
  1.8 0.8 broadcast_in_dim.12
  2.6 8.3 %all-to-all-start = ((bf16[16,96,96]{2,1,0:T(8,128)(2,1)}), bf16[16,96,96]{2,1,0:T(8,128)(2,1)S(1)}, u32[]{:S(2)}, u32[]{:S(2)}) async-start(bf16[16,96,96]{2,1,0:T(8,128)(2,1)} %broadcast_in_dim.12), calls=%async_computation | async-start | bytes 786432 | tf_op jit(solution)/shard_map/all_to_all | solution.py:825
  11.6 12.0 %all-to-all-done.chunk_ref = bf16[16,96,96]{2,1,0:T(8,128)(2,1)S(1)} async-done(((bf16[16,96,96]{2,1,0:T(8,128)(2,1)}), bf16[16,96,96]{2,1,0:T(8,128)(2,1)S(1)}, u32[]{:S(2)}, u32[]{:S(2)}) %all-to-all-start) | async-done | bytes 294944 | tf_op jit(solution)/shard_map/all_to_all | solution.py:825
  23.6 0.0 copy-start
  23.6 0.7 copy-done
  24.3 39.7 %image_step.1 = (bf16[96,6400]{1,0:T(8,128)(2,1)}, bf16[16,96,96]{2,1,0:T(8,128)(2,1)}, bf16[96,6400]{1,0:T(8,128)(2,1)}, bf16[96,6400]{1,0:T(8,128)(2,1)}, bf16...) custom-call(s32[1]{0:T(128)S(6)} %copy.18.side_ref, ...), custom_call_target="tpu_custom_call" | custom-call | tf_op jit(solution)/shard_map/image_step/pallas_call | solution.py:770
  64.0 3.6 %all-to-all-start.1 = ((bf16[16,96,96]{2,1,0:T(8,128)(2,1)}), bf16[16,96,96]{2,1,0:T(8,128)(2,1)S(1)}, u32[]{:S(2)}, u32[]{:S(2)}) async-start(bf16[16,96,96]{2,1,0:T(8,128)(2,1)} %get-tuple-element.21), calls=%async_computation.1 | async-start | bytes 786432 | tf_op jit(solution)/shard_map/all_to_all | solution.py:836
  67.6 0.0 copy-start.1
  67.6 0.0 copy-start.2
  67.6 0.0 copy-start.3
  67.7 0.0 copy-start.4
  67.7 5.9 %input_step.1 = bf16[96,6400]{1,0:T(8,128)(2,1)} custom-call(bf16[96,6400]{1,0:T(8,128)(2,1)} %get-tuple-element.22.refs_0_, bf16[96,6400]{1,0:T(8,128)(2,1)} %get-tuple-element.23.refs_1_, bf16[96,6400]{1,0:T(8,128)(2,1)} %get-tuple-element.24.refs_2_, f32[8,6400]{1,0:T(8,128)} %get-tuple-element.25.refs_3_, f32[400,128]{1,0:T(8,128)} %get-tuple-element.26.refs_4_, ...), custom_call_target="tpu_custom_call" | custom-call | flops 353894400 | bytes 16777216 | tf_op jit(solution)/shard_map/input_step/pallas_call | solution.py:792
  73.6 6.1 %all-to-all-done.1 = bf16[16,96,96]{2,1,0:T(8,128)(2,1)S(1)} async-done(((bf16[16,96,96]{2,1,0:T(8,128)(2,1)}), bf16[16,96,96]{2,1,0:T(8,128)(2,1)S(1)}, u32[]{:S(2)}, u32[]{:S(2)}) %all-to-all-start.1) | async-done | bytes 294944 | tf_op jit(solution)/shard_map/all_to_all | solution.py:836
  79.6 0.1 convert_reduce_fusion
  79.7 0.1 collective-permute-start
  79.8 1.2 %collective-permute-done = f32[96,96]{1,0:T(8,128)S(1)} collective-permute-done((f32[96,96]{1,0:T(8,128)S(1)}, f32[96,96]{1,0:T(8,128)S(1)}, u32[]{:S(2)}, u32[]{:S(2)}) %collective-permute-start) | collective-permute-done | bytes 36896 | tf_op jit(solution)/shard_map/ppermute | solution.py:839
  81.0 0.1 reshape.17
  81.1 0.0 copy-done.1
  81.1 0.0 copy-done.2
  81.1 0.0 copy-done.3
  81.1 0.0 copy-done.4
  81.1 1.5 %multiply_add_fusion = (f32[9060]{0:T(1024)}, f32[9060]{0:T(1024)}, f32[9060]{0:T(1024)}, f32[9060]{0:T(1024)}) fusion(f32[9060]{0:T(1024)S(1)} %copy-done.2, f32[9060]{0:T(1024)S(1)} %copy-done.1, f32[144960]{0:T(1024)} %constant.50.clone, s32[]{:T(128)S(6)} %select_n.8, f32[9216]{0:T(1024)S(1)} %reshape.17, s32[]{:T(128)S(6)} %select_n.7, ...), kind=kLoop, calls=%fused_computation.1 | loop fusion | flops 163080 | bytes 362408 | tf_op jit(solution)/shard_map/add | solution.py:811
  (2 shorter events, 0.0 us)
Async XLA Ops:
  2.6 21.0 %all-to-all-start = ((bf16[16,96,96]{2,1,0:T(8,128)(2,1)}), bf16[16,96,96]{2,1,0:T(8,128)(2,1)S(1)}, u32[]{:S(2)}, u32[]{:S(2)}) async-start(bf16[16,96,96]{2,1,0:T(8,128)(2,1)} %broadcast_in_dim.12), calls=%async_computation | async-start | bytes 786432 | tf_op jit(solution)/shard_map/all_to_all | solution.py:825
  23.6 0.7 copy-start
  64.0 15.6 %all-to-all-start.1 = ((bf16[16,96,96]{2,1,0:T(8,128)(2,1)}), bf16[16,96,96]{2,1,0:T(8,128)(2,1)S(1)}, u32[]{:S(2)}, u32[]{:S(2)}) async-start(bf16[16,96,96]{2,1,0:T(8,128)(2,1)} %get-tuple-element.21), calls=%async_computation.1 | async-start | bytes 786432 | tf_op jit(solution)/shard_map/all_to_all | solution.py:836
  67.6 13.5 %copy-start.1 = (f32[9060]{0:T(1024)S(1)}, f32[9060]{0:T(1024)}, u32[]{:S(2)}) copy-start(f32[9060]{0:T(1024)} %param.14) | copy-start | bytes 108724
  67.6 13.5 %copy-start.2 = (f32[9060]{0:T(1024)S(1)}, f32[9060]{0:T(1024)}, u32[]{:S(2)}) copy-start(f32[9060]{0:T(1024)} %param.17) | copy-start | bytes 108724
  67.6 13.5 %copy-start.3 = (f32[9060]{0:T(1024)S(1)}, f32[9060]{0:T(1024)}, u32[]{:S(2)}) copy-start(f32[9060]{0:T(1024)} %param.15) | copy-start | bytes 108724
  67.7 13.5 %copy-start.4 = (f32[9060]{0:T(1024)S(1)}, f32[9060]{0:T(1024)}, u32[]{:S(2)}) copy-start(f32[9060]{0:T(1024)} %param.16) | copy-start | bytes 108724
  79.7 1.3 %collective-permute-start = (f32[96,96]{1,0:T(8,128)S(1)}, f32[96,96]{1,0:T(8,128)S(1)}, u32[]{:S(2)}, u32[]{:S(2)}) collective-permute-start(f32[96,96]{1,0:T(8,128)S(1)} %convert_reduce_fusion), channel_id=1, source_target_pairs={{0,1},{1,0},{2,3},{3,2},{4,5},{5,4},{6,7},{7,6},{8,9},{9,8},{10,11... | collective-permute-start | bytes 110600 | tf_op jit(solution)/shard_map/ppermute | solution.py:839

commit v4 on v3

--- a/solution.py
+++ b/solution.py
@@ -33,6 +33,7 @@
 HALO = 128
 LEAD = 88
 FIELD = LEAD + TOK + 8
+TILE_PROJECT = 3200
 TILE_ONE = 6400
 TILE_TWO = 1280
 TILE_THREE = 1280
@@ -279,15 +280,16 @@
 
 
 def image_kernel(
+    shard_len,
     starts,
     rows_of,
     side_ref,
     chunk_ref,
     x_hbm,
     gy_hbm,
-    idx_ref,
-    zsel_ref,
-    tsel_ref,
+    idx_hbm,
+    zsel_hbm,
+    tsel_hbm,
     out_hbm,
     gchunk_ref,
     field_hbm,
@@ -301,22 +303,43 @@
     wqt,
     wkvg,
     wf, wq, wkt, wvt, wp, wpt, w1, w1t, w2, w2t, relh, rel, relt, cols, kq,
-    fq, fk, fv, gfk, gfv, qb, gq, gm, un, fcol,
+    fq, fk, fv, qb, gm, un, fcol,
     a1, a2, vb, vbt, kp, vpool,
     rhs, gse, n1aug, goaug, gsh, gkv,
-    dw2, dw1, dpr, gv, gkr, hacc, dwq, dwkv, kqacc, gr, x_ref, gy_ref, out_ref, gfield, copy_sem,
+    dw2, dw1, dpr, gv, gkr, hacc, dwq, dwkv, kqacc, gr, x_ref, gy_ref, out_ref, gfield, copy_sem, flat, zsel_ref, tsel_ref, idx_ref, table_sem,
     *slot_refs,
 ):
+    gq, gfk, gfv = fq, fk, fv
     slots = (slot_refs[: len(slot_refs) // 2], slot_refs[len(slot_refs) // 2 :])
     side = side_ref[0]
+    table_copies = [
+        pltpu.make_async_copy(source, target, table_sem.at[k])
+        for k, (source, target) in enumerate(((zsel_hbm, zsel_ref), (tsel_hbm, tsel_ref), (idx_hbm, idx_ref)))
+    ]
+    for copy in table_copies:
+        copy.start()
     x_copy = pltpu.make_async_copy(x_hbm, x_ref, copy_sem.at[0])
     gy_copy = pltpu.make_async_copy(gy_hbm, gy_ref, copy_sem.at[1])
     x_copy.start()
     gy_copy.start()
 
-    wf[...] = jnp.zeros(wf.shape, f32)
-    for w, start in enumerate(starts):
-        wf[start : start + rows_of, 0:D] += chunk_ref[w].astype(f32)
+    flat[...] = jnp.zeros(flat.shape, f32)
+    lane_of = lax.broadcasted_iota(jnp.int32, chunk_ref.shape[1:], 1)
+    for w in range(len(starts)):
+        base, inset = (shard_len * w) // 128, (shard_len * w) % 128
+        part = chunk_ref[w].astype(f32)
+        if inset:
+            part = pltpu.roll(part, inset, 1)
+            flat[base + 1 : base + 1 + part.shape[0], :] += jnp.where(lane_of < inset, part, 0.0)
+            part = jnp.where(lane_of < inset, 0.0, part)
+        flat[base : base + part.shape[0], :] += part
+    groups = -(-(shard_len * len(starts)) // (4 * D))
+    lane_of = lax.broadcasted_iota(jnp.int32, (groups, 128), 1)
+    first, second, third = (flat[pl.ds(k, groups, stride=3), :] for k in range(3))
+    wf[pl.ds(0, groups, stride=4), :] = first
+    wf[pl.ds(1, groups, stride=4), :] = pltpu.roll(jnp.where(lane_of >= 96, first, second), 32, 1)
+    wf[pl.ds(2, groups, stride=4), :] = pltpu.roll(jnp.where(lane_of >= 64, second, third), 64, 1)
+    wf[pl.ds(3, groups, stride=4), :] = pltpu.roll(third, 96, 1)
 
     def piece(name, count, first=0):
         base = ROW[name] + first
@@ -374,6 +397,8 @@
         full = jnp.concatenate([pool_columns(name), jnp.zeros((32, 128), f32)], axis=0)
         return jnp.transpose(full)[0:16, :]
 
+    for copy in table_copies:
+        copy.wait()
     pooled_kernel = pool_columns("pool_q")
     for k in range(9):
         kq[k] = jnp.broadcast_to(pooled_kernel[:, k : k + 1], (D, 128))
@@ -384,7 +409,7 @@
     kk[...] = pool_rows("pool_k")
     kv[...] = pool_rows("pool_v")
 
-    for ref in (fq, gq):
+    for ref in (fq,):
         ref[:, 0:HALO] = jnp.zeros((D, HALO), f32)
         ref[:, HALO + TOK :] = jnp.zeros((D, HALO), f32)
     for ref in (fk, fv):
@@ -396,7 +421,7 @@
     gr[tail:, :] = jnp.zeros((gr.shape[0] - tail, 128), f32)
 
     un[D:, :] = two_ones(TOK)
-    n1aug[D:, :] = two_ones(TILE_ONE)
+    n1aug[D:, :] = two_ones(TILE_PROJECT)
     for slot in slots:
         slot[5][HID:, :] = two_ones(TILE_TWO)
         slot[6][D:, :] = two_ones(TILE_TWO)
@@ -419,18 +444,18 @@
     x_copy.wait()
 
     def project(i, carry):
-        here = plain(i, TILE_ONE)
+        here = plain(i, TILE_PROJECT)
         unit, inv = normalize(x_ref[:, here].astype(f32))
         un[0:D, here] = unit.astype(bf16)
         inv_ref[0:1, here] = inv
         n1aug[0:D, :] = (unit * cols[:, 3:4] + cols[:, 4:5]).astype(bf16)
-        fq[:, inner(i, TILE_ONE)] = dot(wq[...], n1aug[...]) * token_mask(i, TILE_ONE)
-        field = pl.ds(pl.multiple_of(i * TILE_ONE + LEAD, 8), TILE_ONE)
+        fq[:, inner(i, TILE_PROJECT)] = dot(wq[...], n1aug[...]) * token_mask(i, TILE_PROJECT)
+        field = pl.ds(pl.multiple_of(i * TILE_PROJECT + LEAD, 8), TILE_PROJECT)
         fk[field, :] = dot_tn(n1aug[...], wkt[...])
         fv[field, :] = dot_tn(n1aug[...], wvt[...])
         return carry
 
-    lax.fori_loop(0, TOK // TILE_ONE, project, 0)
+    lax.fori_loop(0, TOK // TILE_PROJECT, project, 0)
 
     unit_copy = pltpu.make_async_copy(un.at[0:D, :], unit_hbm, copy_sem.at[4])
     unit_copy.start()
@@ -623,10 +648,10 @@
         for a in range(KG):
             grad = pooled[KG * a : KG * a + KG, :]
             inside = jnp.where(b_index == 0, 0.0, grad)
-            spread_keys(taps, grad, a, gspread)
             for k in range(9):
                 where = pl.ds(tap_start(a, k // 3, k % 3), KG, stride=KSTR)
                 sums[k] = sums[k] + (inside if k % 3 == 0 else grad) * field[where, :]
+            spread_keys(taps, grad, a, gspread)
         rows = [jnp.sum(total, axis=0, keepdims=True) for total in sums]
         rows = jnp.concatenate(rows + [jnp.zeros((128 - 9, 128), f32)], axis=0)
         pool_gradient(name, jnp.transpose(rows)[:D, :])
@@ -734,8 +759,13 @@
         gchunk_ref[w] = gr[start : start + rows_of, 0:D].astype(bf16)
 
 
-def image_step(starts, rows_of, chunks, pixels, image_side, cotangent):
-    depth = 8 * (-(-(starts[-1] + rows_of) // 8))
+def image_step(shard_len, chunks, pixels, image_side, cotangent):
+    starts = tuple((shard_len * w) // D for w in range(chunks.shape[0]))
+    rows_of = block_rows(shard_len)
+    groups = -(-(shard_len * len(starts)) // (4 * D))
+    depth = max(8 * (-(-(starts[-1] + rows_of) // 8)), 4 * groups)
+    flat_rows = max(3 * groups, (shard_len * (len(starts) - 1)) // 128 + chunks.shape[1] + 1)
+    flat_rows = 8 * (-(-flat_rows // 8))
     zsel, tsel = pool_selectors()
     vm = pltpu.VMEM
     scratch = [
@@ -746,12 +776,11 @@
         vm((168, 128), f32), vm((256, D), bf16), vm((D, 256), bf16),
         vm((D, 128), f32), vm((9, D, 128), f32),
         vm((D, TOK + 2 * HALO), f32), vm((FIELD, 128), f32), vm((FIELD, 128), f32),
-        vm((FIELD, 128), f32), vm((FIELD, 128), f32),
-        vm((D, TOK), bf16), vm((D, TOK + 2 * HALO), f32), vm((D, TOK), bf16),
+        vm((D, TOK), bf16), vm((D, TOK), bf16),
         vm((112, TOK), bf16), vm((3 * D, TOK), bf16),
         vm((KK, 208), bf16), vm((144, KK), bf16), vm((112, KK), bf16), vm((KK, 112), bf16),
         vm((KK, 128), f32), vm((KK, 128), f32),
-        vm((208, TILE_TWO), bf16), vm((KK + 256, TILE_TWO), bf16), vm((112, TILE_ONE), bf16), vm((112, TILE_TWO), bf16),
+        vm((208, TILE_TWO), bf16), vm((KK + 256, TILE_TWO), bf16), vm((112, TILE_PROJECT), bf16), vm((112, TILE_TWO), bf16),
         vm((3 * D, TILE_THREE), bf16), vm((TILE_THREE, 256), bf16),
         vm((D, 512), f32), vm((128, HID), f32), vm((D, 128), f32), vm((128, 512), f32), vm((128, 768), f32),
         vm((TILES, D, 128), f32),
@@ -759,6 +788,8 @@
         vm((depth, 128), f32),
         vm((D, TOK), bf16), vm((D, TOK), bf16), vm((D, TOK), bf16), vm((D, TOK), bf16),
         pltpu.SemaphoreType.DMA((5 + TOK // TILE_THREE,)),
+        vm((flat_rows, 128), f32),
+        vm(zsel.shape, bf16), vm(tsel.shape, bf16), vm((8, TOK + 2 * HALO), jnp.int32), pltpu.SemaphoreType.DMA((3,)),
     ]
     slot = [
         vm((KK, TILE_TWO), f32), vm((KK, TILE_TWO), bf16), vm((D, TILE_TWO), f32), vm((D, TILE_TWO), f32), vm((HID, TILE_TWO), f32),
@@ -768,17 +799,17 @@
     far = pl.BlockSpec(memory_space=pl.ANY)
     shape = jax.ShapeDtypeStruct
     out, grad_chunks, *rest = pl.pallas_call(
-        functools.partial(image_kernel, starts, rows_of),
+        functools.partial(image_kernel, shard_len, starts, rows_of),
         out_shape=(
             shape((D, TOK), bf16), shape((len(starts), rows_of, D), bf16),
             shape((D, TOK), bf16), shape((D, TOK), bf16), shape((D, TOK), bf16), shape((8, TOK), f32),
             shape((KK, 128), f32), shape((KK, 128), f32), shape((16, 128), f32), shape((16, 128), f32),
             shape((D, D), bf16), shape((D, 256), bf16),
         ),
-        in_specs=[pl.BlockSpec(memory_space=pltpu.SMEM), whole, far, far, whole, whole, whole],
+        in_specs=[pl.BlockSpec(memory_space=pltpu.SMEM), whole, far, far, far, far, far],
         out_specs=(far, whole, far, far, far) + (whole,) * 7,
         scratch_shapes=scratch + slot + slot,
-        compiler_params=pltpu.CompilerParams(vmem_limit_bytes=63 * 1024 * 1024),
+        compiler_params=pltpu.CompilerParams(vmem_limit_bytes=54 * 1024 * 1024),
         name="image_step",
     )(image_side, chunks, pixels, cotangent, lane_index(), zsel, tsel)
     return out, grad_chunks, rest
@@ -816,17 +847,16 @@
     shard_len = master.shape[0]
     owners = lax.axis_size("wide")
     images_all = tokens.shape[0] * owners * lax.axis_size("narrow")
-    starts = tuple((shard_len * w) // D for w in range(owners))
     rows_of = block_rows(shard_len)
     inset = lax.rem(lax.axis_index("wide") * shard_len, D)
 
-    own = lax.dynamic_update_slice(jnp.zeros((rows_of * D,), bf16), master.astype(bf16), (inset,))
-    own = jnp.broadcast_to(own.reshape(1, rows_of, D), (owners, rows_of, D))
-    chunks = lax.all_to_all(own, "wide", 0, 0)
+    filled = 1024 * (-(-shard_len // 1024))
+    own = jnp.pad(master, (0, filled - shard_len)).reshape(1, filled // 128, 128).astype(bf16)
+    chunks = lax.all_to_all(jnp.broadcast_to(own, (owners, filled // 128, 128)), "wide", 0, 0)
 
     outs, grads_in, grad_chunks = [], [], None
     for k in range(tokens.shape[0]):
-        out, chunk, rest = image_step(starts, rows_of, chunks, tokens[k], image_sides[k : k + 1], grad_out[k])
+        out, chunk, rest = image_step(shard_len, chunks, tokens[k], image_sides[k : k + 1], grad_out[k])
         outs.append(out)
         grads_in.append(input_step(rest))
         grad_chunks = chunk if k == 0 else (grad_chunks.astype(f32) + chunk.astype(f32)).astype(bf16)

time: 83.2 us -> 81.1 us (0.975)
  waiting for transfers between devices: 19.3 us -> 17.1 us
    all_to_all x1, waiting for transfers between devices: 12 us -> 10 us  [shards(): lax.all_to_all(jnp.broadcast_to(own, (owners, filled // 128, 128)), 'wide...]
where the time goes in v4:
time: 81.1 us; the launch traced here: 80.6 us
  Pallas kernels  46.2 us (57%)
  waiting for transfers between devices  17.1 us (21%)
  starting transfers between devices  11.9 us (15%)
  other arithmetic  2.4 us (3%)
  local copies, waits for them, and re-layouts  1.59 us (2%)
  between operations  1.41 us (2%)
    pallas_call x1, Pallas kernels, image_step(): pl.pallas_call(functools.partial(image_kernel, shard_len, starts, rows_of...  40.3 us
    all_to_all x1, waiting for transfers between devices, shards(): lax.all_to_all(jnp.broadcast_to(own, (owners, filled // 128, 128)), 'wide...  10 us
    all_to_all x1, starting transfers between devices, shards(): lax.all_to_all(jnp.broadcast_to(own, (owners, filled // 128, 128)), 'wide...  8.31 us
    pallas_call x1, Pallas kernels, input_step(): pl.pallas_call(input_kernel, out_shape=jax.ShapeDtypeStruct((D, TOK), bf1...  5.89 us
    all_to_all x1, waiting for transfers between devices, shards(): parts = lax.all_to_all(grad_chunks, 'wide', 0, 0)  5.83 us
    all_to_all x1, starting transfers between devices, shards(): parts = lax.all_to_all(grad_chunks, 'wide', 0, 0)  3.56 us
  transfers between devices with their start and end apart: 3, of which 3 were waited for; matrix products, arithmetic and copies ran while one was open for 0% of the time, Pallas kernels for 7%

profile of v4, /device:TPU:0, one launch (start us, length us, event | category | flops | bytes accessed | tf_op | source)
XLA Modules:
  0.0 80.6 jit_solution(17073800958481732078)
XLA Ops:
  0.6 0.8 convert.4
  1.4 0.8 broadcast_in_dim.2
  2.2 8.3 %all-to-all-start = ((bf16[16,72,128]{2,1,0:T(8,128)(2,1)}), bf16[16,72,128]{2,1,0:T(8,128)(2,1)S(1)}, u32[]{:S(2)}, u32[]{:S(2)}) async-start(bf16[16,72,128]{2,1,0:T(8,128)(2,1)} %broadcast_in_dim.2), calls=%async_computation | async-start | bytes 589824 | tf_op jit(solution)/shard_map/all_to_all | solution.py:855
  11.1 10.0 %all-to-all-done.chunk_ref = bf16[16,72,128]{2,1,0:T(8,128)(2,1)S(1)} async-done(((bf16[16,72,128]{2,1,0:T(8,128)(2,1)}), bf16[16,72,128]{2,1,0:T(8,128)(2,1)S(1)}, u32[]{:S(2)}, u32[]{:S(2)}) %all-to-all-start) | async-done | bytes 294944 | tf_op jit(solution)/shard_map/all_to_all | solution.py:855
  21.2 0.0 copy-start
  21.2 0.7 copy-done
  21.9 40.3 %image_step.1 = (bf16[96,6400]{1,0:T(8,128)(2,1)}, bf16[16,96,96]{2,1,0:T(8,128)(2,1)}, bf16[96,6400]{1,0:T(8,128)(2,1)}, bf16[96,6400]{1,0:T(8,128)(2,1)}, bf16...) custom-call(s32[1]{0:T(128)S(6)} %copy.17.side_ref, ...), custom_call_target="tpu_custom_call" | custom-call | tf_op jit(solution)/shard_map/image_step/pallas_call | solution.py:801
  62.2 3.6 %all-to-all-start.1 = ((bf16[16,96,96]{2,1,0:T(8,128)(2,1)}), bf16[16,96,96]{2,1,0:T(8,128)(2,1)S(1)}, u32[]{:S(2)}, u32[]{:S(2)}) async-start(bf16[16,96,96]{2,1,0:T(8,128)(2,1)} %get-tuple-element.21), calls=%async_computation.1 | async-start | bytes 786432 | tf_op jit(solution)/shard_map/all_to_all | solution.py:866
  65.8 0.0 copy-start.1
  65.8 0.0 copy-start.2
  65.8 0.0 copy-start.3
  65.8 0.0 copy-start.4
  65.8 5.9 %input_step.1 = bf16[96,6400]{1,0:T(8,128)(2,1)} custom-call(bf16[96,6400]{1,0:T(8,128)(2,1)} %get-tuple-element.22.refs_0_, bf16[96,6400]{1,0:T(8,128)(2,1)} %get-tuple-element.23.refs_1_, bf16[96,6400]{1,0:T(8,128)(2,1)} %get-tuple-element.24.refs_2_, f32[8,6400]{1,0:T(8,128)} %get-tuple-element.25.refs_3_, f32[400,128]{1,0:T(8,128)} %get-tuple-element.26.refs_4_, ...), custom_call_target="tpu_custom_call" | custom-call | flops 353894400 | bytes 16777216 | tf_op jit(solution)/shard_map/input_step/pallas_call | solution.py:823
  71.7 5.8 %all-to-all-done.1 = bf16[16,96,96]{2,1,0:T(8,128)(2,1)S(1)} async-done(((bf16[16,96,96]{2,1,0:T(8,128)(2,1)}), bf16[16,96,96]{2,1,0:T(8,128)(2,1)S(1)}, u32[]{:S(2)}, u32[]{:S(2)}) %all-to-all-start.1) | async-done | bytes 294944 | tf_op jit(solution)/shard_map/all_to_all | solution.py:866
  77.6 0.1 convert_reduce_fusion
  77.6 0.1 collective-permute-start
  77.7 1.2 %collective-permute-done = f32[96,96]{1,0:T(8,128)S(1)} collective-permute-done((f32[96,96]{1,0:T(8,128)S(1)}, f32[96,96]{1,0:T(8,128)S(1)}, u32[]{:S(2)}, u32[]{:S(2)}) %collective-permute-start) | collective-permute-done | bytes 36896 | tf_op jit(solution)/shard_map/ppermute | solution.py:869
  79.0 0.1 reshape.24
  79.1 0.0 copy-done.1
  79.1 0.0 copy-done.2
  79.1 0.0 copy-done.3
  79.1 0.0 copy-done.4
  79.1 1.5 %multiply_add_fusion = (f32[9060]{0:T(1024)}, f32[9060]{0:T(1024)}, f32[9060]{0:T(1024)}, f32[9060]{0:T(1024)}) fusion(f32[9060]{0:T(1024)S(1)} %copy-done.2, f32[9060]{0:T(1024)S(1)} %copy-done.1, f32[144960]{0:T(1024)} %constant.51.clone, s32[]{:T(128)S(6)} %select_n.6, f32[9216]{0:T(1024)S(1)} %reshape.24, s32[]{:T(128)S(6)} %select_n.7, ...), kind=kLoop, calls=%fused_computation.1 | loop fusion | flops 163080 | bytes 362408 | tf_op jit(solution)/shard_map/add | solution.py:842
  (2 shorter events, 0.0 us)
Async XLA Ops:
  2.2 19.0 %all-to-all-start = ((bf16[16,72,128]{2,1,0:T(8,128)(2,1)}), bf16[16,72,128]{2,1,0:T(8,128)(2,1)S(1)}, u32[]{:S(2)}, u32[]{:S(2)}) async-start(bf16[16,72,128]{2,1,0:T(8,128)(2,1)} %broadcast_in_dim.2), calls=%async_computation | async-start | bytes 589824 | tf_op jit(solution)/shard_map/all_to_all | solution.py:855
  21.2 0.7 copy-start
  62.2 15.3 %all-to-all-start.1 = ((bf16[16,96,96]{2,1,0:T(8,128)(2,1)}), bf16[16,96,96]{2,1,0:T(8,128)(2,1)S(1)}, u32[]{:S(2)}, u32[]{:S(2)}) async-start(bf16[16,96,96]{2,1,0:T(8,128)(2,1)} %get-tuple-element.21), calls=%async_computation.1 | async-start | bytes 786432 | tf_op jit(solution)/shard_map/all_to_all | solution.py:866
  65.8 13.3 %copy-start.1 = (f32[9060]{0:T(1024)S(1)}, f32[9060]{0:T(1024)}, u32[]{:S(2)}) copy-start(f32[9060]{0:T(1024)} %param.14) | copy-start | bytes 108724
  65.8 13.3 %copy-start.2 = (f32[9060]{0:T(1024)S(1)}, f32[9060]{0:T(1024)}, u32[]{:S(2)}) copy-start(f32[9060]{0:T(1024)} %param.17) | copy-start | bytes 108724
  65.8 13.3 %copy-start.3 = (f32[9060]{0:T(1024)S(1)}, f32[9060]{0:T(1024)}, u32[]{:S(2)}) copy-start(f32[9060]{0:T(1024)} %param.15) | copy-start | bytes 108724
  65.8 13.3 %copy-start.4 = (f32[9060]{0:T(1024)S(1)}, f32[9060]{0:T(1024)}, u32[]{:S(2)}) copy-start(f32[9060]{0:T(1024)} %param.16) | copy-start | bytes 108724
  77.6 1.3 %collective-permute-start = (f32[96,96]{1,0:T(8,128)S(1)}, f32[96,96]{1,0:T(8,128)S(1)}, u32[]{:S(2)}, u32[]{:S(2)}) collective-permute-start(f32[96,96]{1,0:T(8,128)S(1)} %convert_reduce_fusion), channel_id=1, source_target_pairs={{0,1},{1,0},{2,3},{3,2},{4,5},{5,4},{6,7},{7,6},{8,9},{9,8},{10,11... | collective-permute-start | bytes 110600 | tf_op jit(solution)/shard_map/ppermute | solution.py:869

commit v5 on v4

--- a/solution.py
+++ b/solution.py
@@ -33,7 +33,7 @@
 HALO = 128
 LEAD = 88
 FIELD = LEAD + TOK + 8
-TILE_PROJECT = 3200
+TILE_PROJECT = 6400
 TILE_ONE = 6400
 TILE_TWO = 1280
 TILE_THREE = 1280
@@ -230,13 +230,11 @@
 
 def spread_keys(taps, grad, a, gfield):
     idle = LEAD + GRID * (KSTR * a + 2)
-    gfield[idle - 8 : idle + GRID, :] = jnp.zeros((GRID + 8, 128), f32)
+    gfield[pl.ds(aligned(idle - 8, 8), GRID + 8), :] = jnp.zeros((GRID + 8, 128), f32)
     for u in range(3):
         gfield[pl.ds(tap_start(a, u, 3), KG, stride=KSTR), :] = jnp.zeros((KG, 128), f32)
     for k in range(9):
         gfield[pl.ds(tap_start(a, k // 3, k % 3), KG, stride=KSTR), :] = taps[k] * grad
-    if a == KG - 1:
-        gfield[LEAD + TOK - GRID : LEAD + TOK, :] = jnp.zeros((GRID, 128), f32)
 
 
 def input_kernel(*refs):
@@ -250,8 +248,13 @@
         copy.wait()
     for kernel_rows, pooled, gfield in ((kk, gkt, gfk), (kv, gvt, gfv)):
         taps = tap_rows(kernel_rows)
-        for a in range(KG):
-            spread_keys(taps, pooled[KG * a : KG * a + KG, :], a, gfield)
+
+        def spread(a, carry):
+            spread_keys(taps, pooled[pl.ds(KG * a, KG), :], a, gfield)
+            return carry
+
+        lax.fori_loop(0, KG, spread, 0)
+        gfield[LEAD + TOK - GRID : LEAD + TOK, :] = jnp.zeros((GRID, 128), f32)
     for copy in copies[:4]:
         copy.wait()
 
@@ -652,6 +655,8 @@
                 where = pl.ds(tap_start(a, k // 3, k % 3), KG, stride=KSTR)
                 sums[k] = sums[k] + (inside if k % 3 == 0 else grad) * field[where, :]
             spread_keys(taps, grad, a, gspread)
+            if a == KG - 1:
+                gspread[LEAD + TOK - GRID : LEAD + TOK, :] = jnp.zeros((GRID, 128), f32)
         rows = [jnp.sum(total, axis=0, keepdims=True) for total in sums]
         rows = jnp.concatenate(rows + [jnp.zeros((128 - 9, 128), f32)], axis=0)
         pool_gradient(name, jnp.transpose(rows)[:D, :])
@@ -864,13 +869,13 @@
     grad_in = jnp.stack(grads_in)
 
     parts = lax.all_to_all(grad_chunks, "wide", 0, 0)
-    parts, grad_in = lax.optimization_barrier((parts, grad_in))
+    step_rates = lax.dynamic_slice_in_dim(
+        jnp.asarray(rate_values(shard_len * owners)), lax.axis_index("wide") * shard_len, shard_len
+    )
+    parts, grad_in, step_rates = lax.optimization_barrier((parts, grad_in, step_rates))
     total = jnp.sum(parts.astype(f32), axis=0)
     total = total + lax.ppermute(total, "narrow", [(0, 1), (1, 0)])
     reduced = lax.dynamic_slice(total.reshape(rows_of * D), (inset,), (shard_len,))
-    step_rates = lax.dynamic_slice_in_dim(
-        jnp.asarray(rate_values(shard_len * owners)), lax.axis_index("wide") * shard_len, shard_len
-    )
     updated, moment_one, moment_two, blended = adam_update(
         reduced / images_all, master, first_moment, second_moment, weight_average, step_rates
     )

time: 81.1 us -> 79.9 us (0.985)
  waiting for transfers between devices: 17.1 us -> 16.2 us
  local copies, waits for them, and re-layouts: 1.59 us -> 2.46 us
    all_to_all x1, waiting for transfers between devices: 5.83 us -> 4.96 us  [shards(): parts = lax.all_to_all(grad_chunks, 'wide', 0, 0)]
    dynamic_slice x0 -> x1, local copies, waits for them, and re-layouts: none -> 0.87 us  [shards(): lax.dynamic_slice_in_dim(jnp.asarray(rate_values(shard_len * owners)), la...]
  transfers between devices with their start and end apart: 3 -> 3, of which waited for: 3 -> 3; matrix products, arithmetic and copies ran while one was open for 0% -> 1% of each run, Pallas kernels for 7% -> 7%
where the time goes in v5:
time: 79.9 us; the launch traced here: 79.4 us
  Pallas kernels  45.8 us (57%)
  waiting for transfers between devices  16.2 us (20%)
  starting transfers between devices  11.9 us (15%)
  local copies, waits for them, and re-layouts  2.46 us (3%)
  other arithmetic  1.61 us (2%)
  between operations  1.41 us (2%)
    pallas_call x1, Pallas kernels, image_step(): pl.pallas_call(functools.partial(image_kernel, shard_len, starts, rows_of...  39.9 us
    all_to_all x1, waiting for transfers between devices, shards(): lax.all_to_all(jnp.broadcast_to(own, (owners, filled // 128, 128)), 'wide...  10 us
    all_to_all x1, starting transfers between devices, shards(): lax.all_to_all(jnp.broadcast_to(own, (owners, filled // 128, 128)), 'wide...  8.31 us
    pallas_call x1, Pallas kernels, input_step(): pl.pallas_call(input_kernel, out_shape=jax.ShapeDtypeStruct((D, TOK), bf1...  5.89 us
    all_to_all x1, waiting for transfers between devices, shards(): parts = lax.all_to_all(grad_chunks, 'wide', 0, 0)  4.96 us
    all_to_all x1, starting transfers between devices, shards(): parts = lax.all_to_all(grad_chunks, 'wide', 0, 0)  3.56 us
  transfers between devices with their start and end apart: 3, of which 3 were waited for; matrix products, arithmetic and copies ran while one was open for 1% of the time, Pallas kernels for 7%

profile of v5, /device:TPU:0, one launch (start us, length us, event | category | flops | bytes accessed | tf_op | source)
XLA Modules:
  0.0 79.4 jit_solution(13534183983423992773)
XLA Ops:
  0.6 0.8 convert.4
  1.4 0.8 broadcast_in_dim.2
  2.2 8.3 %all-to-all-start = ((bf16[16,72,128]{2,1,0:T(8,128)(2,1)}), bf16[16,72,128]{2,1,0:T(8,128)(2,1)S(1)}, u32[]{:S(2)}, u32[]{:S(2)}) async-start(bf16[16,72,128]{2,1,0:T(8,128)(2,1)} %broadcast_in_dim.2), calls=%async_computation | async-start | bytes 589824 | tf_op jit(solution)/shard_map/all_to_all | solution.py:860
  11.1 10.0 %all-to-all-done.chunk_ref = bf16[16,72,128]{2,1,0:T(8,128)(2,1)S(1)} async-done(((bf16[16,72,128]{2,1,0:T(8,128)(2,1)}), bf16[16,72,128]{2,1,0:T(8,128)(2,1)S(1)}, u32[]{:S(2)}, u32[]{:S(2)}) %all-to-all-start) | async-done | bytes 294944 | tf_op jit(solution)/shard_map/all_to_all | solution.py:860
  21.2 0.0 copy-start
  21.2 0.7 copy-done
  21.9 39.9 %image_step.1 = (bf16[96,6400]{1,0:T(8,128)(2,1)}, bf16[16,96,96]{2,1,0:T(8,128)(2,1)}, bf16[96,6400]{1,0:T(8,128)(2,1)}, bf16[96,6400]{1,0:T(8,128)(2,1)}, bf16...) custom-call(s32[1]{0:T(128)S(6)} %copy.17.side_ref, ...), custom_call_target="tpu_custom_call" | custom-call | tf_op jit(solution)/shard_map/image_step/pallas_call | solution.py:806
  61.8 3.6 %all-to-all-start.1 = ((bf16[16,96,96]{2,1,0:T(8,128)(2,1)}), bf16[16,96,96]{2,1,0:T(8,128)(2,1)S(1)}, u32[]{:S(2)}, u32[]{:S(2)}) async-start(bf16[16,96,96]{2,1,0:T(8,128)(2,1)} %get-tuple-element.22), calls=%async_computation.1 | async-start | bytes 786432 | tf_op jit(solution)/shard_map/all_to_all | solution.py:871
  65.4 0.9 %dynamic_slice.6 = f32[9060]{0:T(1024)S(1)} dynamic-slice(f32[144960]{0:T(1024)} %constant.51.clone, s32[]{:T(128)S(6)} %select_n.6), dynamic_slice_sizes={9060} | dynamic-slice | bytes 72484 | tf_op jit(solution)/shard_map/dynamic_slice | solution.py:872
  66.2 0.0 copy-start.1
  66.2 0.0 copy-start.2
  66.3 0.0 copy-start.3
  66.3 0.0 copy-start.4
  66.3 5.9 %input_step.1 = bf16[96,6400]{1,0:T(8,128)(2,1)} custom-call(bf16[96,6400]{1,0:T(8,128)(2,1)} %get-tuple-element.23.refs_0_, bf16[96,6400]{1,0:T(8,128)(2,1)} %get-tuple-element.24.refs_1_, bf16[96,6400]{1,0:T(8,128)(2,1)} %get-tuple-element.25.refs_2_, f32[8,6400]{1,0:T(8,128)} %get-tuple-element.26.refs_3_, f32[400,128]{1,0:T(8,128)} %get-tuple-element.27.refs_4_, ...), custom_call_target="tpu_custom_call" | custom-call | flops 353894400 | bytes 16777216 | tf_op jit(solution)/shard_map/input_step/pallas_call | solution.py:828
  72.2 5.0 %all-to-all-done.1 = bf16[16,96,96]{2,1,0:T(8,128)(2,1)S(1)} async-done(((bf16[16,96,96]{2,1,0:T(8,128)(2,1)}), bf16[16,96,96]{2,1,0:T(8,128)(2,1)S(1)}, u32[]{:S(2)}, u32[]{:S(2)}) %all-to-all-start.1) | async-done | bytes 294944 | tf_op jit(solution)/shard_map/all_to_all | solution.py:871
  77.1 0.1 convert_reduce_fusion
  77.2 0.1 collective-permute-start
  77.3 1.2 %collective-permute-done = f32[96,96]{1,0:T(8,128)S(1)} collective-permute-done((f32[96,96]{1,0:T(8,128)S(1)}, f32[96,96]{1,0:T(8,128)S(1)}, u32[]{:S(2)}, u32[]{:S(2)}) %collective-permute-start) | collective-permute-done | bytes 36896 | tf_op jit(solution)/shard_map/ppermute | solution.py:877
  78.5 0.1 reshape.24
  78.6 0.0 copy-done.1
  78.6 0.0 copy-done.2
  78.6 0.0 copy-done.3
  78.7 0.0 copy-done.4
  78.7 0.7 multiply_add_fusion
  (2 shorter events, 0.0 us)
Async XLA Ops:
  2.2 19.0 %all-to-all-start = ((bf16[16,72,128]{2,1,0:T(8,128)(2,1)}), bf16[16,72,128]{2,1,0:T(8,128)(2,1)S(1)}, u32[]{:S(2)}, u32[]{:S(2)}) async-start(bf16[16,72,128]{2,1,0:T(8,128)(2,1)} %broadcast_in_dim.2), calls=%async_computation | async-start | bytes 589824 | tf_op jit(solution)/shard_map/all_to_all | solution.py:860
  21.2 0.7 copy-start
  61.8 15.3 %all-to-all-start.1 = ((bf16[16,96,96]{2,1,0:T(8,128)(2,1)}), bf16[16,96,96]{2,1,0:T(8,128)(2,1)S(1)}, u32[]{:S(2)}, u32[]{:S(2)}) async-start(bf16[16,96,96]{2,1,0:T(8,128)(2,1)} %get-tuple-element.22), calls=%async_computation.1 | async-start | bytes 786432 | tf_op jit(solution)/shard_map/all_to_all | solution.py:871
  66.2 12.4 %copy-start.1 = (f32[9060]{0:T(1024)S(1)}, f32[9060]{0:T(1024)}, u32[]{:S(2)}) copy-start(f32[9060]{0:T(1024)} %param.14) | copy-start | bytes 108724
  66.2 12.4 %copy-start.2 = (f32[9060]{0:T(1024)S(1)}, f32[9060]{0:T(1024)}, u32[]{:S(2)}) copy-start(f32[9060]{0:T(1024)} %param.17) | copy-start | bytes 108724
  66.3 12.4 %copy-start.3 = (f32[9060]{0:T(1024)S(1)}, f32[9060]{0:T(1024)}, u32[]{:S(2)}) copy-start(f32[9060]{0:T(1024)} %param.15) | copy-start | bytes 108724
  66.3 12.4 %copy-start.4 = (f32[9060]{0:T(1024)S(1)}, f32[9060]{0:T(1024)}, u32[]{:S(2)}) copy-start(f32[9060]{0:T(1024)} %param.16) | copy-start | bytes 108724
  77.2 1.3 %collective-permute-start = (f32[96,96]{1,0:T(8,128)S(1)}, f32[96,96]{1,0:T(8,128)S(1)}, u32[]{:S(2)}, u32[]{:S(2)}) collective-permute-start(f32[96,96]{1,0:T(8,128)S(1)} %convert_reduce_fusion), channel_id=1, source_target_pairs={{0,1},{1,0},{2,3},{3,2},{4,5},{5,4},{6,7},{7,6},{8,9},{9,8},{10,11... | collective-permute-start | bytes 110600 | tf_op jit(solution)/shard_map/ppermute | solution.py:877

commit v6 on v5

--- a/solution.py
+++ b/solution.py
@@ -184,6 +184,10 @@
     x = jnp.concatenate([jnp.where(far[0:16], 0.0, x[0:16]), jnp.where(far[16:40], x[0:24], x[16:40])], axis=0)
     residue = where & 3
     return jnp.concatenate([jnp.where(residue == k, x, 0.0) for k in range(4)], axis=0)
+
+
+def group_row(pair, shift):
+    return D * (pair // 2) + 32 * shift + 16 * (pair % 2)
 
 
 def aligned(value, step):
@@ -487,7 +491,8 @@
             qb[16 * pair : 16 * pair + 16, plain(i, tile)] = jnp.concatenate(pooled, axis=0).astype(bf16)
             for v in range(3):
                 both = jnp.concatenate([moved[0][v], moved[1][v]], axis=0)
-                fcol[v * D + 16 * pair : v * D + 16 * pair + 16, plain(i, tile)] = both.astype(bf16)
+                place = group_row(pair, v)
+                fcol[place : place + 16, plain(i, tile)] = both.astype(bf16)
         return carry
 
     lax.fori_loop(0, TOK // TILE_ONE, pool_queries, 0)
@@ -686,8 +691,11 @@
             gfield[16 * pair : 16 * pair + 16, here] = jnp.concatenate(fields, axis=0).astype(bf16)
             for u in range(3):
                 both = jnp.concatenate([moved[0][u], moved[1][u]], axis=0)
-                gsh[u * D + 16 * pair : u * D + 16 * pair + 16, :] = both.astype(bf16)
-        kqacc[:, 0 : 3 * D] += dot_nt(gsh[...], fcol[:, here])
+                place = group_row(pair, u)
+                gsh[place : place + 16, :] = both.astype(bf16)
+        for k in range(3):
+            group = slice(k * D, (k + 1) * D)
+            kqacc[group, 0:D] += dot_nt(gsh[group, :], fcol[group, here])
         flat = pl.ds(pl.multiple_of(i * tile + LEAD, 8), tile)
         gkv[:, 0:128] = gfk[flat, :].astype(bf16)
         gkv[:, 128:256] = gfv[flat, :].astype(bf16)
@@ -728,11 +736,12 @@
     write("ln1_b", shift)
 
     lane = lax.broadcasted_iota(jnp.int32, (D, 128), 1)
-    wide_lane = lax.broadcasted_iota(jnp.int32, (D, 3 * 128), 1) - lax.broadcasted_iota(jnp.int32, (D, 3 * 128), 0)
+    within = lane - lax.rem(lax.broadcasted_iota(jnp.int32, (D, 128), 0), 32)
     columns = jnp.zeros((D, 128), f32)
     for k in range(9):
         u, v = k // 3, k % 3
-        one = jnp.where(wide_lane == v * D, kqacc[u * D : u * D + D, :], 0.0)
+        picked = jnp.concatenate([kqacc[D * g + 32 * u : D * g + 32 * u + 32, :] for g in range(3)], axis=0)
+        one = jnp.where(within == 32 * v, picked, 0.0)
         columns = jnp.where(lane == k, jnp.sum(one, axis=1, keepdims=True), columns)
     pool_gradient("pool_q", columns)
 
@@ -789,7 +798,7 @@
         vm((3 * D, TILE_THREE), bf16), vm((TILE_THREE, 256), bf16),
         vm((D, 512), f32), vm((128, HID), f32), vm((D, 128), f32), vm((128, 512), f32), vm((128, 768), f32),
         vm((TILES, D, 128), f32),
-        vm((D, 128), f32), vm((128, 256), f32), vm((3 * D, 3 * 128), f32),
+        vm((D, 128), f32), vm((128, 256), f32), vm((3 * D, 128), f32),
         vm((depth, 128), f32),
         vm((D, TOK), bf16), vm((D, TOK), bf16), vm((D, TOK), bf16), vm((D, TOK), bf16),
         pltpu.SemaphoreType.DMA((5 + TOK // TILE_THREE,)),

time: 79.9 us -> 79.4 us (level)
  no operation moved by 1% of the time
where the time goes in v6:
time: 79.4 us; the launch traced here: 78.9 us
  Pallas kernels  45.3 us (57%)
  waiting for transfers between devices  16.2 us (20%)
  starting transfers between devices  11.9 us (15%)
  local copies, waits for them, and re-layouts  2.46 us (3%)
  other arithmetic  1.61 us (2%)
  between operations  1.41 us (2%)
    pallas_call x1, Pallas kernels, image_step(): pl.pallas_call(functools.partial(image_kernel, shard_len, starts, rows_of...  39.4 us
    all_to_all x1, waiting for transfers between devices, shards(): lax.all_to_all(jnp.broadcast_to(own, (owners, filled // 128, 128)), 'wide...  10 us
    all_to_all x1, starting transfers between devices, shards(): lax.all_to_all(jnp.broadcast_to(own, (owners, filled // 128, 128)), 'wide...  8.31 us
    pallas_call x1, Pallas kernels, input_step(): pl.pallas_call(input_kernel, out_shape=jax.ShapeDtypeStruct((D, TOK), bf1...  5.89 us
    all_to_all x1, waiting for transfers between devices, shards(): parts = lax.all_to_all(grad_chunks, 'wide', 0, 0)  4.96 us
    all_to_all x1, starting transfers between devices, shards(): parts = lax.all_to_all(grad_chunks, 'wide', 0, 0)  3.56 us
  transfers between devices with their start and end apart: 3, of which 3 were waited for; matrix products, arithmetic and copies ran while one was open for 1% of the time, Pallas kernels for 7%

profile of v6, /device:TPU:0, one launch (start us, length us, event | category | flops | bytes accessed | tf_op | source)
XLA Modules:
  0.0 78.9 jit_solution(14169141062547081734)
XLA Ops:
  0.6 0.8 convert.4
  1.4 0.8 broadcast_in_dim.2
  2.2 8.3 %all-to-all-start = ((bf16[16,72,128]{2,1,0:T(8,128)(2,1)}), bf16[16,72,128]{2,1,0:T(8,128)(2,1)S(1)}, u32[]{:S(2)}, u32[]{:S(2)}) async-start(bf16[16,72,128]{2,1,0:T(8,128)(2,1)} %broadcast_in_dim.2), calls=%async_computation | async-start | bytes 589824 | tf_op jit(solution)/shard_map/all_to_all | solution.py:869
  11.1 10.0 %all-to-all-done.chunk_ref = bf16[16,72,128]{2,1,0:T(8,128)(2,1)S(1)} async-done(((bf16[16,72,128]{2,1,0:T(8,128)(2,1)}), bf16[16,72,128]{2,1,0:T(8,128)(2,1)S(1)}, u32[]{:S(2)}, u32[]{:S(2)}) %all-to-all-start) | async-done | bytes 294944 | tf_op jit(solution)/shard_map/all_to_all | solution.py:869
  21.2 0.0 copy-start
  21.2 0.7 copy-done
  21.9 39.4 %image_step.1 = (bf16[96,6400]{1,0:T(8,128)(2,1)}, bf16[16,96,96]{2,1,0:T(8,128)(2,1)}, bf16[96,6400]{1,0:T(8,128)(2,1)}, bf16[96,6400]{1,0:T(8,128)(2,1)}, bf16...) custom-call(s32[1]{0:T(128)S(6)} %copy.17.side_ref, ...), custom_call_target="tpu_custom_call" | custom-call | tf_op jit(solution)/shard_map/image_step/pallas_call | solution.py:815
  61.3 3.6 %all-to-all-start.1 = ((bf16[16,96,96]{2,1,0:T(8,128)(2,1)}), bf16[16,96,96]{2,1,0:T(8,128)(2,1)S(1)}, u32[]{:S(2)}, u32[]{:S(2)}) async-start(bf16[16,96,96]{2,1,0:T(8,128)(2,1)} %get-tuple-element.22), calls=%async_computation.1 | async-start | bytes 786432 | tf_op jit(solution)/shard_map/all_to_all | solution.py:880
  64.9 0.9 %dynamic_slice.6 = f32[9060]{0:T(1024)S(1)} dynamic-slice(f32[144960]{0:T(1024)} %constant.51.clone, s32[]{:T(128)S(6)} %select_n.6), dynamic_slice_sizes={9060} | dynamic-slice | bytes 72484 | tf_op jit(solution)/shard_map/dynamic_slice | solution.py:881
  65.8 0.0 copy-start.1
  65.8 0.0 copy-start.2
  65.8 0.0 copy-start.3
  65.8 0.0 copy-start.4
  65.8 5.9 %input_step.1 = bf16[96,6400]{1,0:T(8,128)(2,1)} custom-call(bf16[96,6400]{1,0:T(8,128)(2,1)} %get-tuple-element.23.refs_0_, bf16[96,6400]{1,0:T(8,128)(2,1)} %get-tuple-element.24.refs_1_, bf16[96,6400]{1,0:T(8,128)(2,1)} %get-tuple-element.25.refs_2_, f32[8,6400]{1,0:T(8,128)} %get-tuple-element.26.refs_3_, f32[400,128]{1,0:T(8,128)} %get-tuple-element.27.refs_4_, ...), custom_call_target="tpu_custom_call" | custom-call | flops 353894400 | bytes 16777216 | tf_op jit(solution)/shard_map/input_step/pallas_call | solution.py:837
  71.7 5.0 %all-to-all-done.1 = bf16[16,96,96]{2,1,0:T(8,128)(2,1)S(1)} async-done(((bf16[16,96,96]{2,1,0:T(8,128)(2,1)}), bf16[16,96,96]{2,1,0:T(8,128)(2,1)S(1)}, u32[]{:S(2)}, u32[]{:S(2)}) %all-to-all-start.1) | async-done | bytes 294944 | tf_op jit(solution)/shard_map/all_to_all | solution.py:880
  76.7 0.1 convert_reduce_fusion
  76.7 0.1 collective-permute-start
  76.8 1.2 %collective-permute-done = f32[96,96]{1,0:T(8,128)S(1)} collective-permute-done((f32[96,96]{1,0:T(8,128)S(1)}, f32[96,96]{1,0:T(8,128)S(1)}, u32[]{:S(2)}, u32[]{:S(2)}) %collective-permute-start) | collective-permute-done | bytes 36896 | tf_op jit(solution)/shard_map/ppermute | solution.py:886
  78.0 0.1 reshape.24
  78.1 0.0 copy-done.1
  78.2 0.0 copy-done.2
  78.2 0.0 copy-done.3
  78.2 0.0 copy-done.4
  78.2 0.7 multiply_add_fusion
  (2 shorter events, 0.0 us)
Async XLA Ops:
  2.2 19.0 %all-to-all-start = ((bf16[16,72,128]{2,1,0:T(8,128)(2,1)}), bf16[16,72,128]{2,1,0:T(8,128)(2,1)S(1)}, u32[]{:S(2)}, u32[]{:S(2)}) async-start(bf16[16,72,128]{2,1,0:T(8,128)(2,1)} %broadcast_in_dim.2), calls=%async_computation | async-start | bytes 589824 | tf_op jit(solution)/shard_map/all_to_all | solution.py:869
  21.2 0.7 copy-start
  61.3 15.3 %all-to-all-start.1 = ((bf16[16,96,96]{2,1,0:T(8,128)(2,1)}), bf16[16,96,96]{2,1,0:T(8,128)(2,1)S(1)}, u32[]{:S(2)}, u32[]{:S(2)}) async-start(bf16[16,96,96]{2,1,0:T(8,128)(2,1)} %get-tuple-element.22), calls=%async_computation.1 | async-start | bytes 786432 | tf_op jit(solution)/shard_map/all_to_all | solution.py:880
  65.8 12.4 %copy-start.1 = (f32[9060]{0:T(1024)S(1)}, f32[9060]{0:T(1024)}, u32[]{:S(2)}) copy-start(f32[9060]{0:T(1024)} %param.14) | copy-start | bytes 108724
  65.8 12.4 %copy-start.2 = (f32[9060]{0:T(1024)S(1)}, f32[9060]{0:T(1024)}, u32[]{:S(2)}) copy-start(f32[9060]{0:T(1024)} %param.17) | copy-start | bytes 108724
  65.8 12.4 %copy-start.3 = (f32[9060]{0:T(1024)S(1)}, f32[9060]{0:T(1024)}, u32[]{:S(2)}) copy-start(f32[9060]{0:T(1024)} %param.15) | copy-start | bytes 108724
  65.8 12.4 %copy-start.4 = (f32[9060]{0:T(1024)S(1)}, f32[9060]{0:T(1024)}, u32[]{:S(2)}) copy-start(f32[9060]{0:T(1024)} %param.16) | copy-start | bytes 108724
  76.7 1.3 %collective-permute-start = (f32[96,96]{1,0:T(8,128)S(1)}, f32[96,96]{1,0:T(8,128)S(1)}, u32[]{:S(2)}, u32[]{:S(2)}) collective-permute-start(f32[96,96]{1,0:T(8,128)S(1)} %convert_reduce_fusion), channel_id=1, source_target_pairs={{0,1},{1,0},{2,3},{3,2},{4,5},{5,4},{6,7},{7,6},{8,9},{9,8},{10,11... | collective-permute-start | bytes 110600 | tf_op jit(solution)/shard_map/ppermute | solution.py:886

commit v7 on v6

--- a/solution.py
+++ b/solution.py
@@ -551,7 +551,6 @@
         scores = dot(a1[...], rhs[...])
         yield True
         weight = jnp.exp2((scores - jnp.max(scores, axis=0, keepdims=True)) * (SCORE_SCALE * LOG2E))
-        weight_ref[...] = weight
         low_ref[...] = weight.astype(bf16)
         yield True
         mixed = dot(vb[...], low_ref[...])
@@ -565,7 +564,6 @@
         center = middle - jnp.sum(middle, axis=0, keepdims=True) * (1.0 / D)
         inv = lax.rsqrt(jnp.sum(center * center, axis=0, keepdims=True) * (1.0 / D) + norm_eps)
         half = center * (inv * math.sqrt(0.5))
-        half_ref[...] = half
         scale_ref[1:2, :] = inv
         n2aug[0:D, :] = half.astype(bf16)
         z = dot(w1[...], n2aug[...])
@@ -594,7 +592,7 @@
         gn = dot(w1t[...], gh_low)
         yield True
         dw1[0:112, :] += dot_nt(n2aug[...], gh_low)
-        half = half_ref[...]
+        half = n2aug[0:D, :].astype(f32)
         mean = jnp.sum(gn, axis=0, keepdims=True) * (1.0 / D)
         along = jnp.sum(gn * half, axis=0, keepdims=True) * (2.0 / D)
         gmid = gy + (gn - mean - half * along) * (inv * math.sqrt(1.0 / math.pi))
@@ -609,7 +607,7 @@
         spread = dot(vbt[...], goaug[...])
         yield True
         gv[0:D, 0:KK] += dot_nt(go_low, low_ref[...])
-        gse[0:KK, :] = (weight_ref[...] * spread).astype(bf16)
+        gse[0:KK, :] = (low_ref[...].astype(f32) * spread).astype(bf16)
         back = dot(a2[...], gse[0:KK, :])
         yield True
         gse[KK : KK + D, :] = unskew_rows(back[D : D + 24], row).astype(bf16)

time: 79.4 us -> 79.3 us (level)
  no operation moved by 1% of the time
where the time goes in v7:
time: 79.3 us; the launch traced here: 78.8 us
  Pallas kernels  45.1 us (57%)
  waiting for transfers between devices  16.2 us (20%)
  starting transfers between devices  11.9 us (15%)
  local copies, waits for them, and re-layouts  2.46 us (3%)
  other arithmetic  1.61 us (2%)
  between operations  1.41 us (2%)
    pallas_call x1, Pallas kernels, image_step(): pl.pallas_call(functools.partial(image_kernel, shard_len, starts, rows_of...  39.3 us
    all_to_all x1, waiting for transfers between devices, shards(): lax.all_to_all(jnp.broadcast_to(own, (owners, filled // 128, 128)), 'wide...  10 us
    all_to_all x1, starting transfers between devices, shards(): lax.all_to_all(jnp.broadcast_to(own, (owners, filled // 128, 128)), 'wide...  8.31 us
    pallas_call x1, Pallas kernels, input_step(): pl.pallas_call(input_kernel, out_shape=jax.ShapeDtypeStruct((D, TOK), bf1...  5.89 us
    all_to_all x1, waiting for transfers between devices, shards(): parts = lax.all_to_all(grad_chunks, 'wide', 0, 0)  4.97 us
    all_to_all x1, starting transfers between devices, shards(): parts = lax.all_to_all(grad_chunks, 'wide', 0, 0)  3.56 us
  transfers between devices with their start and end apart: 3, of which 3 were waited for; matrix products, arithmetic and copies ran while one was open for 1% of the time, Pallas kernels for 7%

profile of v7, /device:TPU:0, one launch (start us, length us, event | category | flops | bytes accessed | tf_op | source)
XLA Modules:
  0.0 78.8 jit_solution(5635055678255826802)
XLA Ops:
  0.6 0.8 convert.4
  1.4 0.8 broadcast_in_dim.2
  2.2 8.3 %all-to-all-start = ((bf16[16,72,128]{2,1,0:T(8,128)(2,1)}), bf16[16,72,128]{2,1,0:T(8,128)(2,1)S(1)}, u32[]{:S(2)}, u32[]{:S(2)}) async-start(bf16[16,72,128]{2,1,0:T(8,128)(2,1)} %broadcast_in_dim.2), calls=%async_computation | async-start | bytes 589824 | tf_op jit(solution)/shard_map/all_to_all | solution.py:867
  11.1 10.0 %all-to-all-done.chunk_ref = bf16[16,72,128]{2,1,0:T(8,128)(2,1)S(1)} async-done(((bf16[16,72,128]{2,1,0:T(8,128)(2,1)}), bf16[16,72,128]{2,1,0:T(8,128)(2,1)S(1)}, u32[]{:S(2)}, u32[]{:S(2)}) %all-to-all-start) | async-done | bytes 294944 | tf_op jit(solution)/shard_map/all_to_all | solution.py:867
  21.2 0.0 copy-start
  21.2 0.7 copy-done
  21.9 39.3 %image_step.1 = (bf16[96,6400]{1,0:T(8,128)(2,1)}, bf16[16,96,96]{2,1,0:T(8,128)(2,1)}, bf16[96,6400]{1,0:T(8,128)(2,1)}, bf16[96,6400]{1,0:T(8,128)(2,1)}, bf16...) custom-call(s32[1]{0:T(128)S(6)} %copy.17.side_ref, ...), custom_call_target="tpu_custom_call" | custom-call | tf_op jit(solution)/shard_map/image_step/pallas_call | solution.py:813
  61.1 3.6 %all-to-all-start.1 = ((bf16[16,96,96]{2,1,0:T(8,128)(2,1)}), bf16[16,96,96]{2,1,0:T(8,128)(2,1)S(1)}, u32[]{:S(2)}, u32[]{:S(2)}) async-start(bf16[16,96,96]{2,1,0:T(8,128)(2,1)} %get-tuple-element.22), calls=%async_computation.1 | async-start | bytes 786432 | tf_op jit(solution)/shard_map/all_to_all | solution.py:878
  64.7 0.9 %dynamic_slice.6 = f32[9060]{0:T(1024)S(1)} dynamic-slice(f32[144960]{0:T(1024)} %constant.51.clone, s32[]{:T(128)S(6)} %select_n.6), dynamic_slice_sizes={9060} | dynamic-slice | bytes 72484 | tf_op jit(solution)/shard_map/dynamic_slice | solution.py:879
  65.6 0.0 copy-start.1
  65.6 0.0 copy-start.2
  65.6 0.0 copy-start.3
  65.6 0.0 copy-start.4
  65.6 5.9 %input_step.1 = bf16[96,6400]{1,0:T(8,128)(2,1)} custom-call(bf16[96,6400]{1,0:T(8,128)(2,1)} %get-tuple-element.23.refs_0_, bf16[96,6400]{1,0:T(8,128)(2,1)} %get-tuple-element.24.refs_1_, bf16[96,6400]{1,0:T(8,128)(2,1)} %get-tuple-element.25.refs_2_, f32[8,6400]{1,0:T(8,128)} %get-tuple-element.26.refs_3_, f32[400,128]{1,0:T(8,128)} %get-tuple-element.27.refs_4_, ...), custom_call_target="tpu_custom_call" | custom-call | flops 353894400 | bytes 16777216 | tf_op jit(solution)/shard_map/input_step/pallas_call | solution.py:835
  71.5 5.0 %all-to-all-done.1 = bf16[16,96,96]{2,1,0:T(8,128)(2,1)S(1)} async-done(((bf16[16,96,96]{2,1,0:T(8,128)(2,1)}), bf16[16,96,96]{2,1,0:T(8,128)(2,1)S(1)}, u32[]{:S(2)}, u32[]{:S(2)}) %all-to-all-start.1) | async-done | bytes 294944 | tf_op jit(solution)/shard_map/all_to_all | solution.py:878
  76.5 0.1 convert_reduce_fusion
  76.6 0.1 collective-permute-start
  76.7 1.2 %collective-permute-done = f32[96,96]{1,0:T(8,128)S(1)} collective-permute-done((f32[96,96]{1,0:T(8,128)S(1)}, f32[96,96]{1,0:T(8,128)S(1)}, u32[]{:S(2)}, u32[]{:S(2)}) %collective-permute-start) | collective-permute-done | bytes 36896 | tf_op jit(solution)/shard_map/ppermute | solution.py:884
  77.9 0.1 reshape.24
  78.0 0.0 copy-done.1
  78.0 0.0 copy-done.2
  78.0 0.0 copy-done.3
  78.0 0.0 copy-done.4
  78.0 0.7 multiply_add_fusion
  (2 shorter events, 0.0 us)
Async XLA Ops:
  2.2 19.0 %all-to-all-start = ((bf16[16,72,128]{2,1,0:T(8,128)(2,1)}), bf16[16,72,128]{2,1,0:T(8,128)(2,1)S(1)}, u32[]{:S(2)}, u32[]{:S(2)}) async-start(bf16[16,72,128]{2,1,0:T(8,128)(2,1)} %broadcast_in_dim.2), calls=%async_computation | async-start | bytes 589824 | tf_op jit(solution)/shard_map/all_to_all | solution.py:867
  21.2 0.7 copy-start
  61.1 15.4 %all-to-all-start.1 = ((bf16[16,96,96]{2,1,0:T(8,128)(2,1)}), bf16[16,96,96]{2,1,0:T(8,128)(2,1)S(1)}, u32[]{:S(2)}, u32[]{:S(2)}) async-start(bf16[16,96,96]{2,1,0:T(8,128)(2,1)} %get-tuple-element.22), calls=%async_computation.1 | async-start | bytes 786432 | tf_op jit(solution)/shard_map/all_to_all | solution.py:878
  65.6 12.4 %copy-start.1 = (f32[9060]{0:T(1024)S(1)}, f32[9060]{0:T(1024)}, u32[]{:S(2)}) copy-start(f32[9060]{0:T(1024)} %param.14) | copy-start | bytes 108724
  65.6 12.4 %copy-start.2 = (f32[9060]{0:T(1024)S(1)}, f32[9060]{0:T(1024)}, u32[]{:S(2)}) copy-start(f32[9060]{0:T(1024)} %param.17) | copy-start | bytes 108724
  65.6 12.4 %copy-start.3 = (f32[9060]{0:T(1024)S(1)}, f32[9060]{0:T(1024)}, u32[]{:S(2)}) copy-start(f32[9060]{0:T(1024)} %param.15) | copy-start | bytes 108724
  65.6 12.4 %copy-start.4 = (f32[9060]{0:T(1024)S(1)}, f32[9060]{0:T(1024)}, u32[]{:S(2)}) copy-start(f32[9060]{0:T(1024)} %param.16) | copy-start | bytes 108724
  76.6 1.3 %collective-permute-start = (f32[96,96]{1,0:T(8,128)S(1)}, f32[96,96]{1,0:T(8,128)S(1)}, u32[]{:S(2)}, u32[]{:S(2)}) collective-permute-start(f32[96,96]{1,0:T(8,128)S(1)} %convert_reduce_fusion), channel_id=1, source_target_pairs={{0,1},{1,0},{2,3},{3,2},{4,5},{5,4},{6,7},{7,6},{8,9},{9,8},{10,11... | collective-permute-start | bytes 110600 | tf_op jit(solution)/shard_map/ppermute | solution.py:884
